TPU v7x, 512 devices: a whole 4x4x16 slice. The times are simulated.
512 devices in a mesh: row: 32 (over z, core), col: 16 (over y, x).
Axes of the slice: x: 4, y: 4, z: 16, core: 2. Of those that a mesh axis runs over, the one named last changes fastest.
Arguments:
- amplitudes: bfloat16 [16384, 16384], P('row', 'col'), may hold values from -6 to 6
- integrals: bfloat16 [16384, 4096], P('col', 'row'), may hold values from -0.09375 to 0.09375
- amp_occupancy: int32 [128, 128], P('row', 'col'), may hold values 0 or 1
- int_occupancy: int32 [128, 32], P('col', 'row'), may hold values 0 or 1
- owner_map: int32 [32], replicated, may hold values from 0 to 31, each once
Outputs:
- residual: bfloat16 [16384, 4096], P('row', 'col')
Inputs may be any that keep to these rules, and one draw needn't show every extreme that they name: `owner_map`: each tile number appears once.
All inputs are finite; a program needn't handle non-finite values. No bound on the sum of `amp_occupancy` or of `int_occupancy` on one device may be relied on, other than what follows from the above.
Results may differ from a plain program's by a relative error of at most 0.014.
Values may be sent and summed in bfloat16 or wider, within the bound.
No kernel may reach another device: no remote copies, remote signals or barrier semaphores. Data moves between devices by JAX's collectives and lax.ppermute only.
A program may use at most 64 MiB of HBM per device.

v0:
```python
import jax
import jax.numpy as jnp
from jax import lax
from jax.sharding import Mesh, PartitionSpec as P


TILE = 128


def mask_tiles(matrix, occupancy):
    nrow, ncolumn = matrix.shape
    blocks = matrix.reshape(nrow // TILE, TILE, ncolumn // TILE, TILE)
    return (blocks * occupancy[:, None, :, None].astype(jnp.bfloat16)).reshape(nrow, ncolumn)


def ring_pairs(nz):
    up = [(2 * z, 2 * ((z + 1) % nz)) for z in range(nz)]
    down = [(2 * z + 1, 2 * ((z - 1) % nz) + 1) for z in range(nz)]
    return up + down


def first_pairs(nz, stream):
    if stream == 0:
        return [(2 * z, 2 * ((z + 1) % nz)) for z in range(nz)] + [(2 * z + 1, 2 * z + 1) for z in range(nz)]
    return [(2 * z + 1, 2 * ((z + 1) % nz)) for z in range(nz)] + [(2 * z, 2 * z + 1) for z in range(nz)]


def chunks_of(nslot):
    return (nslot // 4,) * 4


def make(nz, ncol):
    row = ("z", "core")
    swap = [(r, r ^ 1) for r in range(2 * nz)]
    nslot = nz // 2
    sizes = chunks_of(nslot)
    ends = [sum(sizes[: i + 1]) for i in range(len(sizes))]

    def on_device(amplitudes, integrals, amp_occupancy, int_occupancy, owner_map):
        z = lax.axis_index("z")
        core = lax.axis_index("core")
        own_tile = mask_tiles(integrals, int_occupancy)
        current = [own_tile, own_tile]
        sums = []
        tiles = []
        amp = None
        for slot in range(1, nslot + 1):
            for stream in (0, 1):
                pairs = first_pairs(nz, stream) if slot == 1 else ring_pairs(nz)
                current[stream] = lax.ppermute(current[stream], row, pairs)
            tiles += current
            if slot == 1:
                own_amp = mask_tiles(amplitudes, amp_occupancy)
                other_amp = lax.ppermute(own_amp, row, swap)
                amp = jnp.concatenate(
                    [jnp.where(core == 0, own_amp, other_amp), jnp.where(core == 0, other_amp, own_amp)], 0
                )
                nrow = own_amp.shape[0]
                part = nrow // ncol
            if slot in ends:
                right = jnp.concatenate(tiles, 1)
                product = jnp.dot(amp, right, preferred_element_type=jnp.float32).astype(jnp.bfloat16)
                tiles = []
                width = product.shape[1]
                product = product.reshape(2 * ncol, part, width)
                moved = lax.all_to_all(product, ("core", "col"), 0, 0, tiled=True)
                total = jnp.sum(moved.reshape(2, ncol, part, width).astype(jnp.float32), 1)
                sums.append(total.astype(jnp.bfloat16))
        done = jnp.concatenate(sums, 2).reshape(2, part, 2 * nslot, TILE)
        done = done.transpose(0, 2, 1, 3).reshape(4 * nslot, part, TILE)
        chip = owner_map // 2
        parity = owner_map % 2
        behind = (z - chip) % nz
        upward = (behind >= 1) & (behind <= nslot)
        side = jnp.where(upward, 0, 1)
        slot_of = jnp.where(upward, behind - 1, (chip - z) % nz)
        place = side * (2 * nslot) + slot_of * 2 + (parity ^ side)
        picked = done[place].reshape(ncol, 2, part, TILE).transpose(0, 2, 1, 3).reshape(ncol, part, 2 * TILE)
        final = lax.all_to_all(picked, "col", 0, 0, tiled=True)
        return final.reshape(nrow, 2 * TILE)

    return on_device


def solution(mesh):
    nz = mesh.shape["row"] // 2
    ncol = mesh.shape["col"]
    fine = Mesh(mesh.devices.reshape(nz, 2, ncol), ("z", "core", "col"))
    split = ("z", "core")
    placed = (P(split, "col"), P("col", split), P(split, "col"), P("col", split), P())
    return jax.shard_map(
        make(nz, ncol), mesh=fine, in_specs=placed, out_specs=P(split, "col"), check_vma=False
    )
```

profile of v0, /device:TPU:1, one launch (start us, length us, event | category | flops | bytes accessed | tf_op | source)
XLA Modules:
  0.0 171.2 jit_solution(7764608397742091274)
XLA Ops:
  1.4 8.7 %collective-permute-start = (bf16[512,1024]{1,0:T(8,128)(2,1)S(1)}, bf16[512,1024]{1,0:T(8,128)(2,1)}, u32[]{:S(2)}, u32[]{:S(2)}) collective-permute-start(bf16[512,1024]{1,0:T(8,128)(2,1)S(1)} %bitcast_multiply_fusion), channel_id=1, source_target_pairs={{0,16},{16,0},{32,48},{48,32},{64,80},{80,64},{96,112},{112,96},{1... | collective-permute-start | bytes 3145736 | tf_op jit(solution)/shard_map/ppermute | solution.py:54
  11.8 2.2 %collective-permute-done.2 = bf16[1024,128]{1,0:T(8,128)(2,1)S(1)} collective-permute-done((bf16[1024,128]{1,0:T(8,128)(2,1)S(1)}, bf16[1024,128]{1,0:T(8,128)(2,1)S(1)}, u32[]{:S(2)}, u32[]{:S(2)}) %collective-permute-start.2) | collective-permute-done | bytes 262176 | tf_op jit(solution)/shard_map/ppermute | solution.py:50
  14.0 5.8 %collective-permute-start.4 = (bf16[1024,128]{1,0:T(8,128)(2,1)S(1)}, bf16[1024,128]{1,0:T(8,128)(2,1)S(1)}, u32[]{:S(2)}, u32[]{:S(2)}) collective-permute-start(bf16[1024,128]{1,0:T(8,128)(2,1)S(1)} %collective-permute-done.2), channel_id=1, source_target_pairs={{0,32},{32,64},{64,96},{96,128},{128,160},{160,192},{192,224},{224... | collective-permute-start | bytes 786440 | tf_op jit(solution)/shard_map/ppermute | solution.py:50
  19.8 3.0 %collective-permute-start.3 = (bf16[1024,128]{1,0:T(8,128)(2,1)}, bf16[1024,128]{1,0:T(8,128)(2,1)S(1)}, u32[]{:S(2)}, u32[]{:S(2)}) collective-permute-start(bf16[1024,128]{1,0:T(8,128)(2,1)} %collective-permute-done.1), channel_id=1, source_target_pairs={{0,32},{32,64},{64,96},{96,128},{128,160},{160,192},{192,224},{224... | collective-permute-start | bytes 786440 | tf_op jit(solution)/shard_map/ppermute | solution.py:50
  24.3 3.2 %collective-permute-done.3 = bf16[1024,128]{1,0:T(8,128)(2,1)S(1)} collective-permute-done((bf16[1024,128]{1,0:T(8,128)(2,1)}, bf16[1024,128]{1,0:T(8,128)(2,1)S(1)}, u32[]{:S(2)}, u32[]{:S(2)}) %collective-permute-start.3) | collective-permute-done | bytes 262176 | tf_op jit(solution)/shard_map/ppermute | solution.py:50
  27.4 3.3 %convolution_convert_fusion.3 = bf16[1024,512]{1,0:T(8,128)(2,1)} fusion(bf16[1024,128]{1,0:T(8,128)(2,1)S(1)} %collective-permute-done.4, bf16[1024,128]{1,0:T(8,128)(2,1)S(1)} %collective-permute-done.3, bf16[1024,128]{1,0:T(8,128)(2,1)S(1)} %collective-permute-done.2, bf16[1024,128]{1,0:T(8,128)(2,1)} %collective-permute-done.1, ...), kind=kOutput, calls=%fused_computation.5 | convolution fusion | flops 1082654720 | bytes 4194304 | tf_op jit(solution)/shard_map/dot_general | solution.py:62
  30.7 11.2 %all-to-all-start = ((bf16[32,32,512]{2,1,0:T(8,128)(2,1)}), bf16[32,32,512]{2,1,0:T(8,128)(2,1)S(1)}, u32[]{:S(2)}, u32[]{:S(2)}) async-start(bf16[32,32,512]{2,1,0:T(8,128)(2,1)} %bitcast.42), calls=%async_computation | async-start | bytes 2097152 | tf_op jit(solution)/shard_map/all_to_all | solution.py:66
  41.9 2.9 %collective-permute-start.6 = (bf16[1024,128]{1,0:T(8,128)(2,1)S(1)}, bf16[1024,128]{1,0:T(8,128)(2,1)S(1)}, u32[]{:S(2)}, u32[]{:S(2)}) collective-permute-start(bf16[1024,128]{1,0:T(8,128)(2,1)S(1)} %copy-done.5), channel_id=1, source_target_pairs={{0,32},{32,64},{64,96},{96,128},{128,160},{160,192},{192,224},{224... | collective-permute-start | bytes 786440 | tf_op jit(solution)/shard_map/ppermute | solution.py:50
  44.8 1.9 %collective-permute-start.5 = (bf16[1024,128]{1,0:T(8,128)(2,1)}, bf16[1024,128]{1,0:T(8,128)(2,1)S(1)}, u32[]{:S(2)}, u32[]{:S(2)}) collective-permute-start(bf16[1024,128]{1,0:T(8,128)(2,1)} %copy-done.6), channel_id=1, source_target_pairs={{0,32},{32,64},{64,96},{96,128},{128,160},{160,192},{192,224},{224... | collective-permute-start | bytes 786440 | tf_op jit(solution)/shard_map/ppermute | solution.py:50
  46.8 2.6 %collective-permute-done.6 = bf16[1024,128]{1,0:T(8,128)(2,1)S(1)} collective-permute-done((bf16[1024,128]{1,0:T(8,128)(2,1)S(1)}, bf16[1024,128]{1,0:T(8,128)(2,1)S(1)}, u32[]{:S(2)}, u32[]{:S(2)}) %collective-permute-start.6) | collective-permute-done | bytes 262176 | tf_op jit(solution)/shard_map/ppermute | solution.py:50
  49.3 3.8 %collective-permute-start.8 = (bf16[1024,128]{1,0:T(8,128)(2,1)S(1)}, bf16[1024,128]{1,0:T(8,128)(2,1)S(1)}, u32[]{:S(2)}, u32[]{:S(2)}) collective-permute-start(bf16[1024,128]{1,0:T(8,128)(2,1)S(1)} %collective-permute-done.6), channel_id=1, source_target_pairs={{0,32},{32,64},{64,96},{96,128},{128,160},{160,192},{192,224},{224... | collective-permute-start | bytes 786440 | tf_op jit(solution)/shard_map/ppermute | solution.py:50
  53.2 3.1 %collective-permute-start.7 = (bf16[1024,128]{1,0:T(8,128)(2,1)S(1)}, bf16[1024,128]{1,0:T(8,128)(2,1)S(1)}, u32[]{:S(2)}, u32[]{:S(2)}) collective-permute-start(bf16[1024,128]{1,0:T(8,128)(2,1)S(1)} %collective-permute-done.5), channel_id=1, source_target_pairs={{0,32},{32,64},{64,96},{96,128},{128,160},{160,192},{192,224},{224... | collective-permute-start | bytes 786440 | tf_op jit(solution)/shard_map/ppermute | solution.py:50
  56.7 3.8 %collective-permute-done.7 = bf16[1024,128]{1,0:T(8,128)(2,1)S(1)} collective-permute-done((bf16[1024,128]{1,0:T(8,128)(2,1)S(1)}, bf16[1024,128]{1,0:T(8,128)(2,1)S(1)}, u32[]{:S(2)}, u32[]{:S(2)}) %collective-permute-start.7) | collective-permute-done | bytes 262176 | tf_op jit(solution)/shard_map/ppermute | solution.py:50
  61.3 2.3 %convolution_convert_fusion.2 = bf16[1024,512]{1,0:T(8,128)(2,1)} fusion(bf16[1024,128]{1,0:T(8,128)(2,1)S(1)} %collective-permute-done.8, bf16[1024,128]{1,0:T(8,128)(2,1)S(1)} %collective-permute-done.7, bf16[1024,128]{1,0:T(8,128)(2,1)S(1)} %collective-permute-done.6, bf16[1024,128]{1,0:T(8,128)(2,1)S(1)} %collective-permute-done.5, ...), kind=kOutput, calls=%fused_computation.4 | convolution fusion | flops 1082654720 | bytes 4194304 | tf_op jit(solution)/shard_map/dot_general | solution.py:62
  63.5 10.5 %all-to-all-start.1 = ((bf16[32,32,512]{2,1,0:T(8,128)(2,1)}), bf16[32,32,512]{2,1,0:T(8,128)(2,1)S(1)}, u32[]{:S(2)}, u32[]{:S(2)}) async-start(bf16[32,32,512]{2,1,0:T(8,128)(2,1)} %bitcast.41), calls=%async_computation.1 | async-start | bytes 2097152 | tf_op jit(solution)/shard_map/all_to_all | solution.py:66
  74.0 2.8 %collective-permute-start.10 = (bf16[1024,128]{1,0:T(8,128)(2,1)S(1)}, bf16[1024,128]{1,0:T(8,128)(2,1)S(1)}, u32[]{:S(2)}, u32[]{:S(2)}) collective-permute-start(bf16[1024,128]{1,0:T(8,128)(2,1)S(1)} %collective-permute-done.8), channel_id=1, source_target_pairs={{0,32},{32,64},{64,96},{96,128},{128,160},{160,192},{192,224},{224... | collective-permute-start | bytes 786440 | tf_op jit(solution)/shard_map/ppermute | solution.py:50
  76.8 1.9 %collective-permute-start.9 = (bf16[1024,128]{1,0:T(8,128)(2,1)}, bf16[1024,128]{1,0:T(8,128)(2,1)S(1)}, u32[]{:S(2)}, u32[]{:S(2)}) collective-permute-start(bf16[1024,128]{1,0:T(8,128)(2,1)} %copy-done.7), channel_id=1, source_target_pairs={{0,32},{32,64},{64,96},{96,128},{128,160},{160,192},{192,224},{224... | collective-permute-start | bytes 786440 | tf_op jit(solution)/shard_map/ppermute | solution.py:50
  78.7 2.7 %collective-permute-done.10 = bf16[1024,128]{1,0:T(8,128)(2,1)S(1)} collective-permute-done((bf16[1024,128]{1,0:T(8,128)(2,1)S(1)}, bf16[1024,128]{1,0:T(8,128)(2,1)S(1)}, u32[]{:S(2)}, u32[]{:S(2)}) %collective-permute-start.10) | collective-permute-done | bytes 262176 | tf_op jit(solution)/shard_map/ppermute | solution.py:50
  81.4 3.7 %collective-permute-start.12 = (bf16[1024,128]{1,0:T(8,128)(2,1)S(1)}, bf16[1024,128]{1,0:T(8,128)(2,1)S(1)}, u32[]{:S(2)}, u32[]{:S(2)}) collective-permute-start(bf16[1024,128]{1,0:T(8,128)(2,1)S(1)} %collective-permute-done.10), channel_id=1, source_target_pairs={{0,32},{32,64},{64,96},{96,128},{128,160},{160,192},{192,224},{224... | collective-permute-start | bytes 786440 | tf_op jit(solution)/shard_map/ppermute | solution.py:50
  85.1 3.1 %collective-permute-start.11 = (bf16[1024,128]{1,0:T(8,128)(2,1)S(1)}, bf16[1024,128]{1,0:T(8,128)(2,1)S(1)}, u32[]{:S(2)}, u32[]{:S(2)}) collective-permute-start(bf16[1024,128]{1,0:T(8,128)(2,1)S(1)} %collective-permute-done.9), channel_id=1, source_target_pairs={{0,32},{32,64},{64,96},{96,128},{128,160},{160,192},{192,224},{224... | collective-permute-start | bytes 786440 | tf_op jit(solution)/shard_map/ppermute | solution.py:50
  88.8 3.7 %collective-permute-done.11 = bf16[1024,128]{1,0:T(8,128)(2,1)S(1)} collective-permute-done((bf16[1024,128]{1,0:T(8,128)(2,1)S(1)}, bf16[1024,128]{1,0:T(8,128)(2,1)S(1)}, u32[]{:S(2)}, u32[]{:S(2)}) %collective-permute-start.11) | collective-permute-done | bytes 262176 | tf_op jit(solution)/shard_map/ppermute | solution.py:50
  93.2 3.5 %convolution_convert_fusion.1 = bf16[1024,512]{1,0:T(8,128)(2,1)} fusion(bf16[1024,128]{1,0:T(8,128)(2,1)S(1)} %collective-permute-done.12, bf16[1024,128]{1,0:T(8,128)(2,1)S(1)} %collective-permute-done.11, bf16[1024,128]{1,0:T(8,128)(2,1)S(1)} %collective-permute-done.10, bf16[1024,128]{1,0:T(8,128)(2,1)S(1)} %collective-permute-done.9, ...), kind=kOutput, calls=%fused_computation.3 | convolution fusion | flops 1082654720 | bytes 4194304 | tf_op jit(solution)/shard_map/dot_general | solution.py:62
  96.7 10.6 %all-to-all-start.2 = ((bf16[32,32,512]{2,1,0:T(8,128)(2,1)}), bf16[32,32,512]{2,1,0:T(8,128)(2,1)S(1)}, u32[]{:S(2)}, u32[]{:S(2)}) async-start(bf16[32,32,512]{2,1,0:T(8,128)(2,1)} %bitcast.40), calls=%async_computation.2 | async-start | bytes 2097152 | tf_op jit(solution)/shard_map/all_to_all | solution.py:66
  107.3 2.8 %collective-permute-start.14 = (bf16[1024,128]{1,0:T(8,128)(2,1)S(1)}, bf16[1024,128]{1,0:T(8,128)(2,1)S(1)}, u32[]{:S(2)}, u32[]{:S(2)}) collective-permute-start(bf16[1024,128]{1,0:T(8,128)(2,1)S(1)} %collective-permute-done.12), channel_id=1, source_target_pairs={{0,32},{32,64},{64,96},{96,128},{128,160},{160,192},{192,224},{224... | collective-permute-start | bytes 786440 | tf_op jit(solution)/shard_map/ppermute | solution.py:50
  112.0 2.7 %collective-permute-done.14 = bf16[1024,128]{1,0:T(8,128)(2,1)S(1)} collective-permute-done((bf16[1024,128]{1,0:T(8,128)(2,1)S(1)}, bf16[1024,128]{1,0:T(8,128)(2,1)S(1)}, u32[]{:S(2)}, u32[]{:S(2)}) %collective-permute-start.14) | collective-permute-done | bytes 262176 | tf_op jit(solution)/shard_map/ppermute | solution.py:50
  114.7 3.7 %collective-permute-start.16 = (bf16[1024,128]{1,0:T(8,128)(2,1)S(1)}, bf16[1024,128]{1,0:T(8,128)(2,1)S(1)}, u32[]{:S(2)}, u32[]{:S(2)}) collective-permute-start(bf16[1024,128]{1,0:T(8,128)(2,1)S(1)} %collective-permute-done.14), channel_id=1, source_target_pairs={{0,32},{32,64},{64,96},{96,128},{128,160},{160,192},{192,224},{224... | collective-permute-start | bytes 786440 | tf_op jit(solution)/shard_map/ppermute | solution.py:50
  118.4 3.1 %collective-permute-start.15 = (bf16[1024,128]{1,0:T(8,128)(2,1)S(1)}, bf16[1024,128]{1,0:T(8,128)(2,1)S(1)}, u32[]{:S(2)}, u32[]{:S(2)}) collective-permute-start(bf16[1024,128]{1,0:T(8,128)(2,1)S(1)} %collective-permute-done.13), channel_id=1, source_target_pairs={{0,32},{32,64},{64,96},{96,128},{128,160},{160,192},{192,224},{224... | collective-permute-start | bytes 786440 | tf_op jit(solution)/shard_map/ppermute | solution.py:50
  122.1 3.7 %collective-permute-done.15 = bf16[1024,128]{1,0:T(8,128)(2,1)S(1)} collective-permute-done((bf16[1024,128]{1,0:T(8,128)(2,1)S(1)}, bf16[1024,128]{1,0:T(8,128)(2,1)S(1)}, u32[]{:S(2)}, u32[]{:S(2)}) %collective-permute-start.15) | collective-permute-done | bytes 262176 | tf_op jit(solution)/shard_map/ppermute | solution.py:50
  125.8 3.8 %convolution_convert_fusion = bf16[1024,512]{1,0:T(8,128)(2,1)} fusion(bf16[1024,128]{1,0:T(8,128)(2,1)S(1)} %collective-permute-done.16, bf16[1024,128]{1,0:T(8,128)(2,1)S(1)} %collective-permute-done.15, bf16[1024,128]{1,0:T(8,128)(2,1)S(1)} %collective-permute-done.14, bf16[1024,128]{1,0:T(8,128)(2,1)S(1)} %collective-permute-done.13, ...), kind=kOutput, calls=%fused_computation.2 | convolution fusion | flops 1082654720 | bytes 4194304 | tf_op jit(solution)/shard_map/dot_general | solution.py:62
  129.6 10.8 %all-to-all-start.3 = ((bf16[32,32,512]{2,1,0:T(8,128)(2,1)}), bf16[32,32,512]{2,1,0:T(8,128)(2,1)}, u32[]{:S(2)}, u32[]{:S(2)}) async-start(bf16[32,32,512]{2,1,0:T(8,128)(2,1)} %bitcast.43), calls=%async_computation.3 | async-start | bytes 2097152 | tf_op jit(solution)/shard_map/all_to_all | solution.py:66
  140.9 16.1 %all-to-all-done.3 = bf16[32,32,512]{2,1,0:T(8,128)(2,1)} async-done(((bf16[32,32,512]{2,1,0:T(8,128)(2,1)}), bf16[32,32,512]{2,1,0:T(8,128)(2,1)}, u32[]{:S(2)}, u32[]{:S(2)}) %all-to-all-start.3) | async-done | bytes 1048608 | tf_op jit(solution)/shard_map/all_to_all | solution.py:66
  159.2 11.3 %all_to_all.25 = bf16[16,32,256]{2,1,0:T(8,128)(2,1)S(1)} all-to-all(bf16[16,32,256]{2,1,0:T(8,128)(2,1)S(1)} %bitcast.46), channel_id=1, replica_groups=mesh['z'=16,'core'=2,'col'=16] {'col'}, dimensions={0} | all-to-all | bytes 524288 | tf_op jit(solution)/shard_map/all_to_all | solution.py:79
  (57 shorter events, 12.8 us)
Async XLA Ops:
  0.0 1.2 copy-start
  1.2 8.9 %copy-start.9 = (s32[8,1]{0,1:T(1,128)S(1)}, s32[8,1]{0,1:T(1,128)}, u32[]{:S(2)}) copy-start(s32[8,1]{0,1:T(1,128)} %param.8) | copy-start | bytes 100
  1.2 9.0 %copy-start.3 = (bf16[1024,128]{1,0:T(8,128)(2,1)S(1)}, bf16[1024,128]{1,0:T(8,128)(2,1)}, u32[]{:S(2)}) copy-start(bf16[1024,128]{1,0:T(8,128)(2,1)} %param.6) | copy-start | bytes 786436
  1.4 21.5 %collective-permute-start = (bf16[512,1024]{1,0:T(8,128)(2,1)S(1)}, bf16[512,1024]{1,0:T(8,128)(2,1)}, u32[]{:S(2)}, u32[]{:S(2)}) collective-permute-start(bf16[512,1024]{1,0:T(8,128)(2,1)S(1)} %bitcast_multiply_fusion), channel_id=1, source_target_pairs={{0,16},{16,0},{32,48},{48,32},{64,80},{80,64},{96,112},{112,96},{1... | collective-permute-start | bytes 3145736 | tf_op jit(solution)/shard_map/ppermute | solution.py:54
  10.4 3.6 %collective-permute-start.2 = (bf16[1024,128]{1,0:T(8,128)(2,1)S(1)}, bf16[1024,128]{1,0:T(8,128)(2,1)S(1)}, u32[]{:S(2)}, u32[]{:S(2)}) collective-permute-start(bf16[1024,128]{1,0:T(8,128)(2,1)S(1)} %broadcast_multiply_fusion), channel_id=1, source_target_pairs={{16,32},{48,64},{80,96},{112,128},{144,160},{176,192},{208,224},{2... | collective-permute-start | bytes 786440 | tf_op jit(solution)/shard_map/ppermute | solution.py:50
  10.5 9.3 %collective-permute-start.1 = (bf16[1024,128]{1,0:T(8,128)(2,1)S(1)}, bf16[1024,128]{1,0:T(8,128)(2,1)}, u32[]{:S(2)}, u32[]{:S(2)}) collective-permute-start(bf16[1024,128]{1,0:T(8,128)(2,1)S(1)} %broadcast_multiply_fusion), channel_id=1, source_target_pairs={{0,32},{32,64},{64,96},{96,128},{128,160},{160,192},{192,224},{224... | collective-permute-start | bytes 786440 | tf_op jit(solution)/shard_map/ppermute | solution.py:50
  14.0 10.2 %collective-permute-start.4 = (bf16[1024,128]{1,0:T(8,128)(2,1)S(1)}, bf16[1024,128]{1,0:T(8,128)(2,1)S(1)}, u32[]{:S(2)}, u32[]{:S(2)}) collective-permute-start(bf16[1024,128]{1,0:T(8,128)(2,1)S(1)} %collective-permute-done.2), channel_id=1, source_target_pairs={{0,32},{32,64},{64,96},{96,128},{128,160},{160,192},{192,224},{224... | collective-permute-start | bytes 786440 | tf_op jit(solution)/shard_map/ppermute | solution.py:50
  19.8 7.6 %collective-permute-start.3 = (bf16[1024,128]{1,0:T(8,128)(2,1)}, bf16[1024,128]{1,0:T(8,128)(2,1)S(1)}, u32[]{:S(2)}, u32[]{:S(2)}) collective-permute-start(bf16[1024,128]{1,0:T(8,128)(2,1)} %collective-permute-done.1), channel_id=1, source_target_pairs={{0,32},{32,64},{64,96},{96,128},{128,160},{160,192},{192,224},{224... | collective-permute-start | bytes 786440 | tf_op jit(solution)/shard_map/ppermute | solution.py:50
  24.2 36.3 %copy-start.2 = (bf16[512,1024]{1,0:T(8,128)(2,1)}, bf16[512,1024]{1,0:T(8,128)(2,1)S(1)}, u32[]{:S(2)}) copy-start(bf16[512,1024]{1,0:T(8,128)(2,1)S(1)} %get-tuple-element.6) | copy-start | bytes 3145732
  24.2 68.3 %copy-start.1 = (bf16[512,1024]{1,0:T(8,128)(2,1)}, bf16[512,1024]{1,0:T(8,128)(2,1)S(1)}, u32[]{:S(2)}) copy-start(bf16[512,1024]{1,0:T(8,128)(2,1)S(1)} %get-tuple-element.5) | copy-start | bytes 3145732
  24.2 6.5 %copy-start.4 = (bf16[1024,128]{1,0:T(8,128)(2,1)}, bf16[1024,128]{1,0:T(8,128)(2,1)S(1)}, u32[]{:S(2)}) copy-start(bf16[1024,128]{1,0:T(8,128)(2,1)S(1)} %collective-permute-done.4) | copy-start | bytes 786436
  27.4 3.3 %copy-start.6 = (bf16[1024,128]{1,0:T(8,128)(2,1)}, bf16[1024,128]{1,0:T(8,128)(2,1)S(1)}, u32[]{:S(2)}) copy-start(bf16[1024,128]{1,0:T(8,128)(2,1)S(1)} %collective-permute-done.3) | copy-start | bytes 786436
  30.7 11.2 %copy-start.5 = (bf16[1024,128]{1,0:T(8,128)(2,1)S(1)}, bf16[1024,128]{1,0:T(8,128)(2,1)}, u32[]{:S(2)}) copy-start(bf16[1024,128]{1,0:T(8,128)(2,1)} %copy-done.4) | copy-start | bytes 786436
  30.7 32.8 %all-to-all-start = ((bf16[32,32,512]{2,1,0:T(8,128)(2,1)}), bf16[32,32,512]{2,1,0:T(8,128)(2,1)S(1)}, u32[]{:S(2)}, u32[]{:S(2)}) async-start(bf16[32,32,512]{2,1,0:T(8,128)(2,1)} %bitcast.42), calls=%async_computation | async-start | bytes 2097152 | tf_op jit(solution)/shard_map/all_to_all | solution.py:66
  41.9 7.4 %collective-permute-start.6 = (bf16[1024,128]{1,0:T(8,128)(2,1)S(1)}, bf16[1024,128]{1,0:T(8,128)(2,1)S(1)}, u32[]{:S(2)}, u32[]{:S(2)}) collective-permute-start(bf16[1024,128]{1,0:T(8,128)(2,1)S(1)} %copy-done.5), channel_id=1, source_target_pairs={{0,32},{32,64},{64,96},{96,128},{128,160},{160,192},{192,224},{224... | collective-permute-start | bytes 786440 | tf_op jit(solution)/shard_map/ppermute | solution.py:50
  44.8 8.3 %collective-permute-start.5 = (bf16[1024,128]{1,0:T(8,128)(2,1)}, bf16[1024,128]{1,0:T(8,128)(2,1)S(1)}, u32[]{:S(2)}, u32[]{:S(2)}) collective-permute-start(bf16[1024,128]{1,0:T(8,128)(2,1)} %copy-done.6), channel_id=1, source_target_pairs={{0,32},{32,64},{64,96},{96,128},{128,160},{160,192},{192,224},{224... | collective-permute-start | bytes 786440 | tf_op jit(solution)/shard_map/ppermute | solution.py:50
  49.3 7.4 %collective-permute-start.8 = (bf16[1024,128]{1,0:T(8,128)(2,1)S(1)}, bf16[1024,128]{1,0:T(8,128)(2,1)S(1)}, u32[]{:S(2)}, u32[]{:S(2)}) collective-permute-start(bf16[1024,128]{1,0:T(8,128)(2,1)S(1)} %collective-permute-done.6), channel_id=1, source_target_pairs={{0,32},{32,64},{64,96},{96,128},{128,160},{160,192},{192,224},{224... | collective-permute-start | bytes 786440 | tf_op jit(solution)/shard_map/ppermute | solution.py:50
  53.2 7.4 %collective-permute-start.7 = (bf16[1024,128]{1,0:T(8,128)(2,1)S(1)}, bf16[1024,128]{1,0:T(8,128)(2,1)S(1)}, u32[]{:S(2)}, u32[]{:S(2)}) collective-permute-start(bf16[1024,128]{1,0:T(8,128)(2,1)S(1)} %collective-permute-done.5), channel_id=1, source_target_pairs={{0,32},{32,64},{64,96},{96,128},{128,160},{160,192},{192,224},{224... | collective-permute-start | bytes 786440 | tf_op jit(solution)/shard_map/ppermute | solution.py:50
  60.6 0.7 copy-start.7
  63.5 33.2 %all-to-all-start.1 = ((bf16[32,32,512]{2,1,0:T(8,128)(2,1)}), bf16[32,32,512]{2,1,0:T(8,128)(2,1)S(1)}, u32[]{:S(2)}, u32[]{:S(2)}) async-start(bf16[32,32,512]{2,1,0:T(8,128)(2,1)} %bitcast.41), calls=%async_computation.1 | async-start | bytes 2097152 | tf_op jit(solution)/shard_map/all_to_all | solution.py:66
  74.0 7.4 %collective-permute-start.10 = (bf16[1024,128]{1,0:T(8,128)(2,1)S(1)}, bf16[1024,128]{1,0:T(8,128)(2,1)S(1)}, u32[]{:S(2)}, u32[]{:S(2)}) collective-permute-start(bf16[1024,128]{1,0:T(8,128)(2,1)S(1)} %collective-permute-done.8), channel_id=1, source_target_pairs={{0,32},{32,64},{64,96},{96,128},{128,160},{160,192},{192,224},{224... | collective-permute-start | bytes 786440 | tf_op jit(solution)/shard_map/ppermute | solution.py:50
  76.8 8.3 %collective-permute-start.9 = (bf16[1024,128]{1,0:T(8,128)(2,1)}, bf16[1024,128]{1,0:T(8,128)(2,1)S(1)}, u32[]{:S(2)}, u32[]{:S(2)}) collective-permute-start(bf16[1024,128]{1,0:T(8,128)(2,1)} %copy-done.7), channel_id=1, source_target_pairs={{0,32},{32,64},{64,96},{96,128},{128,160},{160,192},{192,224},{224... | collective-permute-start | bytes 786440 | tf_op jit(solution)/shard_map/ppermute | solution.py:50
  81.4 7.4 %collective-permute-start.12 = (bf16[1024,128]{1,0:T(8,128)(2,1)S(1)}, bf16[1024,128]{1,0:T(8,128)(2,1)S(1)}, u32[]{:S(2)}, u32[]{:S(2)}) collective-permute-start(bf16[1024,128]{1,0:T(8,128)(2,1)S(1)} %collective-permute-done.10), channel_id=1, source_target_pairs={{0,32},{32,64},{64,96},{96,128},{128,160},{160,192},{192,224},{224... | collective-permute-start | bytes 786440 | tf_op jit(solution)/shard_map/ppermute | solution.py:50
  85.1 7.4 %collective-permute-start.11 = (bf16[1024,128]{1,0:T(8,128)(2,1)S(1)}, bf16[1024,128]{1,0:T(8,128)(2,1)S(1)}, u32[]{:S(2)}, u32[]{:S(2)}) collective-permute-start(bf16[1024,128]{1,0:T(8,128)(2,1)S(1)} %collective-permute-done.9), channel_id=1, source_target_pairs={{0,32},{32,64},{64,96},{96,128},{128,160},{160,192},{192,224},{224... | collective-permute-start | bytes 786440 | tf_op jit(solution)/shard_map/ppermute | solution.py:50
  92.5 0.7 copy-start.8
  96.7 32.9 %all-to-all-start.2 = ((bf16[32,32,512]{2,1,0:T(8,128)(2,1)}), bf16[32,32,512]{2,1,0:T(8,128)(2,1)S(1)}, u32[]{:S(2)}, u32[]{:S(2)}) async-start(bf16[32,32,512]{2,1,0:T(8,128)(2,1)} %bitcast.40), calls=%async_computation.2 | async-start | bytes 2097152 | tf_op jit(solution)/shard_map/all_to_all | solution.py:66
  107.3 7.4 %collective-permute-start.14 = (bf16[1024,128]{1,0:T(8,128)(2,1)S(1)}, bf16[1024,128]{1,0:T(8,128)(2,1)S(1)}, u32[]{:S(2)}, u32[]{:S(2)}) collective-permute-start(bf16[1024,128]{1,0:T(8,128)(2,1)S(1)} %collective-permute-done.12), channel_id=1, source_target_pairs={{0,32},{32,64},{64,96},{96,128},{128,160},{160,192},{192,224},{224... | collective-permute-start | bytes 786440 | tf_op jit(solution)/shard_map/ppermute | solution.py:50
  110.1 8.3 %collective-permute-start.13 = (bf16[1024,128]{1,0:T(8,128)(2,1)}, bf16[1024,128]{1,0:T(8,128)(2,1)S(1)}, u32[]{:S(2)}, u32[]{:S(2)}) collective-permute-start(bf16[1024,128]{1,0:T(8,128)(2,1)} %copy-done.8), channel_id=1, source_target_pairs={{0,32},{32,64},{64,96},{96,128},{128,160},{160,192},{192,224},{224... | collective-permute-start | bytes 786440 | tf_op jit(solution)/shard_map/ppermute | solution.py:50
  114.7 7.4 %collective-permute-start.16 = (bf16[1024,128]{1,0:T(8,128)(2,1)S(1)}, bf16[1024,128]{1,0:T(8,128)(2,1)S(1)}, u32[]{:S(2)}, u32[]{:S(2)}) collective-permute-start(bf16[1024,128]{1,0:T(8,128)(2,1)S(1)} %collective-permute-done.14), channel_id=1, source_target_pairs={{0,32},{32,64},{64,96},{96,128},{128,160},{160,192},{192,224},{224... | collective-permute-start | bytes 786440 | tf_op jit(solution)/shard_map/ppermute | solution.py:50
  118.4 7.4 %collective-permute-start.15 = (bf16[1024,128]{1,0:T(8,128)(2,1)S(1)}, bf16[1024,128]{1,0:T(8,128)(2,1)S(1)}, u32[]{:S(2)}, u32[]{:S(2)}) collective-permute-start(bf16[1024,128]{1,0:T(8,128)(2,1)S(1)} %collective-permute-done.13), channel_id=1, source_target_pairs={{0,32},{32,64},{64,96},{96,128},{128,160},{160,192},{192,224},{224... | collective-permute-start | bytes 786440 | tf_op jit(solution)/shard_map/ppermute | solution.py:50
  129.6 10.8 %copy-start.10 = (s32[32]{0:T(128)S(1)}, s32[32]{0:T(128)}, u32[]{:S(2)}) copy-start(s32[32]{0:T(128)} %param.9) | copy-start | bytes 388
  129.6 27.4 %all-to-all-start.3 = ((bf16[32,32,512]{2,1,0:T(8,128)(2,1)}), bf16[32,32,512]{2,1,0:T(8,128)(2,1)}, u32[]{:S(2)}, u32[]{:S(2)}) async-start(bf16[32,32,512]{2,1,0:T(8,128)(2,1)} %bitcast.43), calls=%async_computation.3 | async-start | bytes 2097152 | tf_op jit(solution)/shard_map/all_to_all | solution.py:66
where the time goes:
time: 172 us; the launch traced here: 171 us
  starting transfers between devices  96.6 us (56%)
  waiting for transfers between devices  42.4 us (25%)
  matrix products  12.8 us (7%)
  blocking collectives  11.3 us (7%)
  other arithmetic  4.33 us (3%)
  local copies, waits for them, and re-layouts  3.44 us (2%)
    ppermute x16, starting transfers between devices, on_device(): current[stream] = lax.ppermute(current[stream], row, pairs)  44.8 us
    all_to_all x4, starting transfers between devices, on_device(): moved = lax.all_to_all(product, ('core', 'col'), 0, 0, tiled=True)  43.1 us
    ppermute x16, waiting for transfers between devices, on_device(): current[stream] = lax.ppermute(current[stream], row, pairs)  26.3 us
    all_to_all x4, waiting for transfers between devices, on_device(): moved = lax.all_to_all(product, ('core', 'col'), 0, 0, tiled=True)  16.1 us
    dot_general x4, matrix products, on_device(): jnp.dot(amp, right, preferred_element_type=jnp.float32).astype(jnp.bfloat16)  12.8 us
    all_to_all x1, blocking collectives, on_device(): final = lax.all_to_all(picked, 'col', 0, 0, tiled=True)  11.3 us
    ppermute x1, starting transfers between devices, on_device(): other_amp = lax.ppermute(own_amp, row, swap)  8.75 us
  transfers between devices with their start and end apart: 21, of which 12 were waited for; matrix products, arithmetic and copies ran while one was open for 7% of the time, Pallas kernels for 0%

commit v1 on v0

v1 whole, which is shorter than its diff:
```python
import jax
import jax.numpy as jnp
from jax import lax
from jax.sharding import Mesh, PartitionSpec as P


TILE = 128


def mask_tiles(matrix, occupancy):
    nrow, ncolumn = matrix.shape
    blocks = matrix.reshape(nrow // TILE, TILE, ncolumn // TILE, TILE)
    return (blocks * occupancy[:, None, :, None].astype(jnp.bfloat16)).reshape(nrow, ncolumn)


def rank(nz, ncol, z, core, col):
    return ((z % nz) * 2 + core) * ncol + col


def ring_pairs(nz, ncol):
    pairs = []
    for z in range(nz):
        for col in range(ncol):
            pairs.append((rank(nz, ncol, z, 0, col), rank(nz, ncol, z + 1, 0, col)))
            pairs.append((rank(nz, ncol, z, 1, col), rank(nz, ncol, z - 1, 1, col)))
    return pairs


def first_pairs(nz, ncol, stream):
    pairs = []
    for z in range(nz):
        for col in range(ncol):
            even = col & ~1
            for core in (0, 1):
                source = rank(nz, ncol, z, col & 1, even | (core ^ stream))
                target = rank(nz, ncol, z + 1 if core == 0 else z, core, col)
                pairs.append((source, target))
    return pairs


def swap_pairs(nz, ncol, core, col):
    return [
        (rank(nz, ncol, z, c, x), rank(nz, ncol, z, c ^ core, x ^ col))
        for z in range(nz) for c in (0, 1) for x in range(ncol)
    ]


def chunks_of(nslot):
    last = 3 * nslot // 8
    return (nslot - last, last)


def make(nz, ncol):
    every = ("z", "core", "col")
    nslot = nz // 2
    sizes = chunks_of(nslot)
    ends = [sum(sizes[: i + 1]) for i in range(len(sizes))]

    def on_device(amplitudes, integrals, amp_occupancy, int_occupancy, owner_map):
        z = lax.axis_index("z")
        core = lax.axis_index("core")
        odd = lax.axis_index("col") % 2
        own_tile = mask_tiles(integrals, int_occupancy)
        nrow, kloc = amplitudes.shape
        part = nrow // ncol
        current = [own_tile, own_tile]
        sums = []
        tiles = [[], []]
        for slot in range(1, nslot + 1):
            for stream in (0, 1):
                pairs = first_pairs(nz, ncol, stream) if slot == 1 else ring_pairs(nz, ncol)
                current[stream] = lax.ppermute(current[stream], every, pairs)
                tiles[stream].append(current[stream])
            if slot == 1:
                own = mask_tiles(amplitudes, amp_occupancy)
                beside = lax.ppermute(own, every, swap_pairs(nz, ncol, 0, 1))
                own_other = lax.ppermute(own, every, swap_pairs(nz, ncol, 1, 0))
                beside_other = lax.ppermute(beside, every, swap_pairs(nz, ncol, 1, 0))
                first = (odd ^ core) * kloc
                second = kloc - first
                mine = core * nrow
                theirs = nrow - mine
                amp = jnp.zeros((2 * nrow, 2 * kloc), jnp.bfloat16)
                amp = lax.dynamic_update_slice(amp, own, (mine, first))
                amp = lax.dynamic_update_slice(amp, own_other, (theirs, first))
                amp = lax.dynamic_update_slice(amp, beside, (mine, second))
                amp = lax.dynamic_update_slice(amp, beside_other, (theirs, second))
            if slot in ends:
                right = jnp.concatenate([jnp.concatenate(t, 1) for t in tiles], 0)
                product = jnp.dot(amp, right, preferred_element_type=jnp.float32).astype(jnp.bfloat16)
                tiles = [[], []]
                width = product.shape[1]
                product = product.reshape(2 * ncol, part, width)
                moved = lax.all_to_all(product, ("core", "col"), 0, 0, tiled=True)
                moved = moved.reshape(2, ncol // 2, 2, part, width)
                total = jnp.sum(moved.astype(jnp.float32), 1)
                sums.append(total.astype(jnp.bfloat16))
        done = jnp.concatenate(sums, 3).reshape(4, part, nslot, TILE)
        done = done.transpose(0, 2, 1, 3).reshape(4 * nslot, part, TILE)
        chip = owner_map // 2
        parity = owner_map % 2
        behind = (z - chip) % nz
        upward = (behind >= 1) & (behind <= nslot)
        side = jnp.where(upward, 0, 2)
        slot_of = jnp.where(upward, behind - 1, (chip - z) % nz)
        place = (side + parity) * nslot + slot_of
        picked = done[place].reshape(ncol, 2, part, TILE).transpose(0, 2, 1, 3).reshape(ncol, part, 2 * TILE)
        final = lax.all_to_all(picked, "col", 0, 0, tiled=True)
        return final.reshape(nrow, 2 * TILE)

    return on_device


def solution(mesh):
    nz = mesh.shape["row"] // 2
    ncol = mesh.shape["col"]
    fine = Mesh(mesh.devices.reshape(nz, 2, ncol), ("z", "core", "col"))
    split = ("z", "core")
    placed = (P(split, "col"), P("col", split), P(split, "col"), P("col", split), P())
    return jax.shard_map(
        make(nz, ncol), mesh=fine, in_specs=placed, out_specs=P(split, "col"), check_vma=False
    )
```

time: 172 us -> 187 us (1.087)
  the two profiles are of different devices: /device:TPU:1 before, /device:TPU:64 now
where the time goes in v1:
time: 187 us; the launch traced here: 185 us
  starting transfers between devices  86.8 us (46%)
  local copies, waits for them, and re-layouts  41.7 us (22%)
  waiting for transfers between devices  28.7 us (15%)
  matrix products  12.2 us (7%)
  blocking collectives  11.5 us (6%)
  other arithmetic  3.34 us (2%)
    ppermute x16, starting transfers between devices, on_device(): current[stream] = lax.ppermute(current[stream], every, pairs)  65.5 us
    all_to_all x2, waiting for transfers between devices, on_device(): moved = lax.all_to_all(product, ('core', 'col'), 0, 0, tiled=True)  27.3 us
    dot_general x2, matrix products, on_device(): jnp.dot(amp, right, preferred_element_type=jnp.float32).astype(jnp.bfloat16)  12.2 us
    all_to_all x1, blocking collectives, on_device(): final = lax.all_to_all(picked, 'col', 0, 0, tiled=True)  11.5 us
    all_to_all x2, starting transfers between devices, on_device(): moved = lax.all_to_all(product, ('core', 'col'), 0, 0, tiled=True)  11.4 us
    dynamic_update_slice x1, local copies, waits for them, and re-layouts, on_device(): amp = lax.dynamic_update_slice(amp, beside, (mine, second))  10.3 us
    dynamic_update_slice x1, local copies, waits for them, and re-layouts, on_device(): amp = lax.dynamic_update_slice(amp, own_other, (theirs, first))  10.3 us
    dynamic_update_slice x1, local copies, waits for them, and re-layouts, on_device(): amp = lax.dynamic_update_slice(amp, beside_other, (theirs, second))  9.65 us
  transfers between devices with their start and end apart: 21, of which 4 were waited for; matrix products, arithmetic and copies ran while one was open for 25% of the time, Pallas kernels for 0%

profile of v1, /device:TPU:64, one launch (start us, length us, event | category | flops | bytes accessed | tf_op | source)
XLA Modules:
  0.0 184.8 jit_solution(8750200398800430553)
XLA Ops:
  0.7 1.1 broadcast_multiply_fusion
  1.9 3.8 %collective-permute-start.3 = (bf16[1024,128]{1,0:T(8,128)(2,1)S(1)}, bf16[1024,128]{1,0:T(8,128)(2,1)S(1)}, u32[]{:S(2)}, u32[]{:S(2)}) collective-permute-start(bf16[1024,128]{1,0:T(8,128)(2,1)S(1)} %broadcast_multiply_fusion), channel_id=1, source_target_pairs={{0,32},{1,16},{16,33},{17,17},{2,34},{3,18},{18,35},{19,19},{4,36}... | collective-permute-start | bytes 786440 | tf_op jit(solution)/shard_map/ppermute | solution.py:72
  5.7 3.0 %collective-permute-start.8 = (bf16[1024,128]{1,0:T(8,128)(2,1)S(1)}, bf16[1024,128]{1,0:T(8,128)(2,1)S(1)}, u32[]{:S(2)}, u32[]{:S(2)}) collective-permute-start(bf16[1024,128]{1,0:T(8,128)(2,1)S(1)} %broadcast_multiply_fusion), channel_id=1, source_target_pairs={{1,32},{0,16},{17,33},{16,17},{3,34},{2,18},{19,35},{18,19},{5,36}... | collective-permute-start | bytes 786440 | tf_op jit(solution)/shard_map/ppermute | solution.py:72
  11.3 2.0 %copy-done = bf16[1024,2048]{1,0:T(8,128)(2,1)} copy-done((bf16[1024,2048]{1,0:T(8,128)(2,1)}, bf16[1024,2048]{1,0:T(8,128)(2,1)S(1)}, u32[]{:S(2)}) %copy-start) | copy-done | bytes 4194328
  13.3 5.4 %collective-permute-start.1 = (bf16[512,1024]{1,0:T(8,128)(2,1)S(1)}, bf16[512,1024]{1,0:T(8,128)(2,1)S(1)}, u32[]{:S(2)}, u32[]{:S(2)}) collective-permute-start(bf16[512,1024]{1,0:T(8,128)(2,1)S(1)} %get-tuple-element.6), channel_id=1, source_target_pairs={{0,1},{1,0},{2,3},{3,2},{4,5},{5,4},{6,7},{7,6},{8,9},{9,8},{10,11... | collective-permute-start | bytes 3145736 | tf_op jit(solution)/shard_map/ppermute | solution.py:76
  18.7 3.8 %collective-permute-start.4 = (bf16[1024,128]{1,0:T(8,128)(2,1)S(1)}, bf16[1024,128]{1,0:T(8,128)(2,1)S(1)}, u32[]{:S(2)}, u32[]{:S(2)}) collective-permute-start(bf16[1024,128]{1,0:T(8,128)(2,1)S(1)} %collective-permute-done.3), channel_id=1, source_target_pairs={{0,32},{16,496},{1,33},{17,497},{2,34},{18,498},{3,35},{19,499},{4... | collective-permute-start | bytes 786440 | tf_op jit(solution)/shard_map/ppermute | solution.py:72
  22.6 3.8 %collective-permute-start.9 = (bf16[1024,128]{1,0:T(8,128)(2,1)S(1)}, bf16[1024,128]{1,0:T(8,128)(2,1)S(1)}, u32[]{:S(2)}, u32[]{:S(2)}) collective-permute-start(bf16[1024,128]{1,0:T(8,128)(2,1)S(1)} %collective-permute-done.8), channel_id=1, source_target_pairs={{0,32},{16,496},{1,33},{17,497},{2,34},{18,498},{3,35},{19,499},{4... | collective-permute-start | bytes 786440 | tf_op jit(solution)/shard_map/ppermute | solution.py:72
  27.0 3.8 %collective-permute-start.5 = (bf16[1024,128]{1,0:T(8,128)(2,1)S(1)}, bf16[1024,128]{1,0:T(8,128)(2,1)S(1)}, u32[]{:S(2)}, u32[]{:S(2)}) collective-permute-start(bf16[1024,128]{1,0:T(8,128)(2,1)S(1)} %collective-permute-done.4), channel_id=1, source_target_pairs={{0,32},{16,496},{1,33},{17,497},{2,34},{18,498},{3,35},{19,499},{4... | collective-permute-start | bytes 786440 | tf_op jit(solution)/shard_map/ppermute | solution.py:72
  30.9 5.0 %collective-permute-start.10 = (bf16[1024,128]{1,0:T(8,128)(2,1)S(1)}, bf16[1024,128]{1,0:T(8,128)(2,1)S(1)}, u32[]{:S(2)}, u32[]{:S(2)}) collective-permute-start(bf16[1024,128]{1,0:T(8,128)(2,1)S(1)} %collective-permute-done.9), channel_id=1, source_target_pairs={{0,32},{16,496},{1,33},{17,497},{2,34},{18,498},{3,35},{19,499},{4... | collective-permute-start | bytes 786440 | tf_op jit(solution)/shard_map/ppermute | solution.py:72
  35.9 3.8 %collective-permute-start.6 = (bf16[1024,128]{1,0:T(8,128)(2,1)S(1)}, bf16[1024,128]{1,0:T(8,128)(2,1)}, u32[]{:S(2)}, u32[]{:S(2)}) collective-permute-start(bf16[1024,128]{1,0:T(8,128)(2,1)S(1)} %collective-permute-done.5), channel_id=1, source_target_pairs={{0,32},{16,496},{1,33},{17,497},{2,34},{18,498},{3,35},{19,499},{4... | collective-permute-start | bytes 786440 | tf_op jit(solution)/shard_map/ppermute | solution.py:72
  39.8 5.6 %collective-permute-start.11 = (bf16[1024,128]{1,0:T(8,128)(2,1)S(1)}, bf16[1024,128]{1,0:T(8,128)(2,1)}, u32[]{:S(2)}, u32[]{:S(2)}) collective-permute-start(bf16[1024,128]{1,0:T(8,128)(2,1)S(1)} %collective-permute-done.10), channel_id=1, source_target_pairs={{0,32},{16,496},{1,33},{17,497},{2,34},{18,498},{3,35},{19,499},{4... | collective-permute-start | bytes 786440 | tf_op jit(solution)/shard_map/ppermute | solution.py:72
  45.4 3.8 %collective-permute-start.7 = (bf16[1024,128]{1,0:T(8,128)(2,1)}, bf16[1024,128]{1,0:T(8,128)(2,1)}, u32[]{:S(2)}, u32[]{:S(2)}) collective-permute-start(bf16[1024,128]{1,0:T(8,128)(2,1)} %collective-permute-done.6), channel_id=1, source_target_pairs={{0,32},{16,496},{1,33},{17,497},{2,34},{18,498},{3,35},{19,499},{4... | collective-permute-start | bytes 786440 | tf_op jit(solution)/shard_map/ppermute | solution.py:72
  49.2 5.7 %collective-permute-start.12 = (bf16[1024,128]{1,0:T(8,128)(2,1)}, bf16[1024,128]{1,0:T(8,128)(2,1)}, u32[]{:S(2)}, u32[]{:S(2)}) collective-permute-start(bf16[1024,128]{1,0:T(8,128)(2,1)} %collective-permute-done.11), channel_id=1, source_target_pairs={{0,32},{16,496},{1,33},{17,497},{2,34},{18,498},{3,35},{19,499},{4... | collective-permute-start | bytes 786440 | tf_op jit(solution)/shard_map/ppermute | solution.py:72
  55.0 1.9 %collective-permute-start = (bf16[512,1024]{1,0:T(8,128)(2,1)S(1)}, bf16[512,1024]{1,0:T(8,128)(2,1)S(1)}, u32[]{:S(2)}, u32[]{:S(2)}) collective-permute-start(bf16[512,1024]{1,0:T(8,128)(2,1)S(1)} %get-tuple-element.6), channel_id=1, source_target_pairs={{0,16},{1,17},{2,18},{3,19},{4,20},{5,21},{6,22},{7,23},{8,24},{9,... | collective-permute-start | bytes 3145736 | tf_op jit(solution)/shard_map/ppermute | solution.py:77
  57.0 2.5 %collective-permute-start.2 = (bf16[512,1024]{1,0:T(8,128)(2,1)S(1)}, bf16[512,1024]{1,0:T(8,128)(2,1)S(1)}, u32[]{:S(2)}, u32[]{:S(2)}) collective-permute-start(bf16[512,1024]{1,0:T(8,128)(2,1)S(1)} %collective-permute-done.1), channel_id=1, source_target_pairs={{0,16},{1,17},{2,18},{3,19},{4,20},{5,21},{6,22},{7,23},{8,24},{9,... | collective-permute-start | bytes 3145736 | tf_op jit(solution)/shard_map/ppermute | solution.py:78
  59.5 3.8 %collective-permute-start.13 = (bf16[1024,128]{1,0:T(8,128)(2,1)}, bf16[1024,128]{1,0:T(8,128)(2,1)S(1)}, u32[]{:S(2)}, u32[]{:S(2)}) collective-permute-start(bf16[1024,128]{1,0:T(8,128)(2,1)} %collective-permute-done.7), channel_id=1, source_target_pairs={{0,32},{16,496},{1,33},{17,497},{2,34},{18,498},{3,35},{19,499},{4... | collective-permute-start | bytes 786440 | tf_op jit(solution)/shard_map/ppermute | solution.py:72
  63.4 1.9 %collective-permute-start.16 = (bf16[1024,128]{1,0:T(8,128)(2,1)}, bf16[1024,128]{1,0:T(8,128)(2,1)S(1)}, u32[]{:S(2)}, u32[]{:S(2)}) collective-permute-start(bf16[1024,128]{1,0:T(8,128)(2,1)} %collective-permute-done.12), channel_id=1, source_target_pairs={{0,32},{16,496},{1,33},{17,497},{2,34},{18,498},{3,35},{19,499},{4... | collective-permute-start | bytes 786440 | tf_op jit(solution)/shard_map/ppermute | solution.py:72
  68.0 3.8 %collective-permute-start.14 = (bf16[1024,128]{1,0:T(8,128)(2,1)S(1)}, bf16[1024,128]{1,0:T(8,128)(2,1)S(1)}, u32[]{:S(2)}, u32[]{:S(2)}) collective-permute-start(bf16[1024,128]{1,0:T(8,128)(2,1)S(1)} %collective-permute-done.13), channel_id=1, source_target_pairs={{0,32},{16,496},{1,33},{17,497},{2,34},{18,498},{3,35},{19,499},{4... | collective-permute-start | bytes 786440 | tf_op jit(solution)/shard_map/ppermute | solution.py:72
  71.8 4.5 %collective-permute-start.17 = (bf16[1024,128]{1,0:T(8,128)(2,1)S(1)}, bf16[1024,128]{1,0:T(8,128)(2,1)S(1)}, u32[]{:S(2)}, u32[]{:S(2)}) collective-permute-start(bf16[1024,128]{1,0:T(8,128)(2,1)S(1)} %collective-permute-done.16), channel_id=1, source_target_pairs={{0,32},{16,496},{1,33},{17,497},{2,34},{18,498},{3,35},{19,499},{4... | collective-permute-start | bytes 786440 | tf_op jit(solution)/shard_map/ppermute | solution.py:72
  76.6 3.6 %collective-permute-start.15 = (bf16[1024,128]{1,0:T(8,128)(2,1)S(1)}, bf16[1024,128]{1,0:T(8,128)(2,1)S(1)}, u32[]{:S(2)}, u32[]{:S(2)}) collective-permute-start(bf16[1024,128]{1,0:T(8,128)(2,1)S(1)} %collective-permute-done.14), channel_id=1, source_target_pairs={{0,32},{16,496},{1,33},{17,497},{2,34},{18,498},{3,35},{19,499},{4... | collective-permute-start | bytes 786440 | tf_op jit(solution)/shard_map/ppermute | solution.py:72
  80.2 5.6 %collective-permute-start.18 = (bf16[1024,128]{1,0:T(8,128)(2,1)S(1)}, bf16[1024,128]{1,0:T(8,128)(2,1)S(1)}, u32[]{:S(2)}, u32[]{:S(2)}) collective-permute-start(bf16[1024,128]{1,0:T(8,128)(2,1)S(1)} %collective-permute-done.17), channel_id=1, source_target_pairs={{0,32},{16,496},{1,33},{17,497},{2,34},{18,498},{3,35},{19,499},{4... | collective-permute-start | bytes 786440 | tf_op jit(solution)/shard_map/ppermute | solution.py:72
  86.9 10.3 %dynamic_update_slice.13 = bf16[1024,2048]{1,0:T(8,128)(2,1)} dynamic-update-slice(bf16[1024,2048]{1,0:T(8,128)(2,1)} %copy-done, bf16[512,1024]{1,0:T(8,128)(2,1)S(1)} %collective-permute-done, s32[]{:T(128)S(6)} %select_n.55, s32[]{:T(128)S(6)} %select_n.54) | dynamic-update-slice | bytes 2097156 | tf_op jit(solution)/shard_map/dynamic_update_slice | solution.py:85
  97.1 10.3 %dynamic_update_slice.14 = bf16[1024,2048]{1,0:T(8,128)(2,1)} dynamic-update-slice(bf16[1024,2048]{1,0:T(8,128)(2,1)} %dynamic_update_slice.13, bf16[512,1024]{1,0:T(8,128)(2,1)S(1)} %collective-permute-done.1, s32[]{:T(128)S(6)} %select_n.52, s32[]{:T(128)S(6)} %select_n.56) | dynamic-update-slice | bytes 2097156 | tf_op jit(solution)/shard_map/dynamic_update_slice | solution.py:86
  108.5 1.2 constant_dynamic-update-slice_fusion
  109.7 9.7 %dynamic_update_slice.15 = bf16[1024,2048]{1,0:T(8,128)(2,1)} dynamic-update-slice(bf16[1024,2048]{1,0:T(8,128)(2,1)} %dynamic_update_slice.14, bf16[512,1024]{1,0:T(8,128)(2,1)S(1)} %collective-permute-done.2, s32[]{:T(128)S(6)} %select_n.55, s32[]{:T(128)S(6)} %select_n.56) | dynamic-update-slice | bytes 2097156 | tf_op jit(solution)/shard_map/dynamic_update_slice | solution.py:87
  119.4 5.5 %fusion.19 = bf16[1024,384]{1,0:T(8,128)(2,1)} fusion(bf16[1024,2048]{1,0:T(8,128)(2,1)} %dynamic_update_slice.15, bf16[1024,128]{1,0:T(8,128)(2,1)S(1)} %collective-permute-done.18, bf16[1024,128]{1,0:T(8,128)(2,1)S(1)} %collective-permute-done.17, bf16[1024,128]{1,0:T(8,128)(2,1)S(1)} %collective-permute-done.16, ...), kind=kOutput, calls=%fused_computation.18 | convolution fusion | flops 1620443136 | bytes 6553600 | tf_op jit(solution)/shard_map/dot_general | solution.py:90
  124.9 7.5 %all-to-all-start.1 = ((bf16[32,32,384]{2,1,0:T(8,128)(2,1)}), bf16[32,32,384]{2,1,0:T(8,128)(2,1)S(1)}, u32[]{:S(2)}, u32[]{:S(2)}) async-start(bf16[32,32,384]{2,1,0:T(8,128)(2,1)} %bitcast.4), calls=%async_computation.1 | async-start | bytes 1572864 | tf_op jit(solution)/shard_map/all_to_all | solution.py:94
  133.4 6.7 %fusion.4 = bf16[1024,640]{1,0:T(8,128)(2,1)} fusion(bf16[1024,2048]{1,0:T(8,128)(2,1)} %dynamic_update_slice.15, bf16[1024,640]{1,0:T(8,128)(2,1)S(1)} %constant_dynamic-update-slice_fusion.5, bf16[1024,640]{1,0:T(8,128)(2,1)S(1)} %copy-done.13), kind=kOutput, calls=%fused_computation.5 | convolution fusion | flops 2690252800 | bytes 8126464 | tf_op jit(solution)/shard_map/dot_general | solution.py:90
  140.1 6.9 %all-to-all-done.1 = bf16[32,32,384]{2,1,0:T(8,128)(2,1)S(1)} async-done(((bf16[32,32,384]{2,1,0:T(8,128)(2,1)}), bf16[32,32,384]{2,1,0:T(8,128)(2,1)S(1)}, u32[]{:S(2)}, u32[]{:S(2)}) %all-to-all-start.1) | async-done | bytes 786464 | tf_op jit(solution)/shard_map/all_to_all | solution.py:94
  147.1 4.0 %all-to-all-start = ((bf16[32,32,640]{2,1,0:T(8,128)(2,1)}), bf16[32,32,640]{2,1,0:T(8,128)(2,1)S(1)}, u32[]{:S(2)}, u32[]{:S(2)}) async-start(bf16[32,32,640]{2,1,0:T(8,128)(2,1)} %bitcast.2), calls=%async_computation | async-start | bytes 2621440 | tf_op jit(solution)/shard_map/all_to_all | solution.py:94
  151.2 20.4 %all-to-all-done = bf16[32,32,640]{2,1,0:T(8,128)(2,1)S(1)} async-done(((bf16[32,32,640]{2,1,0:T(8,128)(2,1)}), bf16[32,32,640]{2,1,0:T(8,128)(2,1)S(1)}, u32[]{:S(2)}, u32[]{:S(2)}) %all-to-all-start) | async-done | bytes 1310752 | tf_op jit(solution)/shard_map/all_to_all | solution.py:94
  172.6 11.5 %all_to_all.15 = bf16[16,32,256]{2,1,0:T(8,128)(2,1)S(1)} all-to-all(bf16[16,32,256]{2,1,0:T(8,128)(2,1)S(1)} %bitcast.40), channel_id=1, replica_groups=mesh['z'=16,'core'=2,'col'=16] {'col'}, dimensions={0} | all-to-all | bytes 524288 | tf_op jit(solution)/shard_map/all_to_all | solution.py:108
  (74 shorter events, 11.8 us)
Async XLA Ops:
  1.9 16.8 %collective-permute-start.3 = (bf16[1024,128]{1,0:T(8,128)(2,1)S(1)}, bf16[1024,128]{1,0:T(8,128)(2,1)S(1)}, u32[]{:S(2)}, u32[]{:S(2)}) collective-permute-start(bf16[1024,128]{1,0:T(8,128)(2,1)S(1)} %broadcast_multiply_fusion), channel_id=1, source_target_pairs={{0,32},{1,16},{16,33},{17,17},{2,34},{3,18},{18,35},{19,19},{4,36}... | collective-permute-start | bytes 786440 | tf_op jit(solution)/shard_map/ppermute | solution.py:72
  5.7 16.9 %collective-permute-start.8 = (bf16[1024,128]{1,0:T(8,128)(2,1)S(1)}, bf16[1024,128]{1,0:T(8,128)(2,1)S(1)}, u32[]{:S(2)}, u32[]{:S(2)}) collective-permute-start(bf16[1024,128]{1,0:T(8,128)(2,1)S(1)} %broadcast_multiply_fusion), channel_id=1, source_target_pairs={{1,32},{0,16},{17,33},{16,17},{3,34},{2,18},{19,35},{18,19},{5,36}... | collective-permute-start | bytes 786440 | tf_op jit(solution)/shard_map/ppermute | solution.py:72
  13.3 43.7 %collective-permute-start.1 = (bf16[512,1024]{1,0:T(8,128)(2,1)S(1)}, bf16[512,1024]{1,0:T(8,128)(2,1)S(1)}, u32[]{:S(2)}, u32[]{:S(2)}) collective-permute-start(bf16[512,1024]{1,0:T(8,128)(2,1)S(1)} %get-tuple-element.6), channel_id=1, source_target_pairs={{0,1},{1,0},{2,3},{3,2},{4,5},{5,4},{6,7},{7,6},{8,9},{9,8},{10,11... | collective-permute-start | bytes 3145736 | tf_op jit(solution)/shard_map/ppermute | solution.py:76
  18.7 8.3 %collective-permute-start.4 = (bf16[1024,128]{1,0:T(8,128)(2,1)S(1)}, bf16[1024,128]{1,0:T(8,128)(2,1)S(1)}, u32[]{:S(2)}, u32[]{:S(2)}) collective-permute-start(bf16[1024,128]{1,0:T(8,128)(2,1)S(1)} %collective-permute-done.3), channel_id=1, source_target_pairs={{0,32},{16,496},{1,33},{17,497},{2,34},{18,498},{3,35},{19,499},{4... | collective-permute-start | bytes 786440 | tf_op jit(solution)/shard_map/ppermute | solution.py:72
  22.6 26.7 %copy-start.2 = (bf16[1024,128]{1,0:T(8,128)(2,1)}, bf16[1024,128]{1,0:T(8,128)(2,1)S(1)}, u32[]{:S(2)}) copy-start(bf16[1024,128]{1,0:T(8,128)(2,1)S(1)} %collective-permute-done.8) | copy-start | bytes 786436
  22.6 8.3 %collective-permute-start.9 = (bf16[1024,128]{1,0:T(8,128)(2,1)S(1)}, bf16[1024,128]{1,0:T(8,128)(2,1)S(1)}, u32[]{:S(2)}, u32[]{:S(2)}) collective-permute-start(bf16[1024,128]{1,0:T(8,128)(2,1)S(1)} %collective-permute-done.8), channel_id=1, source_target_pairs={{0,32},{16,496},{1,33},{17,497},{2,34},{18,498},{3,35},{19,499},{4... | collective-permute-start | bytes 786440 | tf_op jit(solution)/shard_map/ppermute | solution.py:72
  27.0 27.9 %copy-start.9 = (bf16[1024,128]{1,0:T(8,128)(2,1)}, bf16[1024,128]{1,0:T(8,128)(2,1)S(1)}, u32[]{:S(2)}) copy-start(bf16[1024,128]{1,0:T(8,128)(2,1)S(1)} %collective-permute-done.4) | copy-start | bytes 786436
  27.0 8.9 %collective-permute-start.5 = (bf16[1024,128]{1,0:T(8,128)(2,1)S(1)}, bf16[1024,128]{1,0:T(8,128)(2,1)S(1)}, u32[]{:S(2)}, u32[]{:S(2)}) collective-permute-start(bf16[1024,128]{1,0:T(8,128)(2,1)S(1)} %collective-permute-done.4), channel_id=1, source_target_pairs={{0,32},{16,496},{1,33},{17,497},{2,34},{18,498},{3,35},{19,499},{4... | collective-permute-start | bytes 786440 | tf_op jit(solution)/shard_map/ppermute | solution.py:72
  30.9 24.1 %copy-start.3 = (bf16[1024,128]{1,0:T(8,128)(2,1)}, bf16[1024,128]{1,0:T(8,128)(2,1)S(1)}, u32[]{:S(2)}) copy-start(bf16[1024,128]{1,0:T(8,128)(2,1)S(1)} %collective-permute-done.9) | copy-start | bytes 786436
  30.9 8.9 %collective-permute-start.10 = (bf16[1024,128]{1,0:T(8,128)(2,1)S(1)}, bf16[1024,128]{1,0:T(8,128)(2,1)S(1)}, u32[]{:S(2)}, u32[]{:S(2)}) collective-permute-start(bf16[1024,128]{1,0:T(8,128)(2,1)S(1)} %collective-permute-done.9), channel_id=1, source_target_pairs={{0,32},{16,496},{1,33},{17,497},{2,34},{18,498},{3,35},{19,499},{4... | collective-permute-start | bytes 786440 | tf_op jit(solution)/shard_map/ppermute | solution.py:72
  35.9 19.1 %copy-start.5 = (bf16[1024,128]{1,0:T(8,128)(2,1)}, bf16[1024,128]{1,0:T(8,128)(2,1)S(1)}, u32[]{:S(2)}) copy-start(bf16[1024,128]{1,0:T(8,128)(2,1)S(1)} %collective-permute-done.5) | copy-start | bytes 786436
  35.9 9.5 %collective-permute-start.6 = (bf16[1024,128]{1,0:T(8,128)(2,1)S(1)}, bf16[1024,128]{1,0:T(8,128)(2,1)}, u32[]{:S(2)}, u32[]{:S(2)}) collective-permute-start(bf16[1024,128]{1,0:T(8,128)(2,1)S(1)} %collective-permute-done.5), channel_id=1, source_target_pairs={{0,32},{16,496},{1,33},{17,497},{2,34},{18,498},{3,35},{19,499},{4... | collective-permute-start | bytes 786440 | tf_op jit(solution)/shard_map/ppermute | solution.py:72
  39.8 15.2 %copy-start.7 = (bf16[1024,128]{1,0:T(8,128)(2,1)}, bf16[1024,128]{1,0:T(8,128)(2,1)S(1)}, u32[]{:S(2)}) copy-start(bf16[1024,128]{1,0:T(8,128)(2,1)S(1)} %collective-permute-done.10) | copy-start | bytes 786436
  39.8 9.5 %collective-permute-start.11 = (bf16[1024,128]{1,0:T(8,128)(2,1)S(1)}, bf16[1024,128]{1,0:T(8,128)(2,1)}, u32[]{:S(2)}, u32[]{:S(2)}) collective-permute-start(bf16[1024,128]{1,0:T(8,128)(2,1)S(1)} %collective-permute-done.10), channel_id=1, source_target_pairs={{0,32},{16,496},{1,33},{17,497},{2,34},{18,498},{3,35},{19,499},{4... | collective-permute-start | bytes 786440 | tf_op jit(solution)/shard_map/ppermute | solution.py:72
  45.4 14.1 %collective-permute-start.7 = (bf16[1024,128]{1,0:T(8,128)(2,1)}, bf16[1024,128]{1,0:T(8,128)(2,1)}, u32[]{:S(2)}, u32[]{:S(2)}) collective-permute-start(bf16[1024,128]{1,0:T(8,128)(2,1)} %collective-permute-done.6), channel_id=1, source_target_pairs={{0,32},{16,496},{1,33},{17,497},{2,34},{18,498},{3,35},{19,499},{4... | collective-permute-start | bytes 786440 | tf_op jit(solution)/shard_map/ppermute | solution.py:72
  49.2 14.1 %collective-permute-start.12 = (bf16[1024,128]{1,0:T(8,128)(2,1)}, bf16[1024,128]{1,0:T(8,128)(2,1)}, u32[]{:S(2)}, u32[]{:S(2)}) collective-permute-start(bf16[1024,128]{1,0:T(8,128)(2,1)} %collective-permute-done.11), channel_id=1, source_target_pairs={{0,32},{16,496},{1,33},{17,497},{2,34},{18,498},{3,35},{19,499},{4... | collective-permute-start | bytes 786440 | tf_op jit(solution)/shard_map/ppermute | solution.py:72
  55.0 31.9 %collective-permute-start = (bf16[512,1024]{1,0:T(8,128)(2,1)S(1)}, bf16[512,1024]{1,0:T(8,128)(2,1)S(1)}, u32[]{:S(2)}, u32[]{:S(2)}) collective-permute-start(bf16[512,1024]{1,0:T(8,128)(2,1)S(1)} %get-tuple-element.6), channel_id=1, source_target_pairs={{0,16},{1,17},{2,18},{3,19},{4,20},{5,21},{6,22},{7,23},{8,24},{9,... | collective-permute-start | bytes 3145736 | tf_op jit(solution)/shard_map/ppermute | solution.py:77
  56.9 19.4 %copy-start.4 = (bf16[1024,128]{1,0:T(8,128)(2,1)S(1)}, bf16[1024,128]{1,0:T(8,128)(2,1)}, u32[]{:S(2)}) copy-start(bf16[1024,128]{1,0:T(8,128)(2,1)} %copy-done.3) | copy-start | bytes 786436
  56.9 19.5 %copy-start.6 = (bf16[1024,128]{1,0:T(8,128)(2,1)S(1)}, bf16[1024,128]{1,0:T(8,128)(2,1)}, u32[]{:S(2)}) copy-start(bf16[1024,128]{1,0:T(8,128)(2,1)} %copy-done.5) | copy-start | bytes 786436
  56.9 19.6 %copy-start.8 = (bf16[1024,128]{1,0:T(8,128)(2,1)S(1)}, bf16[1024,128]{1,0:T(8,128)(2,1)}, u32[]{:S(2)}) copy-start(bf16[1024,128]{1,0:T(8,128)(2,1)} %copy-done.7) | copy-start | bytes 786436
  57.0 52.7 %collective-permute-start.2 = (bf16[512,1024]{1,0:T(8,128)(2,1)S(1)}, bf16[512,1024]{1,0:T(8,128)(2,1)S(1)}, u32[]{:S(2)}, u32[]{:S(2)}) collective-permute-start(bf16[512,1024]{1,0:T(8,128)(2,1)S(1)} %collective-permute-done.1), channel_id=1, source_target_pairs={{0,16},{1,17},{2,18},{3,19},{4,20},{5,21},{6,22},{7,23},{8,24},{9,... | collective-permute-start | bytes 3145736 | tf_op jit(solution)/shard_map/ppermute | solution.py:78
  59.5 8.5 %collective-permute-start.13 = (bf16[1024,128]{1,0:T(8,128)(2,1)}, bf16[1024,128]{1,0:T(8,128)(2,1)S(1)}, u32[]{:S(2)}, u32[]{:S(2)}) collective-permute-start(bf16[1024,128]{1,0:T(8,128)(2,1)} %collective-permute-done.7), channel_id=1, source_target_pairs={{0,32},{16,496},{1,33},{17,497},{2,34},{18,498},{3,35},{19,499},{4... | collective-permute-start | bytes 786440 | tf_op jit(solution)/shard_map/ppermute | solution.py:72
  63.4 8.5 %collective-permute-start.16 = (bf16[1024,128]{1,0:T(8,128)(2,1)}, bf16[1024,128]{1,0:T(8,128)(2,1)S(1)}, u32[]{:S(2)}, u32[]{:S(2)}) collective-permute-start(bf16[1024,128]{1,0:T(8,128)(2,1)} %collective-permute-done.12), channel_id=1, source_target_pairs={{0,32},{16,496},{1,33},{17,497},{2,34},{18,498},{3,35},{19,499},{4... | collective-permute-start | bytes 786440 | tf_op jit(solution)/shard_map/ppermute | solution.py:72
  68.0 8.6 %collective-permute-start.14 = (bf16[1024,128]{1,0:T(8,128)(2,1)S(1)}, bf16[1024,128]{1,0:T(8,128)(2,1)S(1)}, u32[]{:S(2)}, u32[]{:S(2)}) collective-permute-start(bf16[1024,128]{1,0:T(8,128)(2,1)S(1)} %collective-permute-done.13), channel_id=1, source_target_pairs={{0,32},{16,496},{1,33},{17,497},{2,34},{18,498},{3,35},{19,499},{4... | collective-permute-start | bytes 786440 | tf_op jit(solution)/shard_map/ppermute | solution.py:72
  71.8 8.4 %collective-permute-start.17 = (bf16[1024,128]{1,0:T(8,128)(2,1)S(1)}, bf16[1024,128]{1,0:T(8,128)(2,1)S(1)}, u32[]{:S(2)}, u32[]{:S(2)}) collective-permute-start(bf16[1024,128]{1,0:T(8,128)(2,1)S(1)} %collective-permute-done.16), channel_id=1, source_target_pairs={{0,32},{16,496},{1,33},{17,497},{2,34},{18,498},{3,35},{19,499},{4... | collective-permute-start | bytes 786440 | tf_op jit(solution)/shard_map/ppermute | solution.py:72
  76.6 42.8 %collective-permute-start.15 = (bf16[1024,128]{1,0:T(8,128)(2,1)S(1)}, bf16[1024,128]{1,0:T(8,128)(2,1)S(1)}, u32[]{:S(2)}, u32[]{:S(2)}) collective-permute-start(bf16[1024,128]{1,0:T(8,128)(2,1)S(1)} %collective-permute-done.14), channel_id=1, source_target_pairs={{0,32},{16,496},{1,33},{17,497},{2,34},{18,498},{3,35},{19,499},{4... | collective-permute-start | bytes 786440 | tf_op jit(solution)/shard_map/ppermute | solution.py:72
  80.2 39.2 %collective-permute-start.18 = (bf16[1024,128]{1,0:T(8,128)(2,1)S(1)}, bf16[1024,128]{1,0:T(8,128)(2,1)S(1)}, u32[]{:S(2)}, u32[]{:S(2)}) collective-permute-start(bf16[1024,128]{1,0:T(8,128)(2,1)S(1)} %collective-permute-done.17), channel_id=1, source_target_pairs={{0,32},{16,496},{1,33},{17,497},{2,34},{18,498},{3,35},{19,499},{4... | collective-permute-start | bytes 786440 | tf_op jit(solution)/shard_map/ppermute | solution.py:72
  108.5 10.9 %copy-start.10 = (bf16[1024,640]{1,0:T(8,128)(2,1)}, bf16[1024,640]{1,0:T(8,128)(2,1)S(1)}, u32[]{:S(2)}) copy-start(bf16[1024,640]{1,0:T(8,128)(2,1)S(1)} %constant_dynamic-update-slice_fusion.6) | copy-start | bytes 3932164
  119.4 14.0 %copy-start.13 = (bf16[1024,640]{1,0:T(8,128)(2,1)S(1)}, bf16[1024,640]{1,0:T(8,128)(2,1)}, u32[]{:S(2)}) copy-start(bf16[1024,640]{1,0:T(8,128)(2,1)} %copy-done.12) | copy-start | bytes 3932164
  124.9 22.1 %all-to-all-start.1 = ((bf16[32,32,384]{2,1,0:T(8,128)(2,1)}), bf16[32,32,384]{2,1,0:T(8,128)(2,1)S(1)}, u32[]{:S(2)}, u32[]{:S(2)}) async-start(bf16[32,32,384]{2,1,0:T(8,128)(2,1)} %bitcast.4), calls=%async_computation.1 | async-start | bytes 1572864 | tf_op jit(solution)/shard_map/all_to_all | solution.py:94
  140.1 10.9 %copy-start.14 = (s32[32]{0:T(128)S(1)}, s32[32]{0:T(128)}, u32[]{:S(2)}) copy-start(s32[32]{0:T(128)} %param.9) | copy-start | bytes 388
  147.1 24.5 %all-to-all-start = ((bf16[32,32,640]{2,1,0:T(8,128)(2,1)}), bf16[32,32,640]{2,1,0:T(8,128)(2,1)S(1)}, u32[]{:S(2)}, u32[]{:S(2)}) async-start(bf16[32,32,640]{2,1,0:T(8,128)(2,1)} %bitcast.2), calls=%async_computation | async-start | bytes 2621440 | tf_op jit(solution)/shard_map/all_to_all | solution.py:94
  (4 other events, 20.4 us)

commit v2 on v1

--- a/solution.py
+++ b/solution.py
@@ -1,6 +1,8 @@
 import jax
 import jax.numpy as jnp
 from jax import lax
+from jax.experimental import pallas as pl
+from jax.experimental.pallas import tpu as pltpu
 from jax.sharding import Mesh, PartitionSpec as P
 
 
@@ -50,6 +52,44 @@
     return (nslot - last, last)
 
 
+def multiply(choice, blocks, tiles):
+    nrow, kloc = blocks[0].shape
+    count = len(tiles[0])
+    width = count * TILE
+    step = nrow // 2
+
+    def body(choice_ref, own, beside, own_other, beside_other, *rest):
+        tile_refs, out, right = rest[: 2 * count], rest[2 * count], rest[2 * count + 1]
+
+        @pl.when(pl.program_id(0) == 0)
+        def _():
+            for i in range(2 * count):
+                right[i // count, :, (i % count) * TILE : (i % count + 1) * TILE] = tile_refs[i][...]
+
+        near = jnp.concatenate([own[...], own_other[...]], 0)
+        far = jnp.concatenate([beside[...], beside_other[...]], 0)
+        stream, core = choice_ref[0], choice_ref[1]
+        for start in range(0, width, 2 * TILE):
+            cols = slice(start, min(start + 2 * TILE, width))
+            total = jnp.dot(near, right[stream, :, cols], preferred_element_type=jnp.float32)
+            total += jnp.dot(far, right[1 - stream, :, cols], preferred_element_type=jnp.float32)
+            total = total.astype(jnp.bfloat16)
+            out[core, :, cols] = total[:step]
+            out[1 - core, :, cols] = total[step:]
+
+    left = pl.BlockSpec((step, kloc), lambda m: (m, 0))
+    whole = pl.BlockSpec((kloc, TILE), lambda m: (0, 0))
+    return pl.pallas_call(
+        body,
+        grid=(nrow // step,),
+        in_specs=[pl.BlockSpec(memory_space=pltpu.SMEM)] + [left] * 4 + [whole] * (2 * count),
+        out_specs=pl.BlockSpec((2, step, width), lambda m: (0, m, 0)),
+        out_shape=jax.ShapeDtypeStruct((2, nrow, width), jnp.bfloat16),
+        scratch_shapes=[pltpu.VMEM((2, kloc, width), jnp.bfloat16)],
+        name="multiply",
+    )(choice, *blocks, *tiles[0], *tiles[1])
+
+
 def make(nz, ncol):
     every = ("z", "core", "col")
     nslot = nz // 2
@@ -61,7 +101,7 @@
         core = lax.axis_index("core")
         odd = lax.axis_index("col") % 2
         own_tile = mask_tiles(integrals, int_occupancy)
-        nrow, kloc = amplitudes.shape
+        nrow, _ = amplitudes.shape
         part = nrow // ncol
         current = [own_tile, own_tile]
         sums = []
@@ -76,20 +116,12 @@
                 beside = lax.ppermute(own, every, swap_pairs(nz, ncol, 0, 1))
                 own_other = lax.ppermute(own, every, swap_pairs(nz, ncol, 1, 0))
                 beside_other = lax.ppermute(beside, every, swap_pairs(nz, ncol, 1, 0))
-                first = (odd ^ core) * kloc
-                second = kloc - first
-                mine = core * nrow
-                theirs = nrow - mine
-                amp = jnp.zeros((2 * nrow, 2 * kloc), jnp.bfloat16)
-                amp = lax.dynamic_update_slice(amp, own, (mine, first))
-                amp = lax.dynamic_update_slice(amp, own_other, (theirs, first))
-                amp = lax.dynamic_update_slice(amp, beside, (mine, second))
-                amp = lax.dynamic_update_slice(amp, beside_other, (theirs, second))
+                blocks = (own, beside, own_other, beside_other)
+                choice = jnp.stack([odd ^ core, core]).astype(jnp.int32)
             if slot in ends:
-                right = jnp.concatenate([jnp.concatenate(t, 1) for t in tiles], 0)
-                product = jnp.dot(amp, right, preferred_element_type=jnp.float32).astype(jnp.bfloat16)
+                product = multiply(choice, blocks, tiles)
                 tiles = [[], []]
-                width = product.shape[1]
+                width = product.shape[-1]
                 product = product.reshape(2 * ncol, part, width)
                 moved = lax.all_to_all(product, ("core", "col"), 0, 0, tiled=True)
                 moved = moved.reshape(2, ncol // 2, 2, part, width)

time: 187 us -> 158 us (0.84)
  the two profiles are of different devices: /device:TPU:64 before, /device:TPU:1 now
where the time goes in v2:
time: 158 us; the launch traced here: 157 us
  starting transfers between devices  93.1 us (59%)
  waiting for transfers between devices  33.8 us (21%)
  Pallas kernels  13.3 us (8%)
  blocking collectives  10.9 us (7%)
  other arithmetic  3.75 us (2%)
  local copies, waits for them, and re-layouts  1.8 us (1%)
    ppermute x16, starting transfers between devices, on_device(): current[stream] = lax.ppermute(current[stream], every, pairs)  69.7 us
    all_to_all x2, waiting for transfers between devices, on_device(): moved = lax.all_to_all(product, ('core', 'col'), 0, 0, tiled=True)  25.3 us
    all_to_all x2, starting transfers between devices, on_device(): moved = lax.all_to_all(product, ('core', 'col'), 0, 0, tiled=True)  17.7 us
    pallas_call x2, Pallas kernels, multiply(): pl.pallas_call(body, grid=(nrow // step,), in_specs=[pl.BlockSpec(memory_...  13.3 us
    all_to_all x1, blocking collectives, on_device(): final = lax.all_to_all(picked, 'col', 0, 0, tiled=True)  10.9 us
    ppermute x16, waiting for transfers between devices, on_device(): current[stream] = lax.ppermute(current[stream], every, pairs)  8.49 us
  transfers between devices with their start and end apart: 21, of which 9 were waited for; matrix products, arithmetic and copies ran while one was open for 1% of the time, Pallas kernels for 5%

profile of v2, /device:TPU:1, one launch (start us, length us, event | category | flops | bytes accessed | tf_op | source)
XLA Modules:
  0.0 157.2 jit_solution(13149349966457376214)
XLA Ops:
  0.0 0.7 convert_bitcast_fusion
  0.8 1.1 broadcast_multiply_fusion
  2.0 3.9 %collective-permute-start.8 = (bf16[1024,128]{1,0:T(8,128)(2,1)S(1)}, bf16[1024,128]{1,0:T(8,128)(2,1)S(1)}, u32[]{:S(2)}, u32[]{:S(2)}) collective-permute-start(bf16[1024,128]{1,0:T(8,128)(2,1)S(1)} %broadcast_multiply_fusion), channel_id=1, source_target_pairs={{1,32},{0,16},{17,33},{16,17},{3,34},{2,18},{19,35},{18,19},{5,36}... | collective-permute-start | bytes 786440 | tf_op jit(solution)/shard_map/ppermute | solution.py:112
  5.9 5.7 %collective-permute-start.3 = (bf16[1024,128]{1,0:T(8,128)(2,1)S(1)}, bf16[1024,128]{1,0:T(8,128)(2,1)S(1)}, u32[]{:S(2)}, u32[]{:S(2)}) collective-permute-start(bf16[1024,128]{1,0:T(8,128)(2,1)S(1)} %broadcast_multiply_fusion), channel_id=1, source_target_pairs={{0,32},{1,16},{16,33},{17,17},{2,34},{3,18},{18,35},{19,19},{4,36}... | collective-permute-start | bytes 786440 | tf_op jit(solution)/shard_map/ppermute | solution.py:112
  12.7 1.9 %collective-permute-start = (bf16[512,1024]{1,0:T(8,128)(2,1)S(1)}, bf16[512,1024]{1,0:T(8,128)(2,1)S(1)}, u32[]{:S(2)}, u32[]{:S(2)}) collective-permute-start(bf16[512,1024]{1,0:T(8,128)(2,1)S(1)} %bitcast_multiply_fusion.own), channel_id=1, source_target_pairs={{0,1},{1,0},{2,3},{3,2},{4,5},{5,4},{6,7},{7,6},{8,9},{9,8},{10,11... | collective-permute-start | bytes 3145736 | tf_op jit(solution)/shard_map/ppermute | solution.py:116
  14.6 1.9 %collective-permute-done.3.rest_0_ = bf16[1024,128]{1,0:T(8,128)(2,1)S(1)} collective-permute-done((bf16[1024,128]{1,0:T(8,128)(2,1)S(1)}, bf16[1024,128]{1,0:T(8,128)(2,1)S(1)}, u32[]{:S(2)}, u32[]{:S(2)}) %collective-permute-start.3) | collective-permute-done | bytes 262176 | tf_op jit(solution)/shard_map/ppermute | solution.py:112
  16.5 11.8 %collective-permute-start.4 = (bf16[1024,128]{1,0:T(8,128)(2,1)S(1)}, bf16[1024,128]{1,0:T(8,128)(2,1)S(1)}, u32[]{:S(2)}, u32[]{:S(2)}) collective-permute-start(bf16[1024,128]{1,0:T(8,128)(2,1)S(1)} %collective-permute-done.3.rest_0_), channel_id=1, source_target_pairs={{0,32},{16,496},{1,33},{17,497},{2,34},{18,498},{3,35},{19,499},{4... | collective-permute-start | bytes 786440 | tf_op jit(solution)/shard_map/ppermute | solution.py:112
  28.3 2.3 %collective-permute-start.9 = (bf16[1024,128]{1,0:T(8,128)(2,1)S(1)}, bf16[1024,128]{1,0:T(8,128)(2,1)S(1)}, u32[]{:S(2)}, u32[]{:S(2)}) collective-permute-start(bf16[1024,128]{1,0:T(8,128)(2,1)S(1)} %collective-permute-done.8.rest_5_), channel_id=1, source_target_pairs={{0,32},{16,496},{1,33},{17,497},{2,34},{18,498},{3,35},{19,499},{4... | collective-permute-start | bytes 786440 | tf_op jit(solution)/shard_map/ppermute | solution.py:112
  30.7 0.9 collective-permute-done.4.rest_1_
  31.6 5.0 %collective-permute-start.5 = (bf16[1024,128]{1,0:T(8,128)(2,1)S(1)}, bf16[1024,128]{1,0:T(8,128)(2,1)S(1)}, u32[]{:S(2)}, u32[]{:S(2)}) collective-permute-start(bf16[1024,128]{1,0:T(8,128)(2,1)S(1)} %collective-permute-done.4.rest_1_), channel_id=1, source_target_pairs={{0,32},{16,496},{1,33},{17,497},{2,34},{18,498},{3,35},{19,499},{4... | collective-permute-start | bytes 786440 | tf_op jit(solution)/shard_map/ppermute | solution.py:112
  36.6 2.8 %collective-permute-start.10 = (bf16[1024,128]{1,0:T(8,128)(2,1)S(1)}, bf16[1024,128]{1,0:T(8,128)(2,1)S(1)}, u32[]{:S(2)}, u32[]{:S(2)}) collective-permute-start(bf16[1024,128]{1,0:T(8,128)(2,1)S(1)} %collective-permute-done.9.rest_6_), channel_id=1, source_target_pairs={{0,32},{16,496},{1,33},{17,497},{2,34},{18,498},{3,35},{19,499},{4... | collective-permute-start | bytes 786440 | tf_op jit(solution)/shard_map/ppermute | solution.py:112
  39.9 5.0 %collective-permute-start.6 = (bf16[1024,128]{1,0:T(8,128)(2,1)S(1)}, bf16[1024,128]{1,0:T(8,128)(2,1)S(1)}, u32[]{:S(2)}, u32[]{:S(2)}) collective-permute-start(bf16[1024,128]{1,0:T(8,128)(2,1)S(1)} %collective-permute-done.5.rest_2_), channel_id=1, source_target_pairs={{0,32},{16,496},{1,33},{17,497},{2,34},{18,498},{3,35},{19,499},{4... | collective-permute-start | bytes 786440 | tf_op jit(solution)/shard_map/ppermute | solution.py:112
  45.0 2.8 %collective-permute-start.11 = (bf16[1024,128]{1,0:T(8,128)(2,1)S(1)}, bf16[1024,128]{1,0:T(8,128)(2,1)S(1)}, u32[]{:S(2)}, u32[]{:S(2)}) collective-permute-start(bf16[1024,128]{1,0:T(8,128)(2,1)S(1)} %collective-permute-done.10.rest_7_), channel_id=1, source_target_pairs={{0,32},{16,496},{1,33},{17,497},{2,34},{18,498},{3,35},{19,499},{4... | collective-permute-start | bytes 786440 | tf_op jit(solution)/shard_map/ppermute | solution.py:112
  47.8 1.9 %collective-permute-start.1 = (bf16[512,1024]{1,0:T(8,128)(2,1)S(1)}, bf16[512,1024]{1,0:T(8,128)(2,1)S(1)}, u32[]{:S(2)}, u32[]{:S(2)}) collective-permute-start(bf16[512,1024]{1,0:T(8,128)(2,1)S(1)} %bitcast_multiply_fusion.own), channel_id=1, source_target_pairs={{0,16},{1,17},{2,18},{3,19},{4,20},{5,21},{6,22},{7,23},{8,24},{9,... | collective-permute-start | bytes 3145736 | tf_op jit(solution)/shard_map/ppermute | solution.py:117
  49.7 4.4 %collective-permute-start.7 = (bf16[1024,128]{1,0:T(8,128)(2,1)S(1)}, bf16[1024,128]{1,0:T(8,128)(2,1)S(1)}, u32[]{:S(2)}, u32[]{:S(2)}) collective-permute-start(bf16[1024,128]{1,0:T(8,128)(2,1)S(1)} %collective-permute-done.6.rest_3_), channel_id=1, source_target_pairs={{0,32},{16,496},{1,33},{17,497},{2,34},{18,498},{3,35},{19,499},{4... | collective-permute-start | bytes 786440 | tf_op jit(solution)/shard_map/ppermute | solution.py:112
  54.1 2.8 %collective-permute-start.12 = (bf16[1024,128]{1,0:T(8,128)(2,1)S(1)}, bf16[1024,128]{1,0:T(8,128)(2,1)S(1)}, u32[]{:S(2)}, u32[]{:S(2)}) collective-permute-start(bf16[1024,128]{1,0:T(8,128)(2,1)S(1)} %collective-permute-done.11.rest_8_), channel_id=1, source_target_pairs={{0,32},{16,496},{1,33},{17,497},{2,34},{18,498},{3,35},{19,499},{4... | collective-permute-start | bytes 786440 | tf_op jit(solution)/shard_map/ppermute | solution.py:112
  56.9 1.9 %collective-permute-start.2 = (bf16[512,1024]{1,0:T(8,128)(2,1)S(1)}, bf16[512,1024]{1,0:T(8,128)(2,1)}, u32[]{:S(2)}, u32[]{:S(2)}) collective-permute-start(bf16[512,1024]{1,0:T(8,128)(2,1)S(1)} %collective-permute-done.beside), channel_id=1, source_target_pairs={{0,16},{1,17},{2,18},{3,19},{4,20},{5,21},{6,22},{7,23},{8,24},{9,... | collective-permute-start | bytes 3145736 | tf_op jit(solution)/shard_map/ppermute | solution.py:118
  58.9 4.7 %collective-permute-start.13 = (bf16[1024,128]{1,0:T(8,128)(2,1)S(1)}, bf16[1024,128]{1,0:T(8,128)(2,1)S(1)}, u32[]{:S(2)}, u32[]{:S(2)}) collective-permute-start(bf16[1024,128]{1,0:T(8,128)(2,1)S(1)} %collective-permute-done.7.rest_4_), channel_id=1, source_target_pairs={{0,32},{16,496},{1,33},{17,497},{2,34},{18,498},{3,35},{19,499},{4... | collective-permute-start | bytes 786440 | tf_op jit(solution)/shard_map/ppermute | solution.py:112
  63.6 2.8 %collective-permute-start.16 = (bf16[1024,128]{1,0:T(8,128)(2,1)S(1)}, bf16[1024,128]{1,0:T(8,128)(2,1)S(1)}, u32[]{:S(2)}, u32[]{:S(2)}) collective-permute-start(bf16[1024,128]{1,0:T(8,128)(2,1)S(1)} %collective-permute-done.12.rest_9_), channel_id=1, source_target_pairs={{0,32},{16,496},{1,33},{17,497},{2,34},{18,498},{3,35},{19,499},{4... | collective-permute-start | bytes 786440 | tf_op jit(solution)/shard_map/ppermute | solution.py:112
  66.9 5.0 %collective-permute-start.14 = (bf16[1024,128]{1,0:T(8,128)(2,1)S(1)}, bf16[1024,128]{1,0:T(8,128)(2,1)}, u32[]{:S(2)}, u32[]{:S(2)}) collective-permute-start(bf16[1024,128]{1,0:T(8,128)(2,1)S(1)} %collective-permute-done.13.rest_0_), channel_id=1, source_target_pairs={{0,32},{16,496},{1,33},{17,497},{2,34},{18,498},{3,35},{19,499},{4... | collective-permute-start | bytes 786440 | tf_op jit(solution)/shard_map/ppermute | solution.py:112
  72.0 2.8 %collective-permute-start.17 = (bf16[1024,128]{1,0:T(8,128)(2,1)S(1)}, bf16[1024,128]{1,0:T(8,128)(2,1)}, u32[]{:S(2)}, u32[]{:S(2)}) collective-permute-start(bf16[1024,128]{1,0:T(8,128)(2,1)S(1)} %collective-permute-done.16.rest_3_), channel_id=1, source_target_pairs={{0,32},{16,496},{1,33},{17,497},{2,34},{18,498},{3,35},{19,499},{4... | collective-permute-start | bytes 786440 | tf_op jit(solution)/shard_map/ppermute | solution.py:112
  75.2 5.1 %collective-permute-start.15 = (bf16[1024,128]{1,0:T(8,128)(2,1)}, bf16[1024,128]{1,0:T(8,128)(2,1)}, u32[]{:S(2)}, u32[]{:S(2)}) collective-permute-start(bf16[1024,128]{1,0:T(8,128)(2,1)} %collective-permute-done.14.rest_1_), channel_id=1, source_target_pairs={{0,32},{16,496},{1,33},{17,497},{2,34},{18,498},{3,35},{19,499},{4... | collective-permute-start | bytes 786440 | tf_op jit(solution)/shard_map/ppermute | solution.py:112
  80.3 2.8 %collective-permute-start.18 = (bf16[1024,128]{1,0:T(8,128)(2,1)}, bf16[1024,128]{1,0:T(8,128)(2,1)}, u32[]{:S(2)}, u32[]{:S(2)}) collective-permute-start(bf16[1024,128]{1,0:T(8,128)(2,1)} %collective-permute-done.17.rest_4_), channel_id=1, source_target_pairs={{0,32},{16,496},{1,33},{17,497},{2,34},{18,498},{3,35},{19,499},{4... | collective-permute-start | bytes 786440 | tf_op jit(solution)/shard_map/ppermute | solution.py:112
  83.9 4.1 %collective-permute-done.18.rest_5_ = bf16[1024,128]{1,0:T(8,128)(2,1)} collective-permute-done((bf16[1024,128]{1,0:T(8,128)(2,1)}, bf16[1024,128]{1,0:T(8,128)(2,1)}, u32[]{:S(2)}, u32[]{:S(2)}) %collective-permute-start.18) | collective-permute-done | bytes 262176 | tf_op jit(solution)/shard_map/ppermute | solution.py:112
  88.1 5.8 %multiply.3 = bf16[2,512,384]{2,1,0:T(8,128)(2,1)} custom-call(s32[2]{0:T(128)} %pad_add_fusion.choice_ref, bf16[512,1024]{1,0:T(8,128)(2,1)} %copy-done, bf16[512,1024]{1,0:T(8,128)(2,1)} %copy-done.1, bf16[512,1024]{1,0:T(8,128)(2,1)} %copy-done.2, bf16[512,1024]{1,0:T(8,128)(2,1)} %collective-permute-done.2.beside_other, bf16[1024,128]{1,0:T(8,128)(2,1)} %copy-done.14, ...), custom_call_target="tpu_custom_call" | custom-call | tf_op jit(solution)/shard_map/multiply/pallas_call | solution.py:82
  93.9 12.6 %all-to-all-start.1 = ((bf16[32,32,384]{2,1,0:T(8,128)(2,1)}), bf16[32,32,384]{2,1,0:T(8,128)(2,1)S(1)}, u32[]{:S(2)}, u32[]{:S(2)}) async-start(bf16[32,32,384]{2,1,0:T(8,128)(2,1)} %bitcast.36), calls=%async_computation.1 | async-start | bytes 1572864 | tf_op jit(solution)/shard_map/all_to_all | solution.py:126
  106.5 7.5 %multiply.2 = bf16[2,512,640]{2,1,0:T(8,128)(2,1)} custom-call(s32[2]{0:T(128)} %pad_add_fusion.choice_ref, bf16[512,1024]{1,0:T(8,128)(2,1)} %copy-done, bf16[512,1024]{1,0:T(8,128)(2,1)} %copy-done.1, bf16[512,1024]{1,0:T(8,128)(2,1)} %copy-done.2, bf16[512,1024]{1,0:T(8,128)(2,1)} %collective-permute-done.2.beside_other, bf16[1024,128]{1,0:T(8,128)(2,1)} %copy-done.5, ...), custom_call_target="tpu_custom_call" | custom-call | tf_op jit(solution)/shard_map/multiply/pallas_call | solution.py:82
  114.0 6.1 %all-to-all-done.1 = bf16[32,32,384]{2,1,0:T(8,128)(2,1)S(1)} async-done(((bf16[32,32,384]{2,1,0:T(8,128)(2,1)}), bf16[32,32,384]{2,1,0:T(8,128)(2,1)S(1)}, u32[]{:S(2)}, u32[]{:S(2)}) %all-to-all-start.1) | async-done | bytes 786464 | tf_op jit(solution)/shard_map/all_to_all | solution.py:126
  120.2 5.1 %all-to-all-start = ((bf16[32,32,640]{2,1,0:T(8,128)(2,1)}), bf16[32,32,640]{2,1,0:T(8,128)(2,1)S(1)}, u32[]{:S(2)}, u32[]{:S(2)}) async-start(bf16[32,32,640]{2,1,0:T(8,128)(2,1)} %bitcast.32), calls=%async_computation | async-start | bytes 2621440 | tf_op jit(solution)/shard_map/all_to_all | solution.py:126
  125.5 19.1 %all-to-all-done = bf16[32,32,640]{2,1,0:T(8,128)(2,1)S(1)} async-done(((bf16[32,32,640]{2,1,0:T(8,128)(2,1)}), bf16[32,32,640]{2,1,0:T(8,128)(2,1)S(1)}, u32[]{:S(2)}, u32[]{:S(2)}) %all-to-all-start) | async-done | bytes 1310752 | tf_op jit(solution)/shard_map/all_to_all | solution.py:126
  145.6 10.9 %all_to_all.15 = bf16[16,32,256]{2,1,0:T(8,128)(2,1)S(1)} all-to-all(bf16[16,32,256]{2,1,0:T(8,128)(2,1)S(1)} %bitcast.41), channel_id=1, replica_groups=mesh['z'=16,'core'=2,'col'=16] {'col'}, dimensions={0} | all-to-all | bytes 524288 | tf_op jit(solution)/shard_map/all_to_all | solution.py:140
  156.5 0.7 copy.15
  (65 shorter events, 4.5 us)
Async XLA Ops:
  2.0 26.3 %collective-permute-start.8 = (bf16[1024,128]{1,0:T(8,128)(2,1)S(1)}, bf16[1024,128]{1,0:T(8,128)(2,1)S(1)}, u32[]{:S(2)}, u32[]{:S(2)}) collective-permute-start(bf16[1024,128]{1,0:T(8,128)(2,1)S(1)} %broadcast_multiply_fusion), channel_id=1, source_target_pairs={{1,32},{0,16},{17,33},{16,17},{3,34},{2,18},{19,35},{18,19},{5,36}... | collective-permute-start | bytes 786440 | tf_op jit(solution)/shard_map/ppermute | solution.py:112
  5.9 10.6 %collective-permute-start.3 = (bf16[1024,128]{1,0:T(8,128)(2,1)S(1)}, bf16[1024,128]{1,0:T(8,128)(2,1)S(1)}, u32[]{:S(2)}, u32[]{:S(2)}) collective-permute-start(bf16[1024,128]{1,0:T(8,128)(2,1)S(1)} %broadcast_multiply_fusion), channel_id=1, source_target_pairs={{0,32},{1,16},{16,33},{17,17},{2,34},{3,18},{18,35},{19,19},{4,36}... | collective-permute-start | bytes 786440 | tf_op jit(solution)/shard_map/ppermute | solution.py:112
  12.7 75.4 %copy-start = (bf16[512,1024]{1,0:T(8,128)(2,1)}, bf16[512,1024]{1,0:T(8,128)(2,1)S(1)}, u32[]{:S(2)}) copy-start(bf16[512,1024]{1,0:T(8,128)(2,1)S(1)} %bitcast_multiply_fusion.own) | copy-start | bytes 3145732
  12.7 44.2 %collective-permute-start = (bf16[512,1024]{1,0:T(8,128)(2,1)S(1)}, bf16[512,1024]{1,0:T(8,128)(2,1)S(1)}, u32[]{:S(2)}, u32[]{:S(2)}) collective-permute-start(bf16[512,1024]{1,0:T(8,128)(2,1)S(1)} %bitcast_multiply_fusion.own), channel_id=1, source_target_pairs={{0,1},{1,0},{2,3},{3,2},{4,5},{5,4},{6,7},{7,6},{8,9},{9,8},{10,11... | collective-permute-start | bytes 3145736 | tf_op jit(solution)/shard_map/ppermute | solution.py:116
  16.5 40.4 %copy-start.5 = (bf16[1024,128]{1,0:T(8,128)(2,1)}, bf16[1024,128]{1,0:T(8,128)(2,1)S(1)}, u32[]{:S(2)}) copy-start(bf16[1024,128]{1,0:T(8,128)(2,1)S(1)} %collective-permute-done.3.rest_0_) | copy-start | bytes 786436
  16.5 15.1 %collective-permute-start.4 = (bf16[1024,128]{1,0:T(8,128)(2,1)S(1)}, bf16[1024,128]{1,0:T(8,128)(2,1)S(1)}, u32[]{:S(2)}, u32[]{:S(2)}) collective-permute-start(bf16[1024,128]{1,0:T(8,128)(2,1)S(1)} %collective-permute-done.3.rest_0_), channel_id=1, source_target_pairs={{0,32},{16,496},{1,33},{17,497},{2,34},{18,498},{3,35},{19,499},{4... | collective-permute-start | bytes 786440 | tf_op jit(solution)/shard_map/ppermute | solution.py:112
  28.3 65.6 %copy-start.4 = (bf16[1024,128]{1,0:T(8,128)(2,1)}, bf16[1024,128]{1,0:T(8,128)(2,1)S(1)}, u32[]{:S(2)}) copy-start(bf16[1024,128]{1,0:T(8,128)(2,1)S(1)} %collective-permute-done.8.rest_5_) | copy-start | bytes 786436
  28.3 8.3 %collective-permute-start.9 = (bf16[1024,128]{1,0:T(8,128)(2,1)S(1)}, bf16[1024,128]{1,0:T(8,128)(2,1)S(1)}, u32[]{:S(2)}, u32[]{:S(2)}) collective-permute-start(bf16[1024,128]{1,0:T(8,128)(2,1)S(1)} %collective-permute-done.8.rest_5_), channel_id=1, source_target_pairs={{0,32},{16,496},{1,33},{17,497},{2,34},{18,498},{3,35},{19,499},{4... | collective-permute-start | bytes 786440 | tf_op jit(solution)/shard_map/ppermute | solution.py:112
  31.6 27.2 %copy-start.6 = (bf16[1024,128]{1,0:T(8,128)(2,1)}, bf16[1024,128]{1,0:T(8,128)(2,1)S(1)}, u32[]{:S(2)}) copy-start(bf16[1024,128]{1,0:T(8,128)(2,1)S(1)} %collective-permute-done.4.rest_1_) | copy-start | bytes 786436
  31.6 8.3 %collective-permute-start.5 = (bf16[1024,128]{1,0:T(8,128)(2,1)S(1)}, bf16[1024,128]{1,0:T(8,128)(2,1)S(1)}, u32[]{:S(2)}, u32[]{:S(2)}) collective-permute-start(bf16[1024,128]{1,0:T(8,128)(2,1)S(1)} %collective-permute-done.4.rest_1_), channel_id=1, source_target_pairs={{0,32},{16,496},{1,33},{17,497},{2,34},{18,498},{3,35},{19,499},{4... | collective-permute-start | bytes 786440 | tf_op jit(solution)/shard_map/ppermute | solution.py:112
  36.6 22.2 %copy-start.7 = (bf16[1024,128]{1,0:T(8,128)(2,1)}, bf16[1024,128]{1,0:T(8,128)(2,1)S(1)}, u32[]{:S(2)}) copy-start(bf16[1024,128]{1,0:T(8,128)(2,1)S(1)} %collective-permute-done.9.rest_6_) | copy-start | bytes 786436
  36.6 8.3 %collective-permute-start.10 = (bf16[1024,128]{1,0:T(8,128)(2,1)S(1)}, bf16[1024,128]{1,0:T(8,128)(2,1)S(1)}, u32[]{:S(2)}, u32[]{:S(2)}) collective-permute-start(bf16[1024,128]{1,0:T(8,128)(2,1)S(1)} %collective-permute-done.9.rest_6_), channel_id=1, source_target_pairs={{0,32},{16,496},{1,33},{17,497},{2,34},{18,498},{3,35},{19,499},{4... | collective-permute-start | bytes 786440 | tf_op jit(solution)/shard_map/ppermute | solution.py:112
  39.9 23.7 %copy-start.8 = (bf16[1024,128]{1,0:T(8,128)(2,1)}, bf16[1024,128]{1,0:T(8,128)(2,1)S(1)}, u32[]{:S(2)}) copy-start(bf16[1024,128]{1,0:T(8,128)(2,1)S(1)} %collective-permute-done.5.rest_2_) | copy-start | bytes 786436
  39.9 9.8 %collective-permute-start.6 = (bf16[1024,128]{1,0:T(8,128)(2,1)S(1)}, bf16[1024,128]{1,0:T(8,128)(2,1)S(1)}, u32[]{:S(2)}, u32[]{:S(2)}) collective-permute-start(bf16[1024,128]{1,0:T(8,128)(2,1)S(1)} %collective-permute-done.5.rest_2_), channel_id=1, source_target_pairs={{0,32},{16,496},{1,33},{17,497},{2,34},{18,498},{3,35},{19,499},{4... | collective-permute-start | bytes 786440 | tf_op jit(solution)/shard_map/ppermute | solution.py:112
  45.0 18.7 %copy-start.9 = (bf16[1024,128]{1,0:T(8,128)(2,1)}, bf16[1024,128]{1,0:T(8,128)(2,1)S(1)}, u32[]{:S(2)}) copy-start(bf16[1024,128]{1,0:T(8,128)(2,1)S(1)} %collective-permute-done.10.rest_7_) | copy-start | bytes 786436
  45.0 9.1 %collective-permute-start.11 = (bf16[1024,128]{1,0:T(8,128)(2,1)S(1)}, bf16[1024,128]{1,0:T(8,128)(2,1)S(1)}, u32[]{:S(2)}, u32[]{:S(2)}) collective-permute-start(bf16[1024,128]{1,0:T(8,128)(2,1)S(1)} %collective-permute-done.10.rest_7_), channel_id=1, source_target_pairs={{0,32},{16,496},{1,33},{17,497},{2,34},{18,498},{3,35},{19,499},{4... | collective-permute-start | bytes 786440 | tf_op jit(solution)/shard_map/ppermute | solution.py:112
  47.8 36.1 %collective-permute-start.1 = (bf16[512,1024]{1,0:T(8,128)(2,1)S(1)}, bf16[512,1024]{1,0:T(8,128)(2,1)S(1)}, u32[]{:S(2)}, u32[]{:S(2)}) collective-permute-start(bf16[512,1024]{1,0:T(8,128)(2,1)S(1)} %bitcast_multiply_fusion.own), channel_id=1, source_target_pairs={{0,16},{1,17},{2,18},{3,19},{4,20},{5,21},{6,22},{7,23},{8,24},{9,... | collective-permute-start | bytes 3145736 | tf_op jit(solution)/shard_map/ppermute | solution.py:117
  49.7 16.7 %copy-start.10 = (bf16[1024,128]{1,0:T(8,128)(2,1)}, bf16[1024,128]{1,0:T(8,128)(2,1)S(1)}, u32[]{:S(2)}) copy-start(bf16[1024,128]{1,0:T(8,128)(2,1)S(1)} %collective-permute-done.6.rest_3_) | copy-start | bytes 786436
  49.7 9.2 %collective-permute-start.7 = (bf16[1024,128]{1,0:T(8,128)(2,1)S(1)}, bf16[1024,128]{1,0:T(8,128)(2,1)S(1)}, u32[]{:S(2)}, u32[]{:S(2)}) collective-permute-start(bf16[1024,128]{1,0:T(8,128)(2,1)S(1)} %collective-permute-done.6.rest_3_), channel_id=1, source_target_pairs={{0,32},{16,496},{1,33},{17,497},{2,34},{18,498},{3,35},{19,499},{4... | collective-permute-start | bytes 786440 | tf_op jit(solution)/shard_map/ppermute | solution.py:112
  54.1 12.8 %copy-start.11 = (bf16[1024,128]{1,0:T(8,128)(2,1)}, bf16[1024,128]{1,0:T(8,128)(2,1)S(1)}, u32[]{:S(2)}) copy-start(bf16[1024,128]{1,0:T(8,128)(2,1)S(1)} %collective-permute-done.11.rest_8_) | copy-start | bytes 786436
  54.1 9.5 %collective-permute-start.12 = (bf16[1024,128]{1,0:T(8,128)(2,1)S(1)}, bf16[1024,128]{1,0:T(8,128)(2,1)S(1)}, u32[]{:S(2)}, u32[]{:S(2)}) collective-permute-start(bf16[1024,128]{1,0:T(8,128)(2,1)S(1)} %collective-permute-done.11.rest_8_), channel_id=1, source_target_pairs={{0,32},{16,496},{1,33},{17,497},{2,34},{18,498},{3,35},{19,499},{4... | collective-permute-start | bytes 786440 | tf_op jit(solution)/shard_map/ppermute | solution.py:112
  56.9 31.2 %copy-start.1 = (bf16[512,1024]{1,0:T(8,128)(2,1)}, bf16[512,1024]{1,0:T(8,128)(2,1)S(1)}, u32[]{:S(2)}) copy-start(bf16[512,1024]{1,0:T(8,128)(2,1)S(1)} %collective-permute-done.beside) | copy-start | bytes 3145732
  56.9 26.9 %collective-permute-start.2 = (bf16[512,1024]{1,0:T(8,128)(2,1)S(1)}, bf16[512,1024]{1,0:T(8,128)(2,1)}, u32[]{:S(2)}, u32[]{:S(2)}) collective-permute-start(bf16[512,1024]{1,0:T(8,128)(2,1)S(1)} %collective-permute-done.beside), channel_id=1, source_target_pairs={{0,16},{1,17},{2,18},{3,19},{4,20},{5,21},{6,22},{7,23},{8,24},{9,... | collective-permute-start | bytes 3145736 | tf_op jit(solution)/shard_map/ppermute | solution.py:118
  58.9 13.0 %copy-start.12 = (bf16[1024,128]{1,0:T(8,128)(2,1)}, bf16[1024,128]{1,0:T(8,128)(2,1)S(1)}, u32[]{:S(2)}) copy-start(bf16[1024,128]{1,0:T(8,128)(2,1)S(1)} %collective-permute-done.7.rest_4_) | copy-start | bytes 786436
  58.9 8.0 %collective-permute-start.13 = (bf16[1024,128]{1,0:T(8,128)(2,1)S(1)}, bf16[1024,128]{1,0:T(8,128)(2,1)S(1)}, u32[]{:S(2)}, u32[]{:S(2)}) collective-permute-start(bf16[1024,128]{1,0:T(8,128)(2,1)S(1)} %collective-permute-done.7.rest_4_), channel_id=1, source_target_pairs={{0,32},{16,496},{1,33},{17,497},{2,34},{18,498},{3,35},{19,499},{4... | collective-permute-start | bytes 786440 | tf_op jit(solution)/shard_map/ppermute | solution.py:112
  63.6 8.3 %collective-permute-start.16 = (bf16[1024,128]{1,0:T(8,128)(2,1)S(1)}, bf16[1024,128]{1,0:T(8,128)(2,1)S(1)}, u32[]{:S(2)}, u32[]{:S(2)}) collective-permute-start(bf16[1024,128]{1,0:T(8,128)(2,1)S(1)} %collective-permute-done.12.rest_9_), channel_id=1, source_target_pairs={{0,32},{16,496},{1,33},{17,497},{2,34},{18,498},{3,35},{19,499},{4... | collective-permute-start | bytes 786440 | tf_op jit(solution)/shard_map/ppermute | solution.py:112
  66.9 8.3 %collective-permute-start.14 = (bf16[1024,128]{1,0:T(8,128)(2,1)S(1)}, bf16[1024,128]{1,0:T(8,128)(2,1)}, u32[]{:S(2)}, u32[]{:S(2)}) collective-permute-start(bf16[1024,128]{1,0:T(8,128)(2,1)S(1)} %collective-permute-done.13.rest_0_), channel_id=1, source_target_pairs={{0,32},{16,496},{1,33},{17,497},{2,34},{18,498},{3,35},{19,499},{4... | collective-permute-start | bytes 786440 | tf_op jit(solution)/shard_map/ppermute | solution.py:112
  72.0 8.4 %collective-permute-start.17 = (bf16[1024,128]{1,0:T(8,128)(2,1)S(1)}, bf16[1024,128]{1,0:T(8,128)(2,1)}, u32[]{:S(2)}, u32[]{:S(2)}) collective-permute-start(bf16[1024,128]{1,0:T(8,128)(2,1)S(1)} %collective-permute-done.16.rest_3_), channel_id=1, source_target_pairs={{0,32},{16,496},{1,33},{17,497},{2,34},{18,498},{3,35},{19,499},{4... | collective-permute-start | bytes 786440 | tf_op jit(solution)/shard_map/ppermute | solution.py:112
  75.2 8.7 %collective-permute-start.15 = (bf16[1024,128]{1,0:T(8,128)(2,1)}, bf16[1024,128]{1,0:T(8,128)(2,1)}, u32[]{:S(2)}, u32[]{:S(2)}) collective-permute-start(bf16[1024,128]{1,0:T(8,128)(2,1)} %collective-permute-done.14.rest_1_), channel_id=1, source_target_pairs={{0,32},{16,496},{1,33},{17,497},{2,34},{18,498},{3,35},{19,499},{4... | collective-permute-start | bytes 786440 | tf_op jit(solution)/shard_map/ppermute | solution.py:112
  80.3 7.7 %collective-permute-start.18 = (bf16[1024,128]{1,0:T(8,128)(2,1)}, bf16[1024,128]{1,0:T(8,128)(2,1)}, u32[]{:S(2)}, u32[]{:S(2)}) collective-permute-start(bf16[1024,128]{1,0:T(8,128)(2,1)} %collective-permute-done.17.rest_4_), channel_id=1, source_target_pairs={{0,32},{16,496},{1,33},{17,497},{2,34},{18,498},{3,35},{19,499},{4... | collective-permute-start | bytes 786440 | tf_op jit(solution)/shard_map/ppermute | solution.py:112
  93.9 26.3 %all-to-all-start.1 = ((bf16[32,32,384]{2,1,0:T(8,128)(2,1)}), bf16[32,32,384]{2,1,0:T(8,128)(2,1)S(1)}, u32[]{:S(2)}, u32[]{:S(2)}) async-start(bf16[32,32,384]{2,1,0:T(8,128)(2,1)} %bitcast.36), calls=%async_computation.1 | async-start | bytes 1572864 | tf_op jit(solution)/shard_map/all_to_all | solution.py:126
  120.2 24.4 %all-to-all-start = ((bf16[32,32,640]{2,1,0:T(8,128)(2,1)}), bf16[32,32,640]{2,1,0:T(8,128)(2,1)S(1)}, u32[]{:S(2)}, u32[]{:S(2)}) async-start(bf16[32,32,640]{2,1,0:T(8,128)(2,1)} %bitcast.32), calls=%async_computation | async-start | bytes 2621440 | tf_op jit(solution)/shard_map/all_to_all | solution.py:126
  (6 other events, 41.3 us)

commit v3 on v2

--- a/solution.py
+++ b/solution.py
@@ -47,65 +47,121 @@
     ]
 
 
-def chunks_of(nslot):
-    last = 3 * nslot // 8
-    return (nslot - last, last)
-
-
-def multiply(choice, blocks, tiles):
+CHUNKS = ((3, 2), (2, 1))
+
+
+def calls_of():
+    calls = []
+    slot = 0
+    for k, chunk in enumerate(CHUNKS):
+        begin = 0
+        for count in chunk:
+            slot += count
+            calls.append((slot, k, count, begin, sum(chunk)))
+            begin += count
+    return calls
+
+
+def masked_tile(integrals, occupancy):
+    def body(occ, tile, out):
+        for k in range(tile.shape[0] // TILE):
+            rows = slice(k * TILE, (k + 1) * TILE)
+            out[rows, :] = tile[rows, :] * occ[k].astype(jnp.float32).astype(jnp.bfloat16)
+
+    return pl.pallas_call(
+        body,
+        in_specs=[pl.BlockSpec(memory_space=pltpu.SMEM), pl.BlockSpec(memory_space=pltpu.VMEM)],
+        out_specs=pl.BlockSpec(memory_space=pltpu.VMEM),
+        out_shape=jax.ShapeDtypeStruct(integrals.shape, jnp.bfloat16),
+        name="masked_tile",
+    )(occupancy.reshape(-1), integrals)
+
+
+def multiply(choice, blocks, tiles, start, width, previous):
     nrow, kloc = blocks[0].shape
     count = len(tiles[0])
-    width = count * TILE
+    part = count * TILE
     step = nrow // 2
+    steps = nrow // step
 
     def body(choice_ref, own, beside, own_other, beside_other, *rest):
-        tile_refs, out, right = rest[: 2 * count], rest[2 * count], rest[2 * count + 1]
-
-        @pl.when(pl.program_id(0) == 0)
+        tile_refs = rest[: 2 * count]
+        out, right, total, sem = rest[-4:]
+        m = pl.program_id(0)
+        stream, core = choice_ref[0], choice_ref[1]
+
+        def copy_out(at, half):
+            side = core if half == 0 else 1 - core
+            target = out.at[side, pl.ds(at * step, step), pl.ds(start, part)]
+            return pltpu.make_async_copy(total.at[at, half], target, sem.at[at, half])
+
+        @pl.when(m == 0)
         def _():
             for i in range(2 * count):
                 right[i // count, :, (i % count) * TILE : (i % count + 1) * TILE] = tile_refs[i][...]
 
         near = jnp.concatenate([own[...], own_other[...]], 0)
         far = jnp.concatenate([beside[...], beside_other[...]], 0)
-        stream, core = choice_ref[0], choice_ref[1]
-        for start in range(0, width, 2 * TILE):
-            cols = slice(start, min(start + 2 * TILE, width))
-            total = jnp.dot(near, right[stream, :, cols], preferred_element_type=jnp.float32)
-            total += jnp.dot(far, right[1 - stream, :, cols], preferred_element_type=jnp.float32)
-            total = total.astype(jnp.bfloat16)
-            out[core, :, cols] = total[:step]
-            out[1 - core, :, cols] = total[step:]
+        for first in range(0, part, 2 * TILE):
+            cols = slice(first, min(first + 2 * TILE, part))
+            value = jnp.dot(near, right[stream, :, cols], preferred_element_type=jnp.float32)
+            value += jnp.dot(far, right[1 - stream, :, cols], preferred_element_type=jnp.float32)
+            value = value.astype(jnp.bfloat16)
+            total[m, 0, :, cols] = value[:step]
+            total[m, 1, :, cols] = value[step:]
+        for half in (0, 1):
+            copy_out(m, half).start()
+
+        @pl.when(m == steps - 1)
+        def _():
+            for at in range(steps):
+                for half in (0, 1):
+                    copy_out(at, half).wait()
 
     left = pl.BlockSpec((step, kloc), lambda m: (m, 0))
     whole = pl.BlockSpec((kloc, TILE), lambda m: (0, 0))
+    anywhere = pl.BlockSpec(memory_space=pl.ANY)
+    operands = [choice, *blocks, *tiles[0], *tiles[1]]
+    specs = [pl.BlockSpec(memory_space=pltpu.SMEM)] + [left] * 4 + [whole] * (2 * count)
+    aliases = {}
+    if previous is not None:
+        aliases = {len(operands): 0}
+        operands.append(previous)
+        specs.append(anywhere)
     return pl.pallas_call(
         body,
-        grid=(nrow // step,),
-        in_specs=[pl.BlockSpec(memory_space=pltpu.SMEM)] + [left] * 4 + [whole] * (2 * count),
-        out_specs=pl.BlockSpec((2, step, width), lambda m: (0, m, 0)),
+        grid=(steps,),
+        in_specs=specs,
+        out_specs=anywhere,
         out_shape=jax.ShapeDtypeStruct((2, nrow, width), jnp.bfloat16),
-        scratch_shapes=[pltpu.VMEM((2, kloc, width), jnp.bfloat16)],
+        scratch_shapes=[
+            pltpu.VMEM((2, kloc, part), jnp.bfloat16),
+            pltpu.VMEM((steps, 2, step, part), jnp.bfloat16),
+            pltpu.SemaphoreType.DMA((steps, 2)),
+        ],
+        input_output_aliases=aliases,
         name="multiply",
-    )(choice, *blocks, *tiles[0], *tiles[1])
+    )(*operands)
 
 
 def make(nz, ncol):
     every = ("z", "core", "col")
     nslot = nz // 2
-    sizes = chunks_of(nslot)
-    ends = [sum(sizes[: i + 1]) for i in range(len(sizes))]
+    assert sum(map(sum, CHUNKS)) == nslot
 
     def on_device(amplitudes, integrals, amp_occupancy, int_occupancy, owner_map):
         z = lax.axis_index("z")
         core = lax.axis_index("core")
         odd = lax.axis_index("col") % 2
-        own_tile = mask_tiles(integrals, int_occupancy)
+        own_tile = masked_tile(integrals, int_occupancy)
         nrow, _ = amplitudes.shape
         part = nrow // ncol
         current = [own_tile, own_tile]
         sums = []
         tiles = [[], []]
+        ends = calls_of()
+        call = 0
+        product = None
         for slot in range(1, nslot + 1):
             for stream in (0, 1):
                 pairs = first_pairs(nz, ncol, stream) if slot == 1 else ring_pairs(nz, ncol)
@@ -118,12 +174,17 @@
                 beside_other = lax.ppermute(beside, every, swap_pairs(nz, ncol, 1, 0))
                 blocks = (own, beside, own_other, beside_other)
                 choice = jnp.stack([odd ^ core, core]).astype(jnp.int32)
-            if slot in ends:
-                product = multiply(choice, blocks, tiles)
+            if slot == ends[call][0]:
+                _, _, count, begin, width = ends[call]
+                product = multiply(choice, blocks, tiles, begin * TILE, width * TILE, product)
                 tiles = [[], []]
+                call += 1
+                if begin + count < width:
+                    continue
                 width = product.shape[-1]
-                product = product.reshape(2 * ncol, part, width)
-                moved = lax.all_to_all(product, ("core", "col"), 0, 0, tiled=True)
+                moved = product.reshape(2 * ncol, part, width)
+                product = None
+                moved = lax.all_to_all(moved, ("core", "col"), 0, 0, tiled=True)
                 moved = moved.reshape(2, ncol // 2, 2, part, width)
                 total = jnp.sum(moved.astype(jnp.float32), 1)
                 sums.append(total.astype(jnp.bfloat16))

time: 158 us -> 173 us (1.095)
  waiting for transfers between devices: 33.8 us -> 44.1 us
  Pallas kernels: 13.3 us -> 20.5 us
  other arithmetic: 3.75 us -> 1.84 us
    ppermute x16, waiting for transfers between devices: 8.49 us -> 21.6 us  [on_device(): current[stream] = lax.ppermute(current[stream], every, pairs)]
    pallas_call x2 -> x5, Pallas kernels: 13.3 us -> 20.5 us  [the longest x4 18.7 us: multiply(): pl.pallas_call(body, grid=(steps,), in_specs=specs, out_specs=anywhere, o...]
    all_to_all x2, waiting for transfers between devices: 25.3 us -> 22.5 us  [on_device(): moved = lax.all_to_all(moved, ('core', 'col'), 0, 0, tiled=True)]
    ppermute x16, starting transfers between devices: 69.7 us -> 67.3 us  [on_device(): current[stream] = lax.ppermute(current[stream], every, pairs)]
  transfers between devices with their start and end apart: 21 -> 21, of which waited for: 9 -> 6; matrix products, arithmetic and copies ran while one was open for 1% -> 1% of each run, Pallas kernels for 5% -> 9%
where the time goes in v3:
time: 173 us; the launch traced here: 172 us
  starting transfers between devices  91.7 us (53%)
  waiting for transfers between devices  44.1 us (25%)
  Pallas kernels  20.5 us (12%)
  blocking collectives  10.9 us (6%)
  local copies, waits for them, and re-layouts  2.71 us (2%)
  other arithmetic  1.84 us (1%)
    ppermute x16, starting transfers between devices, on_device(): current[stream] = lax.ppermute(current[stream], every, pairs)  67.3 us
    all_to_all x2, waiting for transfers between devices, on_device(): moved = lax.all_to_all(moved, ('core', 'col'), 0, 0, tiled=True)  22.5 us
    ppermute x16, waiting for transfers between devices, on_device(): current[stream] = lax.ppermute(current[stream], every, pairs)  21.6 us
    pallas_call x4, Pallas kernels, multiply(): pl.pallas_call(body, grid=(steps,), in_specs=specs, out_specs=anywhere, o...  18.7 us
    all_to_all x2, starting transfers between devices, on_device(): moved = lax.all_to_all(moved, ('core', 'col'), 0, 0, tiled=True)  18.1 us
    all_to_all x1, blocking collectives, on_device(): final = lax.all_to_all(picked, 'col', 0, 0, tiled=True)  10.9 us
  transfers between devices with their start and end apart: 21, of which 6 were waited for; matrix products, arithmetic and copies ran while one was open for 1% of the time, Pallas kernels for 9%

profile of v3, /device:TPU:1, one launch (start us, length us, event | category | flops | bytes accessed | tf_op | source)
XLA Modules:
  0.0 172.4 jit_solution(17171378674308807555)
XLA Ops:
  0.0 1.8 %masked_tile.1 = bf16[1024,128]{1,0:T(8,128)(2,1)} custom-call(s32[8]{0:T(128)} %bitcast.40, bf16[1024,128]{1,0:T(8,128)(2,1)} %tile.1), custom_call_target="tpu_custom_call" | custom-call | tf_op jit(solution)/shard_map/masked_tile/pallas_call | solution.py:71
  1.8 5.8 %collective-permute-start.3 = (bf16[1024,128]{1,0:T(8,128)(2,1)}, bf16[1024,128]{1,0:T(8,128)(2,1)S(1)}, u32[]{:S(2)}, u32[]{:S(2)}) collective-permute-start(bf16[1024,128]{1,0:T(8,128)(2,1)} %masked_tile.1), channel_id=1, source_target_pairs={{0,32},{1,16},{16,33},{17,17},{2,34},{3,18},{18,35},{19,19},{4,36}... | collective-permute-start | bytes 786440 | tf_op jit(solution)/shard_map/ppermute | solution.py:168
  8.7 1.9 %collective-permute-start = (bf16[512,1024]{1,0:T(8,128)(2,1)S(1)}, bf16[512,1024]{1,0:T(8,128)(2,1)S(1)}, u32[]{:S(2)}, u32[]{:S(2)}) collective-permute-start(bf16[512,1024]{1,0:T(8,128)(2,1)S(1)} %bitcast_multiply_fusion.own), channel_id=1, source_target_pairs={{0,1},{1,0},{2,3},{3,2},{4,5},{5,4},{6,7},{7,6},{8,9},{9,8},{10,11... | collective-permute-start | bytes 3145736 | tf_op jit(solution)/shard_map/ppermute | solution.py:172
  10.7 3.4 %collective-permute-start.8 = (bf16[1024,128]{1,0:T(8,128)(2,1)S(1)}, bf16[1024,128]{1,0:T(8,128)(2,1)S(1)}, u32[]{:S(2)}, u32[]{:S(2)}) collective-permute-start(bf16[1024,128]{1,0:T(8,128)(2,1)S(1)} %copy-done.16), channel_id=1, source_target_pairs={{1,32},{0,16},{17,33},{16,17},{3,34},{2,18},{19,35},{18,19},{5,36}... | collective-permute-start | bytes 786440 | tf_op jit(solution)/shard_map/ppermute | solution.py:168
  14.0 8.5 %collective-permute-start.4 = (bf16[1024,128]{1,0:T(8,128)(2,1)S(1)}, bf16[1024,128]{1,0:T(8,128)(2,1)S(1)}, u32[]{:S(2)}, u32[]{:S(2)}) collective-permute-start(bf16[1024,128]{1,0:T(8,128)(2,1)S(1)} %collective-permute-done.3.rest_0_), channel_id=1, source_target_pairs={{0,32},{16,496},{1,33},{17,497},{2,34},{18,498},{3,35},{19,499},{4... | collective-permute-start | bytes 786440 | tf_op jit(solution)/shard_map/ppermute | solution.py:168
  22.6 16.4 %collective-permute-done.8.rest_3_ = bf16[1024,128]{1,0:T(8,128)(2,1)S(1)} collective-permute-done((bf16[1024,128]{1,0:T(8,128)(2,1)S(1)}, bf16[1024,128]{1,0:T(8,128)(2,1)S(1)}, u32[]{:S(2)}, u32[]{:S(2)}) %collective-permute-start.8) | collective-permute-done | bytes 262176 | tf_op jit(solution)/shard_map/ppermute | solution.py:168
  39.0 8.6 %collective-permute-start.9 = (bf16[1024,128]{1,0:T(8,128)(2,1)S(1)}, bf16[1024,128]{1,0:T(8,128)(2,1)S(1)}, u32[]{:S(2)}, u32[]{:S(2)}) collective-permute-start(bf16[1024,128]{1,0:T(8,128)(2,1)S(1)} %collective-permute-done.8.rest_3_), channel_id=1, source_target_pairs={{0,32},{16,496},{1,33},{17,497},{2,34},{18,498},{3,35},{19,499},{4... | collective-permute-start | bytes 786440 | tf_op jit(solution)/shard_map/ppermute | solution.py:168
  47.6 3.3 %collective-permute-start.5 = (bf16[1024,128]{1,0:T(8,128)(2,1)S(1)}, bf16[1024,128]{1,0:T(8,128)(2,1)S(1)}, u32[]{:S(2)}, u32[]{:S(2)}) collective-permute-start(bf16[1024,128]{1,0:T(8,128)(2,1)S(1)} %collective-permute-done.4.rest_1_), channel_id=1, source_target_pairs={{0,32},{16,496},{1,33},{17,497},{2,34},{18,498},{3,35},{19,499},{4... | collective-permute-start | bytes 786440 | tf_op jit(solution)/shard_map/ppermute | solution.py:168
  51.0 5.0 %collective-permute-start.10 = (bf16[1024,128]{1,0:T(8,128)(2,1)S(1)}, bf16[1024,128]{1,0:T(8,128)(2,1)S(1)}, u32[]{:S(2)}, u32[]{:S(2)}) collective-permute-start(bf16[1024,128]{1,0:T(8,128)(2,1)S(1)} %collective-permute-done.9.rest_4_), channel_id=1, source_target_pairs={{0,32},{16,496},{1,33},{17,497},{2,34},{18,498},{3,35},{19,499},{4... | collective-permute-start | bytes 786440 | tf_op jit(solution)/shard_map/ppermute | solution.py:168
  55.9 3.3 %collective-permute-start.6 = (bf16[1024,128]{1,0:T(8,128)(2,1)S(1)}, bf16[1024,128]{1,0:T(8,128)(2,1)S(1)}, u32[]{:S(2)}, u32[]{:S(2)}) collective-permute-start(bf16[1024,128]{1,0:T(8,128)(2,1)S(1)} %collective-permute-done.5.rest_2_), channel_id=1, source_target_pairs={{0,32},{16,496},{1,33},{17,497},{2,34},{18,498},{3,35},{19,499},{4... | collective-permute-start | bytes 786440 | tf_op jit(solution)/shard_map/ppermute | solution.py:168
  59.3 5.0 %collective-permute-start.11 = (bf16[1024,128]{1,0:T(8,128)(2,1)S(1)}, bf16[1024,128]{1,0:T(8,128)(2,1)S(1)}, u32[]{:S(2)}, u32[]{:S(2)}) collective-permute-start(bf16[1024,128]{1,0:T(8,128)(2,1)S(1)} %collective-permute-done.10.rest_5_), channel_id=1, source_target_pairs={{0,32},{16,496},{1,33},{17,497},{2,34},{18,498},{3,35},{19,499},{4... | collective-permute-start | bytes 786440 | tf_op jit(solution)/shard_map/ppermute | solution.py:168
  64.3 1.9 %collective-permute-start.1 = (bf16[512,1024]{1,0:T(8,128)(2,1)S(1)}, bf16[512,1024]{1,0:T(8,128)(2,1)S(1)}, u32[]{:S(2)}, u32[]{:S(2)}) collective-permute-start(bf16[512,1024]{1,0:T(8,128)(2,1)S(1)} %bitcast_multiply_fusion.own), channel_id=1, source_target_pairs={{0,16},{1,17},{2,18},{3,19},{4,20},{5,21},{6,22},{7,23},{8,24},{9,... | collective-permute-start | bytes 3145736 | tf_op jit(solution)/shard_map/ppermute | solution.py:173
  66.2 2.4 %collective-permute-start.2 = (bf16[512,1024]{1,0:T(8,128)(2,1)S(1)}, bf16[512,1024]{1,0:T(8,128)(2,1)}, u32[]{:S(2)}, u32[]{:S(2)}) collective-permute-start(bf16[512,1024]{1,0:T(8,128)(2,1)S(1)} %collective-permute-done.beside), channel_id=1, source_target_pairs={{0,16},{1,17},{2,18},{3,19},{4,20},{5,21},{6,22},{7,23},{8,24},{9,... | collective-permute-start | bytes 3145736 | tf_op jit(solution)/shard_map/ppermute | solution.py:174
  68.7 1.9 %collective-permute-start.7 = (bf16[1024,128]{1,0:T(8,128)(2,1)S(1)}, bf16[1024,128]{1,0:T(8,128)(2,1)S(1)}, u32[]{:S(2)}, u32[]{:S(2)}) collective-permute-start(bf16[1024,128]{1,0:T(8,128)(2,1)S(1)} %collective-permute-done.6.rest_0_), channel_id=1, source_target_pairs={{0,32},{16,496},{1,33},{17,497},{2,34},{18,498},{3,35},{19,499},{4... | collective-permute-start | bytes 786440 | tf_op jit(solution)/shard_map/ppermute | solution.py:168
  70.6 2.2 %collective-permute-start.12 = (bf16[1024,128]{1,0:T(8,128)(2,1)S(1)}, bf16[1024,128]{1,0:T(8,128)(2,1)S(1)}, u32[]{:S(2)}, u32[]{:S(2)}) collective-permute-start(bf16[1024,128]{1,0:T(8,128)(2,1)S(1)} %collective-permute-done.11.rest_2_), channel_id=1, source_target_pairs={{0,32},{16,496},{1,33},{17,497},{2,34},{18,498},{3,35},{19,499},{4... | collective-permute-start | bytes 786440 | tf_op jit(solution)/shard_map/ppermute | solution.py:168
  72.9 3.2 %collective-permute-done.7.rest_1_ = bf16[1024,128]{1,0:T(8,128)(2,1)S(1)} collective-permute-done((bf16[1024,128]{1,0:T(8,128)(2,1)S(1)}, bf16[1024,128]{1,0:T(8,128)(2,1)S(1)}, u32[]{:S(2)}, u32[]{:S(2)}) %collective-permute-start.7) | collective-permute-done | bytes 262176 | tf_op jit(solution)/shard_map/ppermute | solution.py:168
  76.1 2.8 %collective-permute-start.13 = (bf16[1024,128]{1,0:T(8,128)(2,1)S(1)}, bf16[1024,128]{1,0:T(8,128)(2,1)S(1)}, u32[]{:S(2)}, u32[]{:S(2)}) collective-permute-start(bf16[1024,128]{1,0:T(8,128)(2,1)S(1)} %collective-permute-done.7.rest_1_), channel_id=1, source_target_pairs={{0,32},{16,496},{1,33},{17,497},{2,34},{18,498},{3,35},{19,499},{4... | collective-permute-start | bytes 786440 | tf_op jit(solution)/shard_map/ppermute | solution.py:168
  79.0 2.8 %collective-permute-start.16 = (bf16[1024,128]{1,0:T(8,128)(2,1)S(1)}, bf16[1024,128]{1,0:T(8,128)(2,1)S(1)}, u32[]{:S(2)}, u32[]{:S(2)}) collective-permute-start(bf16[1024,128]{1,0:T(8,128)(2,1)S(1)} %collective-permute-done.12.rest_3_), channel_id=1, source_target_pairs={{0,32},{16,496},{1,33},{17,497},{2,34},{18,498},{3,35},{19,499},{4... | collective-permute-start | bytes 786440 | tf_op jit(solution)/shard_map/ppermute | solution.py:168
  81.7 1.5 collective-permute-done.13.rest_0_
  83.2 4.0 %collective-permute-start.14 = (bf16[1024,128]{1,0:T(8,128)(2,1)S(1)}, bf16[1024,128]{1,0:T(8,128)(2,1)}, u32[]{:S(2)}, u32[]{:S(2)}) collective-permute-start(bf16[1024,128]{1,0:T(8,128)(2,1)S(1)} %collective-permute-done.13.rest_0_), channel_id=1, source_target_pairs={{0,32},{16,496},{1,33},{17,497},{2,34},{18,498},{3,35},{19,499},{4... | collective-permute-start | bytes 786440 | tf_op jit(solution)/shard_map/ppermute | solution.py:168
  87.3 2.8 %collective-permute-start.17 = (bf16[1024,128]{1,0:T(8,128)(2,1)S(1)}, bf16[1024,128]{1,0:T(8,128)(2,1)}, u32[]{:S(2)}, u32[]{:S(2)}) collective-permute-start(bf16[1024,128]{1,0:T(8,128)(2,1)S(1)} %collective-permute-done.16.rest_2_), channel_id=1, source_target_pairs={{0,32},{16,496},{1,33},{17,497},{2,34},{18,498},{3,35},{19,499},{4... | collective-permute-start | bytes 786440 | tf_op jit(solution)/shard_map/ppermute | solution.py:168
  90.5 5.1 %collective-permute-start.15 = (bf16[1024,128]{1,0:T(8,128)(2,1)}, bf16[1024,128]{1,0:T(8,128)(2,1)}, u32[]{:S(2)}, u32[]{:S(2)}) collective-permute-start(bf16[1024,128]{1,0:T(8,128)(2,1)} %collective-permute-done.14.rest_1_), channel_id=1, source_target_pairs={{0,32},{16,496},{1,33},{17,497},{2,34},{18,498},{3,35},{19,499},{4... | collective-permute-start | bytes 786440 | tf_op jit(solution)/shard_map/ppermute | solution.py:168
  95.7 2.8 %collective-permute-start.18 = (bf16[1024,128]{1,0:T(8,128)(2,1)}, bf16[1024,128]{1,0:T(8,128)(2,1)}, u32[]{:S(2)}, u32[]{:S(2)}) collective-permute-start(bf16[1024,128]{1,0:T(8,128)(2,1)} %collective-permute-done.17.rest_3_), channel_id=1, source_target_pairs={{0,32},{16,496},{1,33},{17,497},{2,34},{18,498},{3,35},{19,499},{4... | collective-permute-start | bytes 786440 | tf_op jit(solution)/shard_map/ppermute | solution.py:168
  100.1 4.4 %multiply.6.rest_2_ = bf16[2,512,384]{2,1,0:T(8,128)(2,1)} custom-call(s32[2]{0:T(128)} %pad_add_fusion.choice_ref, bf16[512,1024]{1,0:T(8,128)(2,1)} %copy-done, bf16[512,1024]{1,0:T(8,128)(2,1)} %copy-done.1, bf16[512,1024]{1,0:T(8,128)(2,1)} %copy-done.2, bf16[512,1024]{1,0:T(8,128)(2,1)} %collective-permute-done.2.beside_other, ...), custom_call_target="tpu_custom_call" | custom-call | tf_op jit(solution)/shard_map/multiply/pallas_call | solution.py:131
  104.6 4.1 %multiply.7 = bf16[2,512,384]{2,1,0:T(8,128)(2,1)} custom-call(s32[2]{0:T(128)} %pad_add_fusion.choice_ref, bf16[512,1024]{1,0:T(8,128)(2,1)} %copy-done, bf16[512,1024]{1,0:T(8,128)(2,1)} %copy-done.1, bf16[512,1024]{1,0:T(8,128)(2,1)} %copy-done.2, bf16[512,1024]{1,0:T(8,128)(2,1)} %collective-permute-done.2.beside_other, ...), custom_call_target="tpu_custom_call", output_to_operand_aliasing={{}: (7, {})} | custom-call | tf_op jit(solution)/shard_map/multiply/pallas_call | solution.py:131
  108.6 13.0 %all-to-all-start.1 = ((bf16[32,32,384]{2,1,0:T(8,128)(2,1)}), bf16[32,32,384]{2,1,0:T(8,128)(2,1)S(1)}, u32[]{:S(2)}, u32[]{:S(2)}) async-start(bf16[32,32,384]{2,1,0:T(8,128)(2,1)} %bitcast.30), calls=%async_computation.1 | async-start | bytes 1572864 | tf_op jit(solution)/shard_map/all_to_all | solution.py:187
  121.7 5.8 %multiply.4.rest_4_ = bf16[2,512,640]{2,1,0:T(8,128)(2,1)} custom-call(s32[2]{0:T(128)} %pad_add_fusion.choice_ref, bf16[512,1024]{1,0:T(8,128)(2,1)} %copy-done, bf16[512,1024]{1,0:T(8,128)(2,1)} %copy-done.1, bf16[512,1024]{1,0:T(8,128)(2,1)} %copy-done.2, bf16[512,1024]{1,0:T(8,128)(2,1)} %collective-permute-done.2.beside_other, ...), custom_call_target="tpu_custom_call" | custom-call | tf_op jit(solution)/shard_map/multiply/pallas_call | solution.py:131
  127.5 4.4 %multiply.5 = bf16[2,512,640]{2,1,0:T(8,128)(2,1)} custom-call(s32[2]{0:T(128)} %pad_add_fusion.choice_ref, bf16[512,1024]{1,0:T(8,128)(2,1)} %copy-done, bf16[512,1024]{1,0:T(8,128)(2,1)} %copy-done.1, bf16[512,1024]{1,0:T(8,128)(2,1)} %copy-done.2, bf16[512,1024]{1,0:T(8,128)(2,1)} %collective-permute-done.2.beside_other, ...), custom_call_target="tpu_custom_call", output_to_operand_aliasing={{}: (9, {})} | custom-call | tf_op jit(solution)/shard_map/multiply/pallas_call | solution.py:131
  132.0 3.3 %all-to-all-done.1 = bf16[32,32,384]{2,1,0:T(8,128)(2,1)S(1)} async-done(((bf16[32,32,384]{2,1,0:T(8,128)(2,1)}), bf16[32,32,384]{2,1,0:T(8,128)(2,1)S(1)}, u32[]{:S(2)}, u32[]{:S(2)}) %all-to-all-start.1) | async-done | bytes 786464 | tf_op jit(solution)/shard_map/all_to_all | solution.py:187
  135.4 5.1 %all-to-all-start = ((bf16[32,32,640]{2,1,0:T(8,128)(2,1)}), bf16[32,32,640]{2,1,0:T(8,128)(2,1)S(1)}, u32[]{:S(2)}, u32[]{:S(2)}) async-start(bf16[32,32,640]{2,1,0:T(8,128)(2,1)} %bitcast.29), calls=%async_computation | async-start | bytes 2621440 | tf_op jit(solution)/shard_map/all_to_all | solution.py:187
  140.6 19.1 %all-to-all-done = bf16[32,32,640]{2,1,0:T(8,128)(2,1)S(1)} async-done(((bf16[32,32,640]{2,1,0:T(8,128)(2,1)}), bf16[32,32,640]{2,1,0:T(8,128)(2,1)S(1)}, u32[]{:S(2)}, u32[]{:S(2)}) %all-to-all-start) | async-done | bytes 1310752 | tf_op jit(solution)/shard_map/all_to_all | solution.py:187
  160.8 10.9 %all_to_all.15 = bf16[16,32,256]{2,1,0:T(8,128)(2,1)S(1)} all-to-all(bf16[16,32,256]{2,1,0:T(8,128)(2,1)S(1)} %bitcast.38), channel_id=1, replica_groups=mesh['z'=16,'core'=2,'col'=16] {'col'}, dimensions={0} | all-to-all | bytes 524288 | tf_op jit(solution)/shard_map/all_to_all | solution.py:201
  (67 shorter events, 5.1 us)
Async XLA Ops:
  0.0 8.5 %copy-start.3 = (bf16[512,1024]{1,0:T(8,128)(2,1)S(1)}, bf16[512,1024]{1,0:T(8,128)(2,1)}, u32[]{:S(2)}) copy-start(bf16[512,1024]{1,0:T(8,128)(2,1)} %param.5) | copy-start | bytes 3145732
  1.8 12.2 %collective-permute-start.3 = (bf16[1024,128]{1,0:T(8,128)(2,1)}, bf16[1024,128]{1,0:T(8,128)(2,1)S(1)}, u32[]{:S(2)}, u32[]{:S(2)}) collective-permute-start(bf16[1024,128]{1,0:T(8,128)(2,1)} %masked_tile.1), channel_id=1, source_target_pairs={{0,32},{1,16},{16,33},{17,17},{2,34},{3,18},{18,35},{19,19},{4,36}... | collective-permute-start | bytes 786440 | tf_op jit(solution)/shard_map/ppermute | solution.py:168
  8.7 90.4 %copy-start = (bf16[512,1024]{1,0:T(8,128)(2,1)}, bf16[512,1024]{1,0:T(8,128)(2,1)S(1)}, u32[]{:S(2)}) copy-start(bf16[512,1024]{1,0:T(8,128)(2,1)S(1)} %bitcast_multiply_fusion.own) | copy-start | bytes 3145732
  8.7 57.5 %collective-permute-start = (bf16[512,1024]{1,0:T(8,128)(2,1)S(1)}, bf16[512,1024]{1,0:T(8,128)(2,1)S(1)}, u32[]{:S(2)}, u32[]{:S(2)}) collective-permute-start(bf16[512,1024]{1,0:T(8,128)(2,1)S(1)} %bitcast_multiply_fusion.own), channel_id=1, source_target_pairs={{0,1},{1,0},{2,3},{3,2},{4,5},{5,4},{6,7},{7,6},{8,9},{9,8},{10,11... | collective-permute-start | bytes 3145736 | tf_op jit(solution)/shard_map/ppermute | solution.py:172
  10.7 28.3 %collective-permute-start.8 = (bf16[1024,128]{1,0:T(8,128)(2,1)S(1)}, bf16[1024,128]{1,0:T(8,128)(2,1)S(1)}, u32[]{:S(2)}, u32[]{:S(2)}) collective-permute-start(bf16[1024,128]{1,0:T(8,128)(2,1)S(1)} %copy-done.16), channel_id=1, source_target_pairs={{1,32},{0,16},{17,33},{16,17},{3,34},{2,18},{19,35},{18,19},{5,36}... | collective-permute-start | bytes 786440 | tf_op jit(solution)/shard_map/ppermute | solution.py:168
  14.0 94.6 %copy-start.4 = (bf16[1024,128]{1,0:T(8,128)(2,1)}, bf16[1024,128]{1,0:T(8,128)(2,1)S(1)}, u32[]{:S(2)}) copy-start(bf16[1024,128]{1,0:T(8,128)(2,1)S(1)} %collective-permute-done.3.rest_0_) | copy-start | bytes 786436
  14.0 33.6 %collective-permute-start.4 = (bf16[1024,128]{1,0:T(8,128)(2,1)S(1)}, bf16[1024,128]{1,0:T(8,128)(2,1)S(1)}, u32[]{:S(2)}, u32[]{:S(2)}) collective-permute-start(bf16[1024,128]{1,0:T(8,128)(2,1)S(1)} %collective-permute-done.3.rest_0_), channel_id=1, source_target_pairs={{0,32},{16,496},{1,33},{17,497},{2,34},{18,498},{3,35},{19,499},{4... | collective-permute-start | bytes 786440 | tf_op jit(solution)/shard_map/ppermute | solution.py:168
  39.0 20.3 %copy-start.5 = (bf16[1024,128]{1,0:T(8,128)(2,1)}, bf16[1024,128]{1,0:T(8,128)(2,1)S(1)}, u32[]{:S(2)}) copy-start(bf16[1024,128]{1,0:T(8,128)(2,1)S(1)} %collective-permute-done.8.rest_3_) | copy-start | bytes 786436
  39.0 12.0 %collective-permute-start.9 = (bf16[1024,128]{1,0:T(8,128)(2,1)S(1)}, bf16[1024,128]{1,0:T(8,128)(2,1)S(1)}, u32[]{:S(2)}, u32[]{:S(2)}) collective-permute-start(bf16[1024,128]{1,0:T(8,128)(2,1)S(1)} %collective-permute-done.8.rest_3_), channel_id=1, source_target_pairs={{0,32},{16,496},{1,33},{17,497},{2,34},{18,498},{3,35},{19,499},{4... | collective-permute-start | bytes 786440 | tf_op jit(solution)/shard_map/ppermute | solution.py:168
  47.6 11.7 %copy-start.6 = (bf16[1024,128]{1,0:T(8,128)(2,1)}, bf16[1024,128]{1,0:T(8,128)(2,1)S(1)}, u32[]{:S(2)}) copy-start(bf16[1024,128]{1,0:T(8,128)(2,1)S(1)} %collective-permute-done.4.rest_1_) | copy-start | bytes 786436
  47.6 8.3 %collective-permute-start.5 = (bf16[1024,128]{1,0:T(8,128)(2,1)S(1)}, bf16[1024,128]{1,0:T(8,128)(2,1)S(1)}, u32[]{:S(2)}, u32[]{:S(2)}) collective-permute-start(bf16[1024,128]{1,0:T(8,128)(2,1)S(1)} %collective-permute-done.4.rest_1_), channel_id=1, source_target_pairs={{0,32},{16,496},{1,33},{17,497},{2,34},{18,498},{3,35},{19,499},{4... | collective-permute-start | bytes 786440 | tf_op jit(solution)/shard_map/ppermute | solution.py:168
  50.9 8.3 %copy-start.7 = (bf16[1024,128]{1,0:T(8,128)(2,1)}, bf16[1024,128]{1,0:T(8,128)(2,1)S(1)}, u32[]{:S(2)}) copy-start(bf16[1024,128]{1,0:T(8,128)(2,1)S(1)} %collective-permute-done.9.rest_4_) | copy-start | bytes 786436
  51.0 8.3 %collective-permute-start.10 = (bf16[1024,128]{1,0:T(8,128)(2,1)S(1)}, bf16[1024,128]{1,0:T(8,128)(2,1)S(1)}, u32[]{:S(2)}, u32[]{:S(2)}) collective-permute-start(bf16[1024,128]{1,0:T(8,128)(2,1)S(1)} %collective-permute-done.9.rest_4_), channel_id=1, source_target_pairs={{0,32},{16,496},{1,33},{17,497},{2,34},{18,498},{3,35},{19,499},{4... | collective-permute-start | bytes 786440 | tf_op jit(solution)/shard_map/ppermute | solution.py:168
  55.9 10.3 %copy-start.8 = (bf16[1024,128]{1,0:T(8,128)(2,1)}, bf16[1024,128]{1,0:T(8,128)(2,1)S(1)}, u32[]{:S(2)}) copy-start(bf16[1024,128]{1,0:T(8,128)(2,1)S(1)} %collective-permute-done.5.rest_2_) | copy-start | bytes 786436
  55.9 12.7 %collective-permute-start.6 = (bf16[1024,128]{1,0:T(8,128)(2,1)S(1)}, bf16[1024,128]{1,0:T(8,128)(2,1)S(1)}, u32[]{:S(2)}, u32[]{:S(2)}) collective-permute-start(bf16[1024,128]{1,0:T(8,128)(2,1)S(1)} %collective-permute-done.5.rest_2_), channel_id=1, source_target_pairs={{0,32},{16,496},{1,33},{17,497},{2,34},{18,498},{3,35},{19,499},{4... | collective-permute-start | bytes 786440 | tf_op jit(solution)/shard_map/ppermute | solution.py:168
  59.3 9.4 %copy-start.9 = (bf16[1024,128]{1,0:T(8,128)(2,1)}, bf16[1024,128]{1,0:T(8,128)(2,1)S(1)}, u32[]{:S(2)}) copy-start(bf16[1024,128]{1,0:T(8,128)(2,1)S(1)} %collective-permute-done.10.rest_5_) | copy-start | bytes 786436
  59.3 11.3 %collective-permute-start.11 = (bf16[1024,128]{1,0:T(8,128)(2,1)S(1)}, bf16[1024,128]{1,0:T(8,128)(2,1)S(1)}, u32[]{:S(2)}, u32[]{:S(2)}) collective-permute-start(bf16[1024,128]{1,0:T(8,128)(2,1)S(1)} %collective-permute-done.10.rest_5_), channel_id=1, source_target_pairs={{0,32},{16,496},{1,33},{17,497},{2,34},{18,498},{3,35},{19,499},{4... | collective-permute-start | bytes 786440 | tf_op jit(solution)/shard_map/ppermute | solution.py:168
  64.3 34.9 %collective-permute-start.1 = (bf16[512,1024]{1,0:T(8,128)(2,1)S(1)}, bf16[512,1024]{1,0:T(8,128)(2,1)S(1)}, u32[]{:S(2)}, u32[]{:S(2)}) collective-permute-start(bf16[512,1024]{1,0:T(8,128)(2,1)S(1)} %bitcast_multiply_fusion.own), channel_id=1, source_target_pairs={{0,16},{1,17},{2,18},{3,19},{4,20},{5,21},{6,22},{7,23},{8,24},{9,... | collective-permute-start | bytes 3145736 | tf_op jit(solution)/shard_map/ppermute | solution.py:173
  66.2 32.9 %copy-start.1 = (bf16[512,1024]{1,0:T(8,128)(2,1)}, bf16[512,1024]{1,0:T(8,128)(2,1)S(1)}, u32[]{:S(2)}) copy-start(bf16[512,1024]{1,0:T(8,128)(2,1)S(1)} %collective-permute-done.beside) | copy-start | bytes 3145732
  66.2 32.9 %collective-permute-start.2 = (bf16[512,1024]{1,0:T(8,128)(2,1)S(1)}, bf16[512,1024]{1,0:T(8,128)(2,1)}, u32[]{:S(2)}, u32[]{:S(2)}) collective-permute-start(bf16[512,1024]{1,0:T(8,128)(2,1)S(1)} %collective-permute-done.beside), channel_id=1, source_target_pairs={{0,16},{1,17},{2,18},{3,19},{4,20},{5,21},{6,22},{7,23},{8,24},{9,... | collective-permute-start | bytes 3145736 | tf_op jit(solution)/shard_map/ppermute | solution.py:174
  68.7 7.4 %collective-permute-start.7 = (bf16[1024,128]{1,0:T(8,128)(2,1)S(1)}, bf16[1024,128]{1,0:T(8,128)(2,1)S(1)}, u32[]{:S(2)}, u32[]{:S(2)}) collective-permute-start(bf16[1024,128]{1,0:T(8,128)(2,1)S(1)} %collective-permute-done.6.rest_0_), channel_id=1, source_target_pairs={{0,32},{16,496},{1,33},{17,497},{2,34},{18,498},{3,35},{19,499},{4... | collective-permute-start | bytes 786440 | tf_op jit(solution)/shard_map/ppermute | solution.py:168
  70.6 5.5 %copy-start.11 = (bf16[1024,128]{1,0:T(8,128)(2,1)}, bf16[1024,128]{1,0:T(8,128)(2,1)S(1)}, u32[]{:S(2)}) copy-start(bf16[1024,128]{1,0:T(8,128)(2,1)S(1)} %collective-permute-done.11.rest_2_) | copy-start | bytes 786436
  70.6 8.3 %collective-permute-start.12 = (bf16[1024,128]{1,0:T(8,128)(2,1)S(1)}, bf16[1024,128]{1,0:T(8,128)(2,1)S(1)}, u32[]{:S(2)}, u32[]{:S(2)}) collective-permute-start(bf16[1024,128]{1,0:T(8,128)(2,1)S(1)} %collective-permute-done.11.rest_2_), channel_id=1, source_target_pairs={{0,32},{16,496},{1,33},{17,497},{2,34},{18,498},{3,35},{19,499},{4... | collective-permute-start | bytes 786440 | tf_op jit(solution)/shard_map/ppermute | solution.py:168
  76.1 7.1 %collective-permute-start.13 = (bf16[1024,128]{1,0:T(8,128)(2,1)S(1)}, bf16[1024,128]{1,0:T(8,128)(2,1)S(1)}, u32[]{:S(2)}, u32[]{:S(2)}) collective-permute-start(bf16[1024,128]{1,0:T(8,128)(2,1)S(1)} %collective-permute-done.7.rest_1_), channel_id=1, source_target_pairs={{0,32},{16,496},{1,33},{17,497},{2,34},{18,498},{3,35},{19,499},{4... | collective-permute-start | bytes 786440 | tf_op jit(solution)/shard_map/ppermute | solution.py:168
  79.0 8.3 %collective-permute-start.16 = (bf16[1024,128]{1,0:T(8,128)(2,1)S(1)}, bf16[1024,128]{1,0:T(8,128)(2,1)S(1)}, u32[]{:S(2)}, u32[]{:S(2)}) collective-permute-start(bf16[1024,128]{1,0:T(8,128)(2,1)S(1)} %collective-permute-done.12.rest_3_), channel_id=1, source_target_pairs={{0,32},{16,496},{1,33},{17,497},{2,34},{18,498},{3,35},{19,499},{4... | collective-permute-start | bytes 786440 | tf_op jit(solution)/shard_map/ppermute | solution.py:168
  83.2 7.3 %collective-permute-start.14 = (bf16[1024,128]{1,0:T(8,128)(2,1)S(1)}, bf16[1024,128]{1,0:T(8,128)(2,1)}, u32[]{:S(2)}, u32[]{:S(2)}) collective-permute-start(bf16[1024,128]{1,0:T(8,128)(2,1)S(1)} %collective-permute-done.13.rest_0_), channel_id=1, source_target_pairs={{0,32},{16,496},{1,33},{17,497},{2,34},{18,498},{3,35},{19,499},{4... | collective-permute-start | bytes 786440 | tf_op jit(solution)/shard_map/ppermute | solution.py:168
  87.3 8.4 %collective-permute-start.17 = (bf16[1024,128]{1,0:T(8,128)(2,1)S(1)}, bf16[1024,128]{1,0:T(8,128)(2,1)}, u32[]{:S(2)}, u32[]{:S(2)}) collective-permute-start(bf16[1024,128]{1,0:T(8,128)(2,1)S(1)} %collective-permute-done.16.rest_2_), channel_id=1, source_target_pairs={{0,32},{16,496},{1,33},{17,497},{2,34},{18,498},{3,35},{19,499},{4... | collective-permute-start | bytes 786440 | tf_op jit(solution)/shard_map/ppermute | solution.py:168
  90.5 14.0 %collective-permute-start.15 = (bf16[1024,128]{1,0:T(8,128)(2,1)}, bf16[1024,128]{1,0:T(8,128)(2,1)}, u32[]{:S(2)}, u32[]{:S(2)}) collective-permute-start(bf16[1024,128]{1,0:T(8,128)(2,1)} %collective-permute-done.14.rest_1_), channel_id=1, source_target_pairs={{0,32},{16,496},{1,33},{17,497},{2,34},{18,498},{3,35},{19,499},{4... | collective-permute-start | bytes 786440 | tf_op jit(solution)/shard_map/ppermute | solution.py:168
  95.7 8.9 %collective-permute-start.18 = (bf16[1024,128]{1,0:T(8,128)(2,1)}, bf16[1024,128]{1,0:T(8,128)(2,1)}, u32[]{:S(2)}, u32[]{:S(2)}) collective-permute-start(bf16[1024,128]{1,0:T(8,128)(2,1)} %collective-permute-done.17.rest_3_), channel_id=1, source_target_pairs={{0,32},{16,496},{1,33},{17,497},{2,34},{18,498},{3,35},{19,499},{4... | collective-permute-start | bytes 786440 | tf_op jit(solution)/shard_map/ppermute | solution.py:168
  108.6 26.7 %all-to-all-start.1 = ((bf16[32,32,384]{2,1,0:T(8,128)(2,1)}), bf16[32,32,384]{2,1,0:T(8,128)(2,1)S(1)}, u32[]{:S(2)}, u32[]{:S(2)}) async-start(bf16[32,32,384]{2,1,0:T(8,128)(2,1)} %bitcast.30), calls=%async_computation.1 | async-start | bytes 1572864 | tf_op jit(solution)/shard_map/all_to_all | solution.py:187
  135.4 5.1 %copy-start.17 = (s32[32]{0:T(128)S(1)}, s32[32]{0:T(128)}, u32[]{:S(2)}) copy-start(s32[32]{0:T(128)} %param.9) | copy-start | bytes 388
  135.4 24.4 %all-to-all-start = ((bf16[32,32,640]{2,1,0:T(8,128)(2,1)}), bf16[32,32,640]{2,1,0:T(8,128)(2,1)S(1)}, u32[]{:S(2)}, u32[]{:S(2)}) async-start(bf16[32,32,640]{2,1,0:T(8,128)(2,1)} %bitcast.29), calls=%async_computation | async-start | bytes 2621440 | tf_op jit(solution)/shard_map/all_to_all | solution.py:187
  (7 other events, 19.5 us)

commit v4 on v3

--- a/solution.py
+++ b/solution.py
@@ -7,6 +7,7 @@
 
 
 TILE = 128
+KERNEL_VMEM = 16 << 20
 
 
 def mask_tiles(matrix, occupancy):
@@ -72,76 +73,47 @@
         body,
         in_specs=[pl.BlockSpec(memory_space=pltpu.SMEM), pl.BlockSpec(memory_space=pltpu.VMEM)],
         out_specs=pl.BlockSpec(memory_space=pltpu.VMEM),
-        out_shape=jax.ShapeDtypeStruct(integrals.shape, jnp.bfloat16),
+        out_shape=pltpu.VMEM(integrals.shape, jnp.bfloat16),
+        compiler_params=pltpu.CompilerParams(vmem_limit_bytes=KERNEL_VMEM),
         name="masked_tile",
     )(occupancy.reshape(-1), integrals)
 
 
-def multiply(choice, blocks, tiles, start, width, previous):
+def multiply(blocks, tiles, start, width, previous):
     nrow, kloc = blocks[0].shape
     count = len(tiles[0])
     part = count * TILE
-    step = nrow // 2
-    steps = nrow // step
 
-    def body(choice_ref, own, beside, own_other, beside_other, *rest):
+    def body(own, beside, own_other, beside_other, *rest):
         tile_refs = rest[: 2 * count]
-        out, right, total, sem = rest[-4:]
-        m = pl.program_id(0)
-        stream, core = choice_ref[0], choice_ref[1]
+        out, right = rest[-2:]
+        core = lax.axis_index("core")
+        stream = (lax.axis_index("col") + core) % 2
+        for i in range(2 * count):
+            right[i // count, :, (i % count) * TILE : (i % count + 1) * TILE] = tile_refs[i][...]
+        for side, near, far in ((core, own, beside), (1 - core, own_other, beside_other)):
+            for first in range(0, part, 2 * TILE):
+                last = min(first + 2 * TILE, part)
+                value = jnp.dot(near[...], right[stream, :, first:last], preferred_element_type=jnp.float32)
+                value += jnp.dot(far[...], right[1 - stream, :, first:last], preferred_element_type=jnp.float32)
+                out[side, :, start + first : start + last] = value.astype(jnp.bfloat16)
 
-        def copy_out(at, half):
-            side = core if half == 0 else 1 - core
-            target = out.at[side, pl.ds(at * step, step), pl.ds(start, part)]
-            return pltpu.make_async_copy(total.at[at, half], target, sem.at[at, half])
-
-        @pl.when(m == 0)
-        def _():
-            for i in range(2 * count):
-                right[i // count, :, (i % count) * TILE : (i % count + 1) * TILE] = tile_refs[i][...]
-
-        near = jnp.concatenate([own[...], own_other[...]], 0)
-        far = jnp.concatenate([beside[...], beside_other[...]], 0)
-        for first in range(0, part, 2 * TILE):
-            cols = slice(first, min(first + 2 * TILE, part))
-            value = jnp.dot(near, right[stream, :, cols], preferred_element_type=jnp.float32)
-            value += jnp.dot(far, right[1 - stream, :, cols], preferred_element_type=jnp.float32)
-            value = value.astype(jnp.bfloat16)
-            total[m, 0, :, cols] = value[:step]
-            total[m, 1, :, cols] = value[step:]
-        for half in (0, 1):
-            copy_out(m, half).start()
-
-        @pl.when(m == steps - 1)
-        def _():
-            for at in range(steps):
-                for half in (0, 1):
-                    copy_out(at, half).wait()
-
-    left = pl.BlockSpec((step, kloc), lambda m: (m, 0))
-    whole = pl.BlockSpec((kloc, TILE), lambda m: (0, 0))
-    anywhere = pl.BlockSpec(memory_space=pl.ANY)
-    operands = [choice, *blocks, *tiles[0], *tiles[1]]
-    specs = [pl.BlockSpec(memory_space=pltpu.SMEM)] + [left] * 4 + [whole] * (2 * count)
+    vmem = pl.BlockSpec(memory_space=pltpu.VMEM)
+    operands = [*blocks, *tiles[0], *tiles[1]]
     aliases = {}
     if previous is not None:
         aliases = {len(operands): 0}
         operands.append(previous)
-        specs.append(anywhere)
     return pl.pallas_call(
         body,
-        grid=(steps,),
-        in_specs=specs,
-        out_specs=anywhere,
-        out_shape=jax.ShapeDtypeStruct((2, nrow, width), jnp.bfloat16),
-        scratch_shapes=[
-            pltpu.VMEM((2, kloc, part), jnp.bfloat16),
-            pltpu.VMEM((steps, 2, step, part), jnp.bfloat16),
-            pltpu.SemaphoreType.DMA((steps, 2)),
-        ],
+        in_specs=[vmem] * len(operands),
+        out_specs=vmem,
+        out_shape=pltpu.VMEM((2, nrow, width), jnp.bfloat16),
+        scratch_shapes=[pltpu.VMEM((2, kloc, part), jnp.bfloat16)],
         input_output_aliases=aliases,
+        compiler_params=pltpu.CompilerParams(vmem_limit_bytes=KERNEL_VMEM),
         name="multiply",
-    )(*operands)
+    )(*[pltpu.with_memory_space_constraint(o, pltpu.VMEM) for o in operands])
 
 
 def make(nz, ncol):
@@ -151,8 +123,6 @@
 
     def on_device(amplitudes, integrals, amp_occupancy, int_occupancy, owner_map):
         z = lax.axis_index("z")
-        core = lax.axis_index("core")
-        odd = lax.axis_index("col") % 2
         own_tile = masked_tile(integrals, int_occupancy)
         nrow, _ = amplitudes.shape
         part = nrow // ncol
@@ -173,10 +143,9 @@
                 own_other = lax.ppermute(own, every, swap_pairs(nz, ncol, 1, 0))
                 beside_other = lax.ppermute(beside, every, swap_pairs(nz, ncol, 1, 0))
                 blocks = (own, beside, own_other, beside_other)
-                choice = jnp.stack([odd ^ core, core]).astype(jnp.int32)
             if slot == ends[call][0]:
                 _, _, count, begin, width = ends[call]
-                product = multiply(choice, blocks, tiles, begin * TILE, width * TILE, product)
+                product = multiply(blocks, tiles, begin * TILE, width * TILE, product)
                 tiles = [[], []]
                 call += 1
                 if begin + count < width:

time: 173 us -> 172 us (level)
  local copies, waits for them, and re-layouts: 2.71 us -> 17.5 us
  Pallas kernels: 20.5 us -> 6.95 us
  waiting for transfers between devices: 44.1 us -> 39.7 us
    unnamed x38 -> x54, local copies, waits for them, and re-layouts: 1.8 us -> 16.6 us
    pallas_call x4, Pallas kernels: 18.7 us -> 6.37 us  [multiply(): pl.pallas_call(body, in_specs=[vmem] * len(operands), out_specs=vmem, out...]
    ppermute x16, waiting for transfers between devices: 21.6 us -> 18.9 us  [on_device(): current[stream] = lax.ppermute(current[stream], every, pairs)]
  transfers between devices with their start and end apart: 21 -> 21, of which waited for: 6 -> 4; matrix products, arithmetic and copies ran while one was open for 1% -> 1% of each run, Pallas kernels for 9% -> 3%
where the time goes in v4:
time: 172 us; the launch traced here: 171 us
  starting transfers between devices  93 us (54%)
  waiting for transfers between devices  39.7 us (23%)
  local copies, waits for them, and re-layouts  17.5 us (10%)
  blocking collectives  10.9 us (6%)
  Pallas kernels  6.95 us (4%)
  other arithmetic  2.33 us (1%)
    ppermute x16, starting transfers between devices, on_device(): current[stream] = lax.ppermute(current[stream], every, pairs)  67.8 us
    all_to_all x2, waiting for transfers between devices, on_device(): moved = lax.all_to_all(moved, ('core', 'col'), 0, 0, tiled=True)  20.8 us
    all_to_all x2, starting transfers between devices, on_device(): moved = lax.all_to_all(moved, ('core', 'col'), 0, 0, tiled=True)  19 us
    ppermute x16, waiting for transfers between devices, on_device(): current[stream] = lax.ppermute(current[stream], every, pairs)  18.9 us
    unnamed x54, local copies, waits for them, and re-layouts  16.6 us
    all_to_all x1, blocking collectives, on_device(): final = lax.all_to_all(picked, 'col', 0, 0, tiled=True)  10.9 us
    pallas_call x4, Pallas kernels, multiply(): pl.pallas_call(body, in_specs=[vmem] * len(operands), out_specs=vmem, out...  6.37 us
  transfers between devices with their start and end apart: 21, of which 4 were waited for; matrix products, arithmetic and copies ran while one was open for 1% of the time, Pallas kernels for 3%

profile of v4, /device:TPU:1, one launch (start us, length us, event | category | flops | bytes accessed | tf_op | source)
XLA Modules:
  0.0 171.0 jit_solution(9646772896164733931)
XLA Ops:
  2.2 5.9 %collective-permute-start.3 = (bf16[1024,128]{1,0:T(8,128)(2,1)S(1)}, bf16[1024,128]{1,0:T(8,128)(2,1)S(1)}, u32[]{:S(2)}, u32[]{:S(2)}) collective-permute-start(bf16[1024,128]{1,0:T(8,128)(2,1)S(1)} %masked_tile.1), channel_id=1, source_target_pairs={{0,32},{1,16},{16,33},{17,17},{2,34},{3,18},{18,35},{19,19},{4,36}... | collective-permute-start | bytes 786440 | tf_op jit(solution)/shard_map/ppermute | solution.py:138
  9.1 1.9 %collective-permute-start = (bf16[512,1024]{1,0:T(8,128)(2,1)S(1)}, bf16[512,1024]{1,0:T(8,128)(2,1)S(1)}, u32[]{:S(2)}, u32[]{:S(2)}) collective-permute-start(bf16[512,1024]{1,0:T(8,128)(2,1)S(1)} %bitcast_multiply_fusion.own), channel_id=1, source_target_pairs={{0,1},{1,0},{2,3},{3,2},{4,5},{5,4},{6,7},{7,6},{8,9},{9,8},{10,11... | collective-permute-start | bytes 3145736 | tf_op jit(solution)/shard_map/ppermute | solution.py:142
  11.0 3.4 %collective-permute-start.8 = (bf16[1024,128]{1,0:T(8,128)(2,1)S(1)}, bf16[1024,128]{1,0:T(8,128)(2,1)S(1)}, u32[]{:S(2)}, u32[]{:S(2)}) collective-permute-start(bf16[1024,128]{1,0:T(8,128)(2,1)S(1)} %masked_tile.1), channel_id=1, source_target_pairs={{1,32},{0,16},{17,33},{16,17},{3,34},{2,18},{19,35},{18,19},{5,36}... | collective-permute-start | bytes 786440 | tf_op jit(solution)/shard_map/ppermute | solution.py:138
  14.4 8.2 %collective-permute-start.4 = (bf16[1024,128]{1,0:T(8,128)(2,1)S(1)}, bf16[1024,128]{1,0:T(8,128)(2,1)S(1)}, u32[]{:S(2)}, u32[]{:S(2)}) collective-permute-start(bf16[1024,128]{1,0:T(8,128)(2,1)S(1)} %collective-permute-done.3.rest_0_), channel_id=1, source_target_pairs={{0,32},{16,496},{1,33},{17,497},{2,34},{18,498},{3,35},{19,499},{4... | collective-permute-start | bytes 786440 | tf_op jit(solution)/shard_map/ppermute | solution.py:138
  22.6 16.9 %collective-permute-done.8.rest_3_ = bf16[1024,128]{1,0:T(8,128)(2,1)S(1)} collective-permute-done((bf16[1024,128]{1,0:T(8,128)(2,1)S(1)}, bf16[1024,128]{1,0:T(8,128)(2,1)S(1)}, u32[]{:S(2)}, u32[]{:S(2)}) %collective-permute-start.8) | collective-permute-done | bytes 262176 | tf_op jit(solution)/shard_map/ppermute | solution.py:138
  39.5 8.0 %collective-permute-start.9 = (bf16[1024,128]{1,0:T(8,128)(2,1)S(1)}, bf16[1024,128]{1,0:T(8,128)(2,1)S(1)}, u32[]{:S(2)}, u32[]{:S(2)}) collective-permute-start(bf16[1024,128]{1,0:T(8,128)(2,1)S(1)} %collective-permute-done.8.rest_3_), channel_id=1, source_target_pairs={{0,32},{16,496},{1,33},{17,497},{2,34},{18,498},{3,35},{19,499},{4... | collective-permute-start | bytes 786440 | tf_op jit(solution)/shard_map/ppermute | solution.py:138
  48.2 3.7 %collective-permute-start.5 = (bf16[1024,128]{1,0:T(8,128)(2,1)S(1)}, bf16[1024,128]{1,0:T(8,128)(2,1)S(1)}, u32[]{:S(2)}, u32[]{:S(2)}) collective-permute-start(bf16[1024,128]{1,0:T(8,128)(2,1)S(1)} %collective-permute-done.4.rest_1_), channel_id=1, source_target_pairs={{0,32},{16,496},{1,33},{17,497},{2,34},{18,498},{3,35},{19,499},{4... | collective-permute-start | bytes 786440 | tf_op jit(solution)/shard_map/ppermute | solution.py:138
  52.6 3.2 %collective-permute-start.10 = (bf16[1024,128]{1,0:T(8,128)(2,1)S(1)}, bf16[1024,128]{1,0:T(8,128)(2,1)S(1)}, u32[]{:S(2)}, u32[]{:S(2)}) collective-permute-start(bf16[1024,128]{1,0:T(8,128)(2,1)S(1)} %collective-permute-done.9.rest_4_), channel_id=1, source_target_pairs={{0,32},{16,496},{1,33},{17,497},{2,34},{18,498},{3,35},{19,499},{4... | collective-permute-start | bytes 786440 | tf_op jit(solution)/shard_map/ppermute | solution.py:138
  56.5 3.7 %collective-permute-start.6 = (bf16[1024,128]{1,0:T(8,128)(2,1)S(1)}, bf16[1024,128]{1,0:T(8,128)(2,1)S(1)}, u32[]{:S(2)}, u32[]{:S(2)}) collective-permute-start(bf16[1024,128]{1,0:T(8,128)(2,1)S(1)} %collective-permute-done.5.rest_2_), channel_id=1, source_target_pairs={{0,32},{16,496},{1,33},{17,497},{2,34},{18,498},{3,35},{19,499},{4... | collective-permute-start | bytes 786440 | tf_op jit(solution)/shard_map/ppermute | solution.py:138
  60.9 3.1 %collective-permute-start.11 = (bf16[1024,128]{1,0:T(8,128)(2,1)S(1)}, bf16[1024,128]{1,0:T(8,128)(2,1)S(1)}, u32[]{:S(2)}, u32[]{:S(2)}) collective-permute-start(bf16[1024,128]{1,0:T(8,128)(2,1)S(1)} %collective-permute-done.10.rest_5_), channel_id=1, source_target_pairs={{0,32},{16,496},{1,33},{17,497},{2,34},{18,498},{3,35},{19,499},{4... | collective-permute-start | bytes 786440 | tf_op jit(solution)/shard_map/ppermute | solution.py:138
  64.8 1.9 %collective-permute-start.1 = (bf16[512,1024]{1,0:T(8,128)(2,1)S(1)}, bf16[512,1024]{1,0:T(8,128)(2,1)S(1)}, u32[]{:S(2)}, u32[]{:S(2)}) collective-permute-start(bf16[512,1024]{1,0:T(8,128)(2,1)S(1)} %bitcast_multiply_fusion.own), channel_id=1, source_target_pairs={{0,16},{1,17},{2,18},{3,19},{4,20},{5,21},{6,22},{7,23},{8,24},{9,... | collective-permute-start | bytes 3145736 | tf_op jit(solution)/shard_map/ppermute | solution.py:143
  66.7 2.4 %collective-permute-start.2 = (bf16[512,1024]{1,0:T(8,128)(2,1)S(1)}, bf16[512,1024]{1,0:T(8,128)(2,1)S(1)}, u32[]{:S(2)}, u32[]{:S(2)}) collective-permute-start(bf16[512,1024]{1,0:T(8,128)(2,1)S(1)} %collective-permute-done.beside), channel_id=1, source_target_pairs={{0,16},{1,17},{2,18},{3,19},{4,20},{5,21},{6,22},{7,23},{8,24},{9,... | collective-permute-start | bytes 3145736 | tf_op jit(solution)/shard_map/ppermute | solution.py:144
  69.1 1.9 %collective-permute-start.7 = (bf16[1024,128]{1,0:T(8,128)(2,1)S(1)}, bf16[1024,128]{1,0:T(8,128)(2,1)S(1)}, u32[]{:S(2)}, u32[]{:S(2)}) collective-permute-start(bf16[1024,128]{1,0:T(8,128)(2,1)S(1)} %collective-permute-done.6.rest_0_), channel_id=1, source_target_pairs={{0,32},{16,496},{1,33},{17,497},{2,34},{18,498},{3,35},{19,499},{4... | collective-permute-start | bytes 786440 | tf_op jit(solution)/shard_map/ppermute | solution.py:138
  71.8 4.0 %collective-permute-start.12 = (bf16[1024,128]{1,0:T(8,128)(2,1)S(1)}, bf16[1024,128]{1,0:T(8,128)(2,1)S(1)}, u32[]{:S(2)}, u32[]{:S(2)}) collective-permute-start(bf16[1024,128]{1,0:T(8,128)(2,1)S(1)} %collective-permute-done.11.rest_2_), channel_id=1, source_target_pairs={{0,32},{16,496},{1,33},{17,497},{2,34},{18,498},{3,35},{19,499},{4... | collective-permute-start | bytes 786440 | tf_op jit(solution)/shard_map/ppermute | solution.py:138
  76.6 2.8 %collective-permute-start.13 = (bf16[1024,128]{1,0:T(8,128)(2,1)S(1)}, bf16[1024,128]{1,0:T(8,128)(2,1)S(1)}, u32[]{:S(2)}, u32[]{:S(2)}) collective-permute-start(bf16[1024,128]{1,0:T(8,128)(2,1)S(1)} %collective-permute-done.7.rest_1_), channel_id=1, source_target_pairs={{0,32},{16,496},{1,33},{17,497},{2,34},{18,498},{3,35},{19,499},{4... | collective-permute-start | bytes 786440 | tf_op jit(solution)/shard_map/ppermute | solution.py:138
  80.1 4.0 %collective-permute-start.16 = (bf16[1024,128]{1,0:T(8,128)(2,1)S(1)}, bf16[1024,128]{1,0:T(8,128)(2,1)S(1)}, u32[]{:S(2)}, u32[]{:S(2)}) collective-permute-start(bf16[1024,128]{1,0:T(8,128)(2,1)S(1)} %collective-permute-done.12.rest_3_), channel_id=1, source_target_pairs={{0,32},{16,496},{1,33},{17,497},{2,34},{18,498},{3,35},{19,499},{4... | collective-permute-start | bytes 786440 | tf_op jit(solution)/shard_map/ppermute | solution.py:138
  84.9 2.8 %collective-permute-start.14 = (bf16[1024,128]{1,0:T(8,128)(2,1)S(1)}, bf16[1024,128]{1,0:T(8,128)(2,1)S(1)}, u32[]{:S(2)}, u32[]{:S(2)}) collective-permute-start(bf16[1024,128]{1,0:T(8,128)(2,1)S(1)} %collective-permute-done.13.rest_0_), channel_id=1, source_target_pairs={{0,32},{16,496},{1,33},{17,497},{2,34},{18,498},{3,35},{19,499},{4... | collective-permute-start | bytes 786440 | tf_op jit(solution)/shard_map/ppermute | solution.py:138
  87.7 4.7 %collective-permute-start.17 = (bf16[1024,128]{1,0:T(8,128)(2,1)S(1)}, bf16[1024,128]{1,0:T(8,128)(2,1)S(1)}, u32[]{:S(2)}, u32[]{:S(2)}) collective-permute-start(bf16[1024,128]{1,0:T(8,128)(2,1)S(1)} %collective-permute-done.16.rest_2_), channel_id=1, source_target_pairs={{0,32},{16,496},{1,33},{17,497},{2,34},{18,498},{3,35},{19,499},{4... | collective-permute-start | bytes 786440 | tf_op jit(solution)/shard_map/ppermute | solution.py:138
  92.5 3.5 %collective-permute-start.15 = (bf16[1024,128]{1,0:T(8,128)(2,1)S(1)}, bf16[1024,128]{1,0:T(8,128)(2,1)S(1)}, u32[]{:S(2)}, u32[]{:S(2)}) collective-permute-start(bf16[1024,128]{1,0:T(8,128)(2,1)S(1)} %collective-permute-done.14.rest_1_), channel_id=1, source_target_pairs={{0,32},{16,496},{1,33},{17,497},{2,34},{18,498},{3,35},{19,499},{4... | collective-permute-start | bytes 786440 | tf_op jit(solution)/shard_map/ppermute | solution.py:138
  96.0 4.7 %collective-permute-start.18 = (bf16[1024,128]{1,0:T(8,128)(2,1)S(1)}, bf16[1024,128]{1,0:T(8,128)(2,1)S(1)}, u32[]{:S(2)}, u32[]{:S(2)}) collective-permute-start(bf16[1024,128]{1,0:T(8,128)(2,1)S(1)} %collective-permute-done.17.rest_3_), channel_id=1, source_target_pairs={{0,32},{16,496},{1,33},{17,497},{2,34},{18,498},{3,35},{19,499},{4... | collective-permute-start | bytes 786440 | tf_op jit(solution)/shard_map/ppermute | solution.py:138
  100.8 1.3 multiply.6.rest_2_
  102.1 1.9 %collective-permute-done.18.rest_1_ = bf16[1024,128]{1,0:T(8,128)(2,1)S(1)} collective-permute-done((bf16[1024,128]{1,0:T(8,128)(2,1)S(1)}, bf16[1024,128]{1,0:T(8,128)(2,1)S(1)}, u32[]{:S(2)}, u32[]{:S(2)}) %collective-permute-start.18) | collective-permute-done | bytes 262176 | tf_op jit(solution)/shard_map/ppermute | solution.py:138
  104.1 1.3 multiply.7
  106.3 13.9 %all-to-all-start.1 = ((bf16[32,32,384]{2,1,0:T(8,128)(2,1)}), bf16[32,32,384]{2,1,0:T(8,128)(2,1)}, u32[]{:S(2)}, u32[]{:S(2)}) async-start(bf16[32,32,384]{2,1,0:T(8,128)(2,1)} %bitcast.28), calls=%async_computation.1 | async-start | bytes 1572864 | tf_op jit(solution)/shard_map/all_to_all | solution.py:156
  120.2 1.2 copy-done.1
  126.2 2.5 %multiply.4.rest_4_ = bf16[2,512,640]{2,1,0:T(8,128)(2,1)S(1)} custom-call(bf16[512,1024]{1,0:T(8,128)(2,1)S(1)} %bitcast_multiply_fusion.own, bf16[512,1024]{1,0:T(8,128)(2,1)S(1)} %collective-permute-done.beside, bf16[512,1024]{1,0:T(8,128)(2,1)S(1)} %collective-permute-done.1.own_other, bf16[512,1024]{1,0:T(8,128)(2,1)S(1)} %copy-done.1, ...), custom_call_target="tpu_custom_call" | custom-call | tf_op jit(solution)/shard_map/multiply/pallas_call | solution.py:107
  128.7 1.3 multiply.5
  131.1 2.8 %all-to-all-done.1 = bf16[32,32,384]{2,1,0:T(8,128)(2,1)} async-done(((bf16[32,32,384]{2,1,0:T(8,128)(2,1)}), bf16[32,32,384]{2,1,0:T(8,128)(2,1)}, u32[]{:S(2)}, u32[]{:S(2)}) %all-to-all-start.1) | async-done | bytes 786464 | tf_op jit(solution)/shard_map/all_to_all | solution.py:156
  133.9 5.1 %all-to-all-start = ((bf16[32,32,640]{2,1,0:T(8,128)(2,1)}), bf16[32,32,640]{2,1,0:T(8,128)(2,1)S(1)}, u32[]{:S(2)}, u32[]{:S(2)}) async-start(bf16[32,32,640]{2,1,0:T(8,128)(2,1)} %bitcast.27), calls=%async_computation | async-start | bytes 2621440 | tf_op jit(solution)/shard_map/all_to_all | solution.py:156
  139.1 1.2 reduce_sum.25
  140.3 18.0 %all-to-all-done = bf16[32,32,640]{2,1,0:T(8,128)(2,1)S(1)} async-done(((bf16[32,32,640]{2,1,0:T(8,128)(2,1)}), bf16[32,32,640]{2,1,0:T(8,128)(2,1)S(1)}, u32[]{:S(2)}, u32[]{:S(2)}) %all-to-all-start) | async-done | bytes 1310752 | tf_op jit(solution)/shard_map/all_to_all | solution.py:156
  159.4 10.9 %all_to_all.15 = bf16[16,32,256]{2,1,0:T(8,128)(2,1)S(1)} all-to-all(bf16[16,32,256]{2,1,0:T(8,128)(2,1)S(1)} %bitcast.36), channel_id=1, replica_groups=mesh['z'=16,'core'=2,'col'=16] {'col'}, dimensions={0} | all-to-all | bytes 524288 | tf_op jit(solution)/shard_map/all_to_all | solution.py:170
  (82 shorter events, 18.0 us)
Async XLA Ops:
  0.0 0.9 copy-start.22
  1.6 7.4 %copy-start.24 = (bf16[512,1024]{1,0:T(8,128)(2,1)S(1)}, bf16[512,1024]{1,0:T(8,128)(2,1)}, u32[]{:S(2)}) copy-start(bf16[512,1024]{1,0:T(8,128)(2,1)} %param.5) | copy-start | bytes 3145732
  2.2 12.2 %collective-permute-start.3 = (bf16[1024,128]{1,0:T(8,128)(2,1)S(1)}, bf16[1024,128]{1,0:T(8,128)(2,1)S(1)}, u32[]{:S(2)}, u32[]{:S(2)}) collective-permute-start(bf16[1024,128]{1,0:T(8,128)(2,1)S(1)} %masked_tile.1), channel_id=1, source_target_pairs={{0,32},{1,16},{16,33},{17,17},{2,34},{3,18},{18,35},{19,19},{4,36}... | collective-permute-start | bytes 786440 | tf_op jit(solution)/shard_map/ppermute | solution.py:138
  9.1 57.6 %collective-permute-start = (bf16[512,1024]{1,0:T(8,128)(2,1)S(1)}, bf16[512,1024]{1,0:T(8,128)(2,1)S(1)}, u32[]{:S(2)}, u32[]{:S(2)}) collective-permute-start(bf16[512,1024]{1,0:T(8,128)(2,1)S(1)} %bitcast_multiply_fusion.own), channel_id=1, source_target_pairs={{0,1},{1,0},{2,3},{3,2},{4,5},{5,4},{6,7},{7,6},{8,9},{9,8},{10,11... | collective-permute-start | bytes 3145736 | tf_op jit(solution)/shard_map/ppermute | solution.py:142
  11.0 28.4 %collective-permute-start.8 = (bf16[1024,128]{1,0:T(8,128)(2,1)S(1)}, bf16[1024,128]{1,0:T(8,128)(2,1)S(1)}, u32[]{:S(2)}, u32[]{:S(2)}) collective-permute-start(bf16[1024,128]{1,0:T(8,128)(2,1)S(1)} %masked_tile.1), channel_id=1, source_target_pairs={{1,32},{0,16},{17,33},{16,17},{3,34},{2,18},{19,35},{18,19},{5,36}... | collective-permute-start | bytes 786440 | tf_op jit(solution)/shard_map/ppermute | solution.py:138
  14.4 33.7 %collective-permute-start.4 = (bf16[1024,128]{1,0:T(8,128)(2,1)S(1)}, bf16[1024,128]{1,0:T(8,128)(2,1)S(1)}, u32[]{:S(2)}, u32[]{:S(2)}) collective-permute-start(bf16[1024,128]{1,0:T(8,128)(2,1)S(1)} %collective-permute-done.3.rest_0_), channel_id=1, source_target_pairs={{0,32},{16,496},{1,33},{17,497},{2,34},{18,498},{3,35},{19,499},{4... | collective-permute-start | bytes 786440 | tf_op jit(solution)/shard_map/ppermute | solution.py:138
  39.5 13.1 %collective-permute-start.9 = (bf16[1024,128]{1,0:T(8,128)(2,1)S(1)}, bf16[1024,128]{1,0:T(8,128)(2,1)S(1)}, u32[]{:S(2)}, u32[]{:S(2)}) collective-permute-start(bf16[1024,128]{1,0:T(8,128)(2,1)S(1)} %collective-permute-done.8.rest_3_), channel_id=1, source_target_pairs={{0,32},{16,496},{1,33},{17,497},{2,34},{18,498},{3,35},{19,499},{4... | collective-permute-start | bytes 786440 | tf_op jit(solution)/shard_map/ppermute | solution.py:138
  48.2 8.3 %collective-permute-start.5 = (bf16[1024,128]{1,0:T(8,128)(2,1)S(1)}, bf16[1024,128]{1,0:T(8,128)(2,1)S(1)}, u32[]{:S(2)}, u32[]{:S(2)}) collective-permute-start(bf16[1024,128]{1,0:T(8,128)(2,1)S(1)} %collective-permute-done.4.rest_1_), channel_id=1, source_target_pairs={{0,32},{16,496},{1,33},{17,497},{2,34},{18,498},{3,35},{19,499},{4... | collective-permute-start | bytes 786440 | tf_op jit(solution)/shard_map/ppermute | solution.py:138
  52.6 8.3 %collective-permute-start.10 = (bf16[1024,128]{1,0:T(8,128)(2,1)S(1)}, bf16[1024,128]{1,0:T(8,128)(2,1)S(1)}, u32[]{:S(2)}, u32[]{:S(2)}) collective-permute-start(bf16[1024,128]{1,0:T(8,128)(2,1)S(1)} %collective-permute-done.9.rest_4_), channel_id=1, source_target_pairs={{0,32},{16,496},{1,33},{17,497},{2,34},{18,498},{3,35},{19,499},{4... | collective-permute-start | bytes 786440 | tf_op jit(solution)/shard_map/ppermute | solution.py:138
  56.5 12.6 %collective-permute-start.6 = (bf16[1024,128]{1,0:T(8,128)(2,1)S(1)}, bf16[1024,128]{1,0:T(8,128)(2,1)S(1)}, u32[]{:S(2)}, u32[]{:S(2)}) collective-permute-start(bf16[1024,128]{1,0:T(8,128)(2,1)S(1)} %collective-permute-done.5.rest_2_), channel_id=1, source_target_pairs={{0,32},{16,496},{1,33},{17,497},{2,34},{18,498},{3,35},{19,499},{4... | collective-permute-start | bytes 786440 | tf_op jit(solution)/shard_map/ppermute | solution.py:138
  60.9 10.8 %collective-permute-start.11 = (bf16[1024,128]{1,0:T(8,128)(2,1)S(1)}, bf16[1024,128]{1,0:T(8,128)(2,1)S(1)}, u32[]{:S(2)}, u32[]{:S(2)}) collective-permute-start(bf16[1024,128]{1,0:T(8,128)(2,1)S(1)} %collective-permute-done.10.rest_5_), channel_id=1, source_target_pairs={{0,32},{16,496},{1,33},{17,497},{2,34},{18,498},{3,35},{19,499},{4... | collective-permute-start | bytes 786440 | tf_op jit(solution)/shard_map/ppermute | solution.py:138
  64.8 36.0 %collective-permute-start.1 = (bf16[512,1024]{1,0:T(8,128)(2,1)S(1)}, bf16[512,1024]{1,0:T(8,128)(2,1)S(1)}, u32[]{:S(2)}, u32[]{:S(2)}) collective-permute-start(bf16[512,1024]{1,0:T(8,128)(2,1)S(1)} %bitcast_multiply_fusion.own), channel_id=1, source_target_pairs={{0,16},{1,17},{2,18},{3,19},{4,20},{5,21},{6,22},{7,23},{8,24},{9,... | collective-permute-start | bytes 3145736 | tf_op jit(solution)/shard_map/ppermute | solution.py:143
  66.7 34.1 %collective-permute-start.2 = (bf16[512,1024]{1,0:T(8,128)(2,1)S(1)}, bf16[512,1024]{1,0:T(8,128)(2,1)S(1)}, u32[]{:S(2)}, u32[]{:S(2)}) collective-permute-start(bf16[512,1024]{1,0:T(8,128)(2,1)S(1)} %collective-permute-done.beside), channel_id=1, source_target_pairs={{0,16},{1,17},{2,18},{3,19},{4,20},{5,21},{6,22},{7,23},{8,24},{9,... | collective-permute-start | bytes 3145736 | tf_op jit(solution)/shard_map/ppermute | solution.py:144
  69.1 7.4 %collective-permute-start.7 = (bf16[1024,128]{1,0:T(8,128)(2,1)S(1)}, bf16[1024,128]{1,0:T(8,128)(2,1)S(1)}, u32[]{:S(2)}, u32[]{:S(2)}) collective-permute-start(bf16[1024,128]{1,0:T(8,128)(2,1)S(1)} %collective-permute-done.6.rest_0_), channel_id=1, source_target_pairs={{0,32},{16,496},{1,33},{17,497},{2,34},{18,498},{3,35},{19,499},{4... | collective-permute-start | bytes 786440 | tf_op jit(solution)/shard_map/ppermute | solution.py:138
  71.8 8.3 %collective-permute-start.12 = (bf16[1024,128]{1,0:T(8,128)(2,1)S(1)}, bf16[1024,128]{1,0:T(8,128)(2,1)S(1)}, u32[]{:S(2)}, u32[]{:S(2)}) collective-permute-start(bf16[1024,128]{1,0:T(8,128)(2,1)S(1)} %collective-permute-done.11.rest_2_), channel_id=1, source_target_pairs={{0,32},{16,496},{1,33},{17,497},{2,34},{18,498},{3,35},{19,499},{4... | collective-permute-start | bytes 786440 | tf_op jit(solution)/shard_map/ppermute | solution.py:138
  76.6 8.3 %collective-permute-start.13 = (bf16[1024,128]{1,0:T(8,128)(2,1)S(1)}, bf16[1024,128]{1,0:T(8,128)(2,1)S(1)}, u32[]{:S(2)}, u32[]{:S(2)}) collective-permute-start(bf16[1024,128]{1,0:T(8,128)(2,1)S(1)} %collective-permute-done.7.rest_1_), channel_id=1, source_target_pairs={{0,32},{16,496},{1,33},{17,497},{2,34},{18,498},{3,35},{19,499},{4... | collective-permute-start | bytes 786440 | tf_op jit(solution)/shard_map/ppermute | solution.py:138
  80.1 7.6 %collective-permute-start.16 = (bf16[1024,128]{1,0:T(8,128)(2,1)S(1)}, bf16[1024,128]{1,0:T(8,128)(2,1)S(1)}, u32[]{:S(2)}, u32[]{:S(2)}) collective-permute-start(bf16[1024,128]{1,0:T(8,128)(2,1)S(1)} %collective-permute-done.12.rest_3_), channel_id=1, source_target_pairs={{0,32},{16,496},{1,33},{17,497},{2,34},{18,498},{3,35},{19,499},{4... | collective-permute-start | bytes 786440 | tf_op jit(solution)/shard_map/ppermute | solution.py:138
  84.9 7.6 %collective-permute-start.14 = (bf16[1024,128]{1,0:T(8,128)(2,1)S(1)}, bf16[1024,128]{1,0:T(8,128)(2,1)S(1)}, u32[]{:S(2)}, u32[]{:S(2)}) collective-permute-start(bf16[1024,128]{1,0:T(8,128)(2,1)S(1)} %collective-permute-done.13.rest_0_), channel_id=1, source_target_pairs={{0,32},{16,496},{1,33},{17,497},{2,34},{18,498},{3,35},{19,499},{4... | collective-permute-start | bytes 786440 | tf_op jit(solution)/shard_map/ppermute | solution.py:138
  87.7 8.3 %collective-permute-start.17 = (bf16[1024,128]{1,0:T(8,128)(2,1)S(1)}, bf16[1024,128]{1,0:T(8,128)(2,1)S(1)}, u32[]{:S(2)}, u32[]{:S(2)}) collective-permute-start(bf16[1024,128]{1,0:T(8,128)(2,1)S(1)} %collective-permute-done.16.rest_2_), channel_id=1, source_target_pairs={{0,32},{16,496},{1,33},{17,497},{2,34},{18,498},{3,35},{19,499},{4... | collective-permute-start | bytes 786440 | tf_op jit(solution)/shard_map/ppermute | solution.py:138
  92.5 9.7 %collective-permute-start.15 = (bf16[1024,128]{1,0:T(8,128)(2,1)S(1)}, bf16[1024,128]{1,0:T(8,128)(2,1)S(1)}, u32[]{:S(2)}, u32[]{:S(2)}) collective-permute-start(bf16[1024,128]{1,0:T(8,128)(2,1)S(1)} %collective-permute-done.14.rest_1_), channel_id=1, source_target_pairs={{0,32},{16,496},{1,33},{17,497},{2,34},{18,498},{3,35},{19,499},{4... | collective-permute-start | bytes 786440 | tf_op jit(solution)/shard_map/ppermute | solution.py:138
  96.0 8.0 %collective-permute-start.18 = (bf16[1024,128]{1,0:T(8,128)(2,1)S(1)}, bf16[1024,128]{1,0:T(8,128)(2,1)S(1)}, u32[]{:S(2)}, u32[]{:S(2)}) collective-permute-start(bf16[1024,128]{1,0:T(8,128)(2,1)S(1)} %collective-permute-done.17.rest_3_), channel_id=1, source_target_pairs={{0,32},{16,496},{1,33},{17,497},{2,34},{18,498},{3,35},{19,499},{4... | collective-permute-start | bytes 786440 | tf_op jit(solution)/shard_map/ppermute | solution.py:138
  100.8 3.3 %copy-start = (bf16[512,1024]{1,0:T(8,128)(2,1)}, bf16[512,1024]{1,0:T(8,128)(2,1)S(1)}, u32[]{:S(2)}) copy-start(bf16[512,1024]{1,0:T(8,128)(2,1)S(1)} %collective-permute-done.2.beside_other) | copy-start | bytes 3145732
  106.3 27.7 %all-to-all-start.1 = ((bf16[32,32,384]{2,1,0:T(8,128)(2,1)}), bf16[32,32,384]{2,1,0:T(8,128)(2,1)}, u32[]{:S(2)}, u32[]{:S(2)}) async-start(bf16[32,32,384]{2,1,0:T(8,128)(2,1)} %bitcast.28), calls=%async_computation.1 | async-start | bytes 1572864 | tf_op jit(solution)/shard_map/all_to_all | solution.py:156
  120.2 1.2 copy-start.1
  121.4 0.9 copy-start.5
  126.2 2.5 %copy-start.15 = (bf16[1024,128]{1,0:T(8,128)(2,1)S(1)}, bf16[1024,128]{1,0:T(8,128)(2,1)}, u32[]{:S(2)}) copy-start(bf16[1024,128]{1,0:T(8,128)(2,1)} %copy-done.14) | copy-start | bytes 786436
  126.2 2.5 %copy-start.17 = (bf16[1024,128]{1,0:T(8,128)(2,1)S(1)}, bf16[1024,128]{1,0:T(8,128)(2,1)}, u32[]{:S(2)}) copy-start(bf16[1024,128]{1,0:T(8,128)(2,1)} %copy-done.16) | copy-start | bytes 786436
  126.2 2.5 %copy-start.19 = (bf16[1024,128]{1,0:T(8,128)(2,1)S(1)}, bf16[1024,128]{1,0:T(8,128)(2,1)}, u32[]{:S(2)}) copy-start(bf16[1024,128]{1,0:T(8,128)(2,1)} %copy-done.18) | copy-start | bytes 786436
  126.2 2.5 %copy-start.21 = (bf16[1024,128]{1,0:T(8,128)(2,1)S(1)}, bf16[1024,128]{1,0:T(8,128)(2,1)}, u32[]{:S(2)}) copy-start(bf16[1024,128]{1,0:T(8,128)(2,1)} %copy-done.20) | copy-start | bytes 786436
  130.0 1.1 copy-start.2
  133.9 5.1 %copy-start.25 = (s32[32]{0:T(128)S(1)}, s32[32]{0:T(128)}, u32[]{:S(2)}) copy-start(s32[32]{0:T(128)} %param.9) | copy-start | bytes 388
  133.9 24.4 %all-to-all-start = ((bf16[32,32,640]{2,1,0:T(8,128)(2,1)}), bf16[32,32,640]{2,1,0:T(8,128)(2,1)S(1)}, u32[]{:S(2)}, u32[]{:S(2)}) async-start(bf16[32,32,640]{2,1,0:T(8,128)(2,1)} %bitcast.27), calls=%async_computation | async-start | bytes 2621440 | tf_op jit(solution)/shard_map/all_to_all | solution.py:156
  (15 other events, 11.7 us)

commit v5 on v4

v5 whole, which is shorter than its diff:
```python
import jax
import jax.numpy as jnp
from jax import lax
from jax.experimental import pallas as pl
from jax.experimental.pallas import tpu as pltpu
from jax.sharding import Mesh, PartitionSpec as P


TILE = 128
KERNEL_VMEM = 16 << 20


def mask_tiles(matrix, occupancy):
    nrow, ncolumn = matrix.shape
    blocks = matrix.reshape(nrow // TILE, TILE, ncolumn // TILE, TILE)
    return (blocks * occupancy[:, None, :, None].astype(jnp.bfloat16)).reshape(nrow, ncolumn)


def rank(nz, ncol, z, core, col):
    return ((z % nz) * 2 + core) * ncol + col


def ring_pairs(nz, ncol):
    pairs = []
    for z in range(nz):
        for col in range(ncol):
            pairs.append((rank(nz, ncol, z, 0, col), rank(nz, ncol, z + 1, 0, col)))
            pairs.append((rank(nz, ncol, z, 1, col), rank(nz, ncol, z - 1, 1, col)))
    return pairs


def first_pairs(nz, ncol, stream):
    pairs = []
    for z in range(nz):
        for col in range(ncol):
            even = col & ~1
            for core in (0, 1):
                source = rank(nz, ncol, z, col & 1, even | (core ^ stream))
                target = rank(nz, ncol, z + 1 if core == 0 else z, core, col)
                pairs.append((source, target))
    return pairs


def swap_pairs(nz, ncol, core, col):
    return [
        (rank(nz, ncol, z, c, x), rank(nz, ncol, z, c ^ core, x ^ col))
        for z in range(nz) for c in (0, 1) for x in range(ncol)
    ]


NX = 4
CALLS = (4, 2, 1, 1)


def masked_tile(integrals, occupancy):
    def body(occ, tile, out):
        for k in range(tile.shape[0] // TILE):
            rows = slice(k * TILE, (k + 1) * TILE)
            out[rows, :] = tile[rows, :] * occ[k].astype(jnp.float32).astype(jnp.bfloat16)

    return pl.pallas_call(
        body,
        in_specs=[pl.BlockSpec(memory_space=pltpu.SMEM), pl.BlockSpec(memory_space=pltpu.VMEM)],
        out_specs=pl.BlockSpec(memory_space=pltpu.VMEM),
        out_shape=pltpu.VMEM(integrals.shape, jnp.bfloat16),
        compiler_params=pltpu.CompilerParams(vmem_limit_bytes=KERNEL_VMEM),
        name="masked_tile",
    )(occupancy.reshape(-1), integrals)


def multiply(blocks, tiles):
    nrow, kloc = blocks[0].shape
    count = len(tiles[0])
    width = count * TILE
    band = nrow // 4

    def body(own, beside, own_other, beside_other, *rest):
        tile_refs = rest[: 2 * count]
        keep, give, right, both = rest[2 * count :]
        core = lax.axis_index("core")
        odd = lax.axis_index("yp")
        stream = (lax.axis_index("x") + core) % 2
        for i in range(2 * count):
            right[i // count, :, (i % count) * TILE : (i % count + 1) * TILE] = tile_refs[i][...]
        for side, near, far in ((core, own, beside), (1 - core, own_other, beside_other)):
            for first in range(0, width, 2 * TILE):
                last = min(first + 2 * TILE, width)
                value = jnp.dot(near[...], right[stream, :, first:last], preferred_element_type=jnp.float32)
                value += jnp.dot(far[...], right[1 - stream, :, first:last], preferred_element_type=jnp.float32)
                value = value.astype(jnp.bfloat16)
                for quarter in range(4):
                    rows = value[quarter * band : (quarter + 1) * band]
                    both[quarter % 2, side, quarter // 2, :, first:last] = rows
        keep[...] = both[odd]
        give[...] = both[1 - odd]

    vmem = pl.BlockSpec(memory_space=pltpu.VMEM)
    operands = [*blocks, *tiles[0], *tiles[1]]
    half = (2, 2, band, width)
    return pl.pallas_call(
        body,
        in_specs=[vmem] * len(operands),
        out_specs=[vmem, vmem],
        out_shape=[pltpu.VMEM(half, jnp.bfloat16)] * 2,
        scratch_shapes=[pltpu.VMEM((2, kloc, width), jnp.bfloat16), pltpu.VMEM((2, *half), jnp.bfloat16)],
        compiler_params=pltpu.CompilerParams(vmem_limit_bytes=KERNEL_VMEM),
        name="multiply",
    )(*[pltpu.with_memory_space_constraint(o, pltpu.VMEM) for o in operands])


def join(kept, came):
    width = sum(k.shape[-1] for k in kept)
    lead = kept[0].shape[:-1]

    def body(*refs):
        out = refs[-1]
        start = 0
        for mine, other in zip(refs[: len(kept)], refs[len(kept) : -1]):
            last = start + mine.shape[-1]
            total = mine[...].astype(jnp.float32) + other[...].astype(jnp.float32)
            out[:, :, :, start:last] = total.astype(jnp.bfloat16)
            start = last

    vmem = pl.BlockSpec(memory_space=pltpu.VMEM)
    return pl.pallas_call(
        body,
        in_specs=[vmem] * (2 * len(kept)),
        out_specs=vmem,
        out_shape=pltpu.VMEM((*lead, width), jnp.bfloat16),
        compiler_params=pltpu.CompilerParams(vmem_limit_bytes=KERNEL_VMEM),
        name="join",
    )(*[pltpu.with_memory_space_constraint(o, pltpu.VMEM) for o in (*kept, *came)])


def make(nz, ncol):
    every = ("z", "core", "yh", "yp", "x")
    nslot = nz // 2
    assert sum(CALLS) == nslot

    def on_device(amplitudes, integrals, amp_occupancy, int_occupancy, owner_map):
        z = lax.axis_index("z")
        own_tile = masked_tile(integrals, int_occupancy)
        nrow, _ = amplitudes.shape
        part = nrow // ncol
        current = [own_tile, own_tile]
        kept, came = [], []
        tiles = [[], []]
        for slot in range(1, nslot + 1):
            for stream in (0, 1):
                pairs = first_pairs(nz, ncol, stream) if slot == 1 else ring_pairs(nz, ncol)
                current[stream] = lax.ppermute(current[stream], every, pairs)
                tiles[stream].append(current[stream])
            if slot == 1:
                own = mask_tiles(amplitudes, amp_occupancy)
                beside = lax.ppermute(own, every, swap_pairs(nz, ncol, 0, 1))
                own_other = lax.ppermute(own, every, swap_pairs(nz, ncol, 1, 0))
                beside_other = lax.ppermute(beside, every, swap_pairs(nz, ncol, 1, 0))
                blocks = (own, beside, own_other, beside_other)
            call = len(kept)
            if slot == sum(CALLS[: call + 1]):
                keep, give = multiply(blocks, tiles)
                tiles = [[], []]
                came.append(lax.ppermute(give, every, swap_pairs(nz, ncol, 0, NX)))
                kept.append(keep)
        moved = join(kept, came).reshape(ncol, part, nslot * TILE)
        moved = lax.all_to_all(moved, ("core", "yh", "x"), 0, 0, tiled=True)
        moved = moved.reshape(2, ncol // 4, 2, part, nslot * TILE)
        done = jnp.sum(moved.astype(jnp.float32), 1).astype(jnp.bfloat16).reshape(4, part, nslot, TILE)
        done = done.transpose(0, 2, 1, 3).reshape(4 * nslot, part, TILE)
        chip = owner_map // 2
        parity = owner_map % 2
        behind = (z - chip) % nz
        upward = (behind >= 1) & (behind <= nslot)
        side = jnp.where(upward, 0, 2)
        slot_of = jnp.where(upward, behind - 1, (chip - z) % nz)
        place = (side + parity) * nslot + slot_of
        picked = done[place].reshape(ncol, 2, part, TILE).transpose(0, 2, 1, 3).reshape(ncol, part, 2 * TILE)
        final = lax.all_to_all(picked, every[2:], 0, 0, tiled=True)
        return final.reshape(nrow, 2 * TILE)

    return on_device


def solution(mesh):
    nz = mesh.shape["row"] // 2
    ncol = mesh.shape["col"]
    ny = ncol // NX
    fine = Mesh(mesh.devices.reshape(nz, 2, ny // 2, 2, NX), ("z", "core", "yh", "yp", "x"))
    split, col = ("z", "core"), ("yh", "yp", "x")
    placed = (P(split, col), P(col, split), P(split, col), P(col, split), P())
    return jax.shard_map(
        make(nz, ncol), mesh=fine, in_specs=placed, out_specs=P(split, col), check_vma=False
    )
```

time: 172 us -> 164 us (0.953)
  local copies, waits for them, and re-layouts: 17.5 us -> 2.57 us
  waiting for transfers between devices: 39.7 us -> 50.5 us
  starting transfers between devices: 93 us -> 89.5 us
    unnamed x54 -> x10, local copies, waits for them, and re-layouts: 16.6 us -> 1.66 us
    ppermute x16, waiting for transfers between devices: 18.9 us -> 30.9 us  [on_device(): current[stream] = lax.ppermute(current[stream], every, pairs)]
    ppermute x16, starting transfers between devices: 67.8 us -> 56.5 us  [on_device(): current[stream] = lax.ppermute(current[stream], every, pairs)]
    ppermute x0 -> x4, starting transfers between devices: none -> 10.6 us  [on_device(): came.append(lax.ppermute(give, every, swap_pairs(nz, ncol, 0, NX)))]
    all_to_all x2 -> x1, starting transfers between devices: 19 us -> 14.1 us  [on_device(): moved = lax.all_to_all(moved, ('core', 'yh', 'x'), 0, 0, tiled=True)]
    all_to_all x2 -> x1, waiting for transfers between devices: 20.8 us -> 17 us  [on_device(): moved = lax.all_to_all(moved, ('core', 'yh', 'x'), 0, 0, tiled=True)]
    ppermute x0 -> x4, waiting for transfers between devices: none -> 2.55 us  [on_device(): came.append(lax.ppermute(give, every, swap_pairs(nz, ncol, 0, NX)))]
    ppermute x1, starting transfers between devices: 1.92 us -> 3.94 us  [on_device(): beside = lax.ppermute(own, every, swap_pairs(nz, ncol, 0, 1))]
  transfers between devices with their start and end apart: 21 -> 24, of which waited for: 4 -> 9; matrix products, arithmetic and copies ran while one was open for 1% -> 0% of each run, Pallas kernels for 3% -> 4%
where the time goes in v5:
time: 164 us
  starting transfers between devices  89.5 us (55%)
  waiting for transfers between devices  50.5 us (31%)
  blocking collectives  10.9 us (7%)
  Pallas kernels  8.56 us (5%)
  local copies, waits for them, and re-layouts  2.57 us (2%)
    ppermute x16, starting transfers between devices, on_device(): current[stream] = lax.ppermute(current[stream], every, pairs)  56.5 us
    ppermute x16, waiting for transfers between devices, on_device(): current[stream] = lax.ppermute(current[stream], every, pairs)  30.9 us
    all_to_all x1, waiting for transfers between devices, on_device(): moved = lax.all_to_all(moved, ('core', 'yh', 'x'), 0, 0, tiled=True)  17 us
    all_to_all x1, starting transfers between devices, on_device(): moved = lax.all_to_all(moved, ('core', 'yh', 'x'), 0, 0, tiled=True)  14.1 us
    all_to_all x1, blocking collectives, on_device(): final = lax.all_to_all(picked, every[2:], 0, 0, tiled=True)  10.9 us
    ppermute x4, starting transfers between devices, on_device(): came.append(lax.ppermute(give, every, swap_pairs(nz, ncol, 0, NX)))  10.6 us
    pallas_call x4, Pallas kernels, multiply(): pl.pallas_call(body, in_specs=[vmem] * len(operands), out_specs=[vmem, vm...  6.72 us
    ppermute x1, starting transfers between devices, on_device(): beside = lax.ppermute(own, every, swap_pairs(nz, ncol, 0, 1))  3.94 us
  transfers between devices with their start and end apart: 24, of which 9 were waited for; matrix products, arithmetic and copies ran while one was open for 0% of the time, Pallas kernels for 4%

profile of v5, /device:TPU:1, one launch (start us, length us, event | category | flops | bytes accessed | tf_op | source)
XLA Modules:
  0.0 163.6 jit_solution(1252211234696370914)
XLA Ops:
  1.4 3.9 %collective-permute-start = (bf16[512,1024]{1,0:T(8,128)(2,1)S(1)}, bf16[512,1024]{1,0:T(8,128)(2,1)S(1)}, u32[]{:S(2)}, u32[]{:S(2)}) collective-permute-start(bf16[512,1024]{1,0:T(8,128)(2,1)S(1)} %bitcast_multiply_fusion.own), channel_id=1, source_target_pairs={{0,1},{1,0},{2,3},{3,2},{4,5},{5,4},{6,7},{7,6},{8,9},{9,8},{10,11... | collective-permute-start | bytes 3145736 | tf_op jit(solution)/shard_map/ppermute | solution.py:155
  6.0 4.4 %collective-permute-start.3 = (bf16[1024,128]{1,0:T(8,128)(2,1)S(1)}, bf16[1024,128]{1,0:T(8,128)(2,1)S(1)}, u32[]{:S(2)}, u32[]{:S(2)}) collective-permute-start(bf16[1024,128]{1,0:T(8,128)(2,1)S(1)} %masked_tile.1), channel_id=1, source_target_pairs={{0,32},{1,16},{16,33},{17,17},{2,34},{3,18},{18,35},{19,19},{4,36}... | collective-permute-start | bytes 786440 | tf_op jit(solution)/shard_map/ppermute | solution.py:151
  10.3 1.9 %collective-permute-start.7 = (bf16[1024,128]{1,0:T(8,128)(2,1)S(1)}, bf16[1024,128]{1,0:T(8,128)(2,1)S(1)}, u32[]{:S(2)}, u32[]{:S(2)}) collective-permute-start(bf16[1024,128]{1,0:T(8,128)(2,1)S(1)} %masked_tile.1), channel_id=1, source_target_pairs={{1,32},{0,16},{17,33},{16,17},{3,34},{2,18},{19,35},{18,19},{5,36}... | collective-permute-start | bytes 786440 | tf_op jit(solution)/shard_map/ppermute | solution.py:151
  12.2 22.4 %collective-permute-done.3.rest_0_ = bf16[1024,128]{1,0:T(8,128)(2,1)S(1)} collective-permute-done((bf16[1024,128]{1,0:T(8,128)(2,1)S(1)}, bf16[1024,128]{1,0:T(8,128)(2,1)S(1)}, u32[]{:S(2)}, u32[]{:S(2)}) %collective-permute-start.3) | collective-permute-done | bytes 262176 | tf_op jit(solution)/shard_map/ppermute | solution.py:151
  34.7 11.4 %collective-permute-start.4 = (bf16[1024,128]{1,0:T(8,128)(2,1)S(1)}, bf16[1024,128]{1,0:T(8,128)(2,1)S(1)}, u32[]{:S(2)}, u32[]{:S(2)}) collective-permute-start(bf16[1024,128]{1,0:T(8,128)(2,1)S(1)} %collective-permute-done.3.rest_0_), channel_id=1, source_target_pairs={{0,32},{16,496},{1,33},{17,497},{2,34},{18,498},{3,35},{19,499},{4... | collective-permute-start | bytes 786440 | tf_op jit(solution)/shard_map/ppermute | solution.py:151
  46.0 2.6 %collective-permute-start.8 = (bf16[1024,128]{1,0:T(8,128)(2,1)S(1)}, bf16[1024,128]{1,0:T(8,128)(2,1)S(1)}, u32[]{:S(2)}, u32[]{:S(2)}) collective-permute-start(bf16[1024,128]{1,0:T(8,128)(2,1)S(1)} %collective-permute-done.7.rest_4_), channel_id=1, source_target_pairs={{0,32},{16,496},{1,33},{17,497},{2,34},{18,498},{3,35},{19,499},{4... | collective-permute-start | bytes 786440 | tf_op jit(solution)/shard_map/ppermute | solution.py:151
  49.3 5.0 %collective-permute-start.5 = (bf16[1024,128]{1,0:T(8,128)(2,1)S(1)}, bf16[1024,128]{1,0:T(8,128)(2,1)S(1)}, u32[]{:S(2)}, u32[]{:S(2)}) collective-permute-start(bf16[1024,128]{1,0:T(8,128)(2,1)S(1)} %collective-permute-done.4.rest_1_), channel_id=1, source_target_pairs={{0,32},{16,496},{1,33},{17,497},{2,34},{18,498},{3,35},{19,499},{4... | collective-permute-start | bytes 786440 | tf_op jit(solution)/shard_map/ppermute | solution.py:151
  54.4 2.8 %collective-permute-start.9 = (bf16[1024,128]{1,0:T(8,128)(2,1)S(1)}, bf16[1024,128]{1,0:T(8,128)(2,1)S(1)}, u32[]{:S(2)}, u32[]{:S(2)}) collective-permute-start(bf16[1024,128]{1,0:T(8,128)(2,1)S(1)} %collective-permute-done.8.rest_5_), channel_id=1, source_target_pairs={{0,32},{16,496},{1,33},{17,497},{2,34},{18,498},{3,35},{19,499},{4... | collective-permute-start | bytes 786440 | tf_op jit(solution)/shard_map/ppermute | solution.py:151
  57.2 1.9 %collective-permute-start.1 = (bf16[512,1024]{1,0:T(8,128)(2,1)S(1)}, bf16[512,1024]{1,0:T(8,128)(2,1)S(1)}, u32[]{:S(2)}, u32[]{:S(2)}) collective-permute-start(bf16[512,1024]{1,0:T(8,128)(2,1)S(1)} %bitcast_multiply_fusion.own), channel_id=1, source_target_pairs={{0,16},{1,17},{2,18},{3,19},{4,20},{5,21},{6,22},{7,23},{8,24},{9,... | collective-permute-start | bytes 3145736 | tf_op jit(solution)/shard_map/ppermute | solution.py:156
  59.1 2.4 %collective-permute-start.2 = (bf16[512,1024]{1,0:T(8,128)(2,1)S(1)}, bf16[512,1024]{1,0:T(8,128)(2,1)S(1)}, u32[]{:S(2)}, u32[]{:S(2)}) collective-permute-start(bf16[512,1024]{1,0:T(8,128)(2,1)S(1)} %collective-permute-done.beside), channel_id=1, source_target_pairs={{0,16},{1,17},{2,18},{3,19},{4,20},{5,21},{6,22},{7,23},{8,24},{9,... | collective-permute-start | bytes 3145736 | tf_op jit(solution)/shard_map/ppermute | solution.py:157
  61.5 1.9 %collective-permute-start.6 = (bf16[1024,128]{1,0:T(8,128)(2,1)S(1)}, bf16[1024,128]{1,0:T(8,128)(2,1)S(1)}, u32[]{:S(2)}, u32[]{:S(2)}) collective-permute-start(bf16[1024,128]{1,0:T(8,128)(2,1)S(1)} %collective-permute-done.5.rest_2_), channel_id=1, source_target_pairs={{0,32},{16,496},{1,33},{17,497},{2,34},{18,498},{3,35},{19,499},{4... | collective-permute-start | bytes 786440 | tf_op jit(solution)/shard_map/ppermute | solution.py:151
  63.5 2.1 %collective-permute-start.10 = (bf16[1024,128]{1,0:T(8,128)(2,1)S(1)}, bf16[1024,128]{1,0:T(8,128)(2,1)S(1)}, u32[]{:S(2)}, u32[]{:S(2)}) collective-permute-start(bf16[1024,128]{1,0:T(8,128)(2,1)S(1)} %collective-permute-done.9.rest_6_), channel_id=1, source_target_pairs={{0,32},{16,496},{1,33},{17,497},{2,34},{18,498},{3,35},{19,499},{4... | collective-permute-start | bytes 786440 | tf_op jit(solution)/shard_map/ppermute | solution.py:151
  65.6 3.3 %collective-permute-done.6.rest_3_ = bf16[1024,128]{1,0:T(8,128)(2,1)S(1)} collective-permute-done((bf16[1024,128]{1,0:T(8,128)(2,1)S(1)}, bf16[1024,128]{1,0:T(8,128)(2,1)S(1)}, u32[]{:S(2)}, u32[]{:S(2)}) %collective-permute-start.6) | collective-permute-done | bytes 262176 | tf_op jit(solution)/shard_map/ppermute | solution.py:151
  68.9 2.8 %collective-permute-start.11 = (bf16[1024,128]{1,0:T(8,128)(2,1)S(1)}, bf16[1024,128]{1,0:T(8,128)(2,1)S(1)}, u32[]{:S(2)}, u32[]{:S(2)}) collective-permute-start(bf16[1024,128]{1,0:T(8,128)(2,1)S(1)} %collective-permute-done.6.rest_3_), channel_id=1, source_target_pairs={{0,32},{16,496},{1,33},{17,497},{2,34},{18,498},{3,35},{19,499},{4... | collective-permute-start | bytes 786440 | tf_op jit(solution)/shard_map/ppermute | solution.py:151
  71.8 2.8 %collective-permute-start.13 = (bf16[1024,128]{1,0:T(8,128)(2,1)S(1)}, bf16[1024,128]{1,0:T(8,128)(2,1)S(1)}, u32[]{:S(2)}, u32[]{:S(2)}) collective-permute-start(bf16[1024,128]{1,0:T(8,128)(2,1)S(1)} %collective-permute-done.10.rest_7_), channel_id=1, source_target_pairs={{0,32},{16,496},{1,33},{17,497},{2,34},{18,498},{3,35},{19,499},{4... | collective-permute-start | bytes 786440 | tf_op jit(solution)/shard_map/ppermute | solution.py:151
  74.6 1.5 collective-permute-done.11.rest_0_
  76.0 4.0 %collective-permute-start.12 = (bf16[1024,128]{1,0:T(8,128)(2,1)S(1)}, bf16[1024,128]{1,0:T(8,128)(2,1)S(1)}, u32[]{:S(2)}, u32[]{:S(2)}) collective-permute-start(bf16[1024,128]{1,0:T(8,128)(2,1)S(1)} %collective-permute-done.11.rest_0_), channel_id=1, source_target_pairs={{0,32},{16,496},{1,33},{17,497},{2,34},{18,498},{3,35},{19,499},{4... | collective-permute-start | bytes 786440 | tf_op jit(solution)/shard_map/ppermute | solution.py:151
  80.1 2.8 %collective-permute-start.14 = (bf16[1024,128]{1,0:T(8,128)(2,1)S(1)}, bf16[1024,128]{1,0:T(8,128)(2,1)S(1)}, u32[]{:S(2)}, u32[]{:S(2)}) collective-permute-start(bf16[1024,128]{1,0:T(8,128)(2,1)S(1)} %collective-permute-done.13.rest_2_), channel_id=1, source_target_pairs={{0,32},{16,496},{1,33},{17,497},{2,34},{18,498},{3,35},{19,499},{4... | collective-permute-start | bytes 786440 | tf_op jit(solution)/shard_map/ppermute | solution.py:151
  83.4 5.0 %collective-permute-start.15 = (bf16[1024,128]{1,0:T(8,128)(2,1)S(1)}, bf16[1024,128]{1,0:T(8,128)(2,1)S(1)}, u32[]{:S(2)}, u32[]{:S(2)}) collective-permute-start(bf16[1024,128]{1,0:T(8,128)(2,1)S(1)} %collective-permute-done.12.rest_1_), channel_id=1, source_target_pairs={{0,32},{16,496},{1,33},{17,497},{2,34},{18,498},{3,35},{19,499},{4... | collective-permute-start | bytes 786440 | tf_op jit(solution)/shard_map/ppermute | solution.py:151
  88.4 2.8 %collective-permute-start.16 = (bf16[1024,128]{1,0:T(8,128)(2,1)S(1)}, bf16[1024,128]{1,0:T(8,128)(2,1)S(1)}, u32[]{:S(2)}, u32[]{:S(2)}) collective-permute-start(bf16[1024,128]{1,0:T(8,128)(2,1)S(1)} %collective-permute-done.14.rest_3_), channel_id=1, source_target_pairs={{0,32},{16,496},{1,33},{17,497},{2,34},{18,498},{3,35},{19,499},{4... | collective-permute-start | bytes 786440 | tf_op jit(solution)/shard_map/ppermute | solution.py:151
  91.2 2.7 %multiply.4 = (bf16[2,2,128,512]{3,2,1,0:T(8,128)(2,1)S(1)}, bf16[2,2,128,512]{3,2,1,0:T(8,128)(2,1)S(1)}) custom-call(bf16[512,1024]{1,0:T(8,128)(2,1)S(1)} %bitcast_multiply_fusion.own, bf16[512,1024]{1,0:T(8,128)(2,1)S(1)} %collective-permute-done.beside, bf16[512,1024]{1,0:T(8,128)(2,1)S(1)} %collective-permute-done.1.own_other, ...), custom_call_target="tpu_custom_call" | custom-call | tf_op jit(solution)/shard_map/multiply/pallas_call | solution.py:100
  93.9 3.2 %collective-permute-start.19 = (bf16[2,2,128,512]{3,2,1,0:T(8,128)(2,1)S(1)}, bf16[2,2,128,512]{3,2,1,0:T(8,128)(2,1)S(1)}, u32[]{:S(2)}, u32[]{:S(2)}) collective-permute-start(bf16[2,2,128,512]{3,2,1,0:T(8,128)(2,1)S(1)} %get-tuple-element.17), channel_id=1, source_target_pairs={{0,4},{1,5},{2,6},{3,7},{4,0},{5,1},{6,2},{7,3},{8,12},{9,13},{10,... | collective-permute-start | bytes 1572872 | tf_op jit(solution)/shard_map/ppermute | solution.py:163
  97.1 1.9 %collective-permute-start.17 = (bf16[1024,128]{1,0:T(8,128)(2,1)S(1)}, bf16[1024,128]{1,0:T(8,128)(2,1)S(1)}, u32[]{:S(2)}, u32[]{:S(2)}) collective-permute-start(bf16[1024,128]{1,0:T(8,128)(2,1)S(1)} %collective-permute-done.15.rest_0_), channel_id=1, source_target_pairs={{0,32},{16,496},{1,33},{17,497},{2,34},{18,498},{3,35},{19,499},{4... | collective-permute-start | bytes 786440 | tf_op jit(solution)/shard_map/ppermute | solution.py:151
  99.0 2.2 %collective-permute-start.18 = (bf16[1024,128]{1,0:T(8,128)(2,1)S(1)}, bf16[1024,128]{1,0:T(8,128)(2,1)S(1)}, u32[]{:S(2)}, u32[]{:S(2)}) collective-permute-start(bf16[1024,128]{1,0:T(8,128)(2,1)S(1)} %collective-permute-done.16.rest_1_), channel_id=1, source_target_pairs={{0,32},{16,496},{1,33},{17,497},{2,34},{18,498},{3,35},{19,499},{4... | collective-permute-start | bytes 786440 | tf_op jit(solution)/shard_map/ppermute | solution.py:151
  102.7 2.1 %collective-permute-start.20 = (bf16[2,2,128,256]{3,2,1,0:T(8,128)(2,1)S(1)}, bf16[2,2,128,256]{3,2,1,0:T(8,128)(2,1)S(1)}, u32[]{:S(2)}, u32[]{:S(2)}) collective-permute-start(bf16[2,2,128,256]{3,2,1,0:T(8,128)(2,1)S(1)} %get-tuple-element.18), channel_id=1, source_target_pairs={{0,4},{1,5},{2,6},{3,7},{4,0},{5,1},{6,2},{7,3},{8,12},{9,13},{10,... | collective-permute-start | bytes 786440 | tf_op jit(solution)/shard_map/ppermute | solution.py:163
  104.8 2.6 %collective-permute-done.18.rest_1_ = bf16[1024,128]{1,0:T(8,128)(2,1)S(1)} collective-permute-done((bf16[1024,128]{1,0:T(8,128)(2,1)S(1)}, bf16[1024,128]{1,0:T(8,128)(2,1)S(1)}, u32[]{:S(2)}, u32[]{:S(2)}) %collective-permute-start.18) | collective-permute-done | bytes 262176 | tf_op jit(solution)/shard_map/ppermute | solution.py:151
  108.7 2.1 %collective-permute-start.22 = (bf16[2,2,128,128]{3,2,1,0:T(8,128)(2,1)S(1)}, bf16[2,2,128,128]{3,2,1,0:T(8,128)(2,1)S(1)}, u32[]{:S(2)}, u32[]{:S(2)}) collective-permute-start(bf16[2,2,128,128]{3,2,1,0:T(8,128)(2,1)S(1)} %get-tuple-element.20), channel_id=1, source_target_pairs={{0,4},{1,5},{2,6},{3,7},{4,0},{5,1},{6,2},{7,3},{8,12},{9,13},{10,... | collective-permute-start | bytes 393224 | tf_op jit(solution)/shard_map/ppermute | solution.py:163
  112.1 3.2 %collective-permute-start.21 = (bf16[2,2,128,128]{3,2,1,0:T(8,128)(2,1)S(1)}, bf16[2,2,128,128]{3,2,1,0:T(8,128)(2,1)S(1)}, u32[]{:S(2)}, u32[]{:S(2)}) collective-permute-start(bf16[2,2,128,128]{3,2,1,0:T(8,128)(2,1)S(1)} %get-tuple-element.19), channel_id=1, source_target_pairs={{0,4},{1,5},{2,6},{3,7},{4,0},{5,1},{6,2},{7,3},{8,12},{9,13},{10,... | collective-permute-start | bytes 393224 | tf_op jit(solution)/shard_map/ppermute | solution.py:163
  116.1 1.8 %collective-permute-done.21.refs_6_ = bf16[2,2,128,128]{3,2,1,0:T(8,128)(2,1)S(1)} collective-permute-done((bf16[2,2,128,128]{3,2,1,0:T(8,128)(2,1)S(1)}, bf16[2,2,128,128]{3,2,1,0:T(8,128)(2,1)S(1)}, u32[]{:S(2)}, u32[]{:S(2)}) %collective-permute-start.21) | collective-permute-done | bytes 131104 | tf_op jit(solution)/shard_map/ppermute | solution.py:163
  119.1 14.1 %all-to-all-start = ((bf16[16,32,1024]{2,1,0:T(8,128)(2,1)}), bf16[16,32,1024]{2,1,0:T(8,128)(2,1)S(1)}, u32[]{:S(2)}, u32[]{:S(2)}) async-start(bf16[16,32,1024]{2,1,0:T(8,128)(2,1)} %bitcast.1), calls=%async_computation | async-start | bytes 2097152 | tf_op jit(solution)/shard_map/all_to_all | solution.py:166
  134.0 17.0 %all-to-all-done = bf16[16,32,1024]{2,1,0:T(8,128)(2,1)S(1)} async-done(((bf16[16,32,1024]{2,1,0:T(8,128)(2,1)}), bf16[16,32,1024]{2,1,0:T(8,128)(2,1)S(1)}, u32[]{:S(2)}, u32[]{:S(2)}) %all-to-all-start) | async-done | bytes 1048608 | tf_op jit(solution)/shard_map/all_to_all | solution.py:166
  151.9 10.9 %all_to_all.10 = bf16[16,32,256]{2,1,0:T(8,128)(2,1)S(1)} all-to-all(bf16[16,32,256]{2,1,0:T(8,128)(2,1)S(1)} %bitcast.32), channel_id=1, replica_groups=mesh['z'=16,'core'=2,'yh'=2,'yp'=2,'x'=4] {'yh','yp','x'}, dimensions={0} | all-to-all | bytes 524288 | tf_op jit(solution)/shard_map/all_to_all | solution.py:178
  (43 shorter events, 11.5 us)
Async XLA Ops:
  0.0 1.2 copy-start.2
  1.2 4.1 %copy-start = (bf16[1024,128]{1,0:T(8,128)(2,1)S(1)}, bf16[1024,128]{1,0:T(8,128)(2,1)}, u32[]{:S(2)}) copy-start(bf16[1024,128]{1,0:T(8,128)(2,1)} %tile.1) | copy-start | bytes 786436
  1.4 4.0 %copy-start.1 = (s32[8,1]{0,1:T(1,128)S(1)}, s32[8,1]{0,1:T(1,128)}, u32[]{:S(2)}) copy-start(s32[8,1]{0,1:T(1,128)} %param.8) | copy-start | bytes 100
  1.4 57.7 %collective-permute-start = (bf16[512,1024]{1,0:T(8,128)(2,1)S(1)}, bf16[512,1024]{1,0:T(8,128)(2,1)S(1)}, u32[]{:S(2)}, u32[]{:S(2)}) collective-permute-start(bf16[512,1024]{1,0:T(8,128)(2,1)S(1)} %bitcast_multiply_fusion.own), channel_id=1, source_target_pairs={{0,1},{1,0},{2,3},{3,2},{4,5},{5,4},{6,7},{7,6},{8,9},{9,8},{10,11... | collective-permute-start | bytes 3145736 | tf_op jit(solution)/shard_map/ppermute | solution.py:155
  6.0 28.7 %collective-permute-start.3 = (bf16[1024,128]{1,0:T(8,128)(2,1)S(1)}, bf16[1024,128]{1,0:T(8,128)(2,1)S(1)}, u32[]{:S(2)}, u32[]{:S(2)}) collective-permute-start(bf16[1024,128]{1,0:T(8,128)(2,1)S(1)} %masked_tile.1), channel_id=1, source_target_pairs={{0,32},{1,16},{16,33},{17,17},{2,34},{3,18},{18,35},{19,19},{4,36}... | collective-permute-start | bytes 786440 | tf_op jit(solution)/shard_map/ppermute | solution.py:151
  10.3 35.7 %collective-permute-start.7 = (bf16[1024,128]{1,0:T(8,128)(2,1)S(1)}, bf16[1024,128]{1,0:T(8,128)(2,1)S(1)}, u32[]{:S(2)}, u32[]{:S(2)}) collective-permute-start(bf16[1024,128]{1,0:T(8,128)(2,1)S(1)} %masked_tile.1), channel_id=1, source_target_pairs={{1,32},{0,16},{17,33},{16,17},{3,34},{2,18},{19,35},{18,19},{5,36}... | collective-permute-start | bytes 786440 | tf_op jit(solution)/shard_map/ppermute | solution.py:151
  34.7 14.7 %collective-permute-start.4 = (bf16[1024,128]{1,0:T(8,128)(2,1)S(1)}, bf16[1024,128]{1,0:T(8,128)(2,1)S(1)}, u32[]{:S(2)}, u32[]{:S(2)}) collective-permute-start(bf16[1024,128]{1,0:T(8,128)(2,1)S(1)} %collective-permute-done.3.rest_0_), channel_id=1, source_target_pairs={{0,32},{16,496},{1,33},{17,497},{2,34},{18,498},{3,35},{19,499},{4... | collective-permute-start | bytes 786440 | tf_op jit(solution)/shard_map/ppermute | solution.py:151
  46.0 8.3 %collective-permute-start.8 = (bf16[1024,128]{1,0:T(8,128)(2,1)S(1)}, bf16[1024,128]{1,0:T(8,128)(2,1)S(1)}, u32[]{:S(2)}, u32[]{:S(2)}) collective-permute-start(bf16[1024,128]{1,0:T(8,128)(2,1)S(1)} %collective-permute-done.7.rest_4_), channel_id=1, source_target_pairs={{0,32},{16,496},{1,33},{17,497},{2,34},{18,498},{3,35},{19,499},{4... | collective-permute-start | bytes 786440 | tf_op jit(solution)/shard_map/ppermute | solution.py:151
  49.3 12.2 %collective-permute-start.5 = (bf16[1024,128]{1,0:T(8,128)(2,1)S(1)}, bf16[1024,128]{1,0:T(8,128)(2,1)S(1)}, u32[]{:S(2)}, u32[]{:S(2)}) collective-permute-start(bf16[1024,128]{1,0:T(8,128)(2,1)S(1)} %collective-permute-done.4.rest_1_), channel_id=1, source_target_pairs={{0,32},{16,496},{1,33},{17,497},{2,34},{18,498},{3,35},{19,499},{4... | collective-permute-start | bytes 786440 | tf_op jit(solution)/shard_map/ppermute | solution.py:151
  54.4 9.1 %collective-permute-start.9 = (bf16[1024,128]{1,0:T(8,128)(2,1)S(1)}, bf16[1024,128]{1,0:T(8,128)(2,1)S(1)}, u32[]{:S(2)}, u32[]{:S(2)}) collective-permute-start(bf16[1024,128]{1,0:T(8,128)(2,1)S(1)} %collective-permute-done.8.rest_5_), channel_id=1, source_target_pairs={{0,32},{16,496},{1,33},{17,497},{2,34},{18,498},{3,35},{19,499},{4... | collective-permute-start | bytes 786440 | tf_op jit(solution)/shard_map/ppermute | solution.py:151
  57.2 34.1 %collective-permute-start.1 = (bf16[512,1024]{1,0:T(8,128)(2,1)S(1)}, bf16[512,1024]{1,0:T(8,128)(2,1)S(1)}, u32[]{:S(2)}, u32[]{:S(2)}) collective-permute-start(bf16[512,1024]{1,0:T(8,128)(2,1)S(1)} %bitcast_multiply_fusion.own), channel_id=1, source_target_pairs={{0,16},{1,17},{2,18},{3,19},{4,20},{5,21},{6,22},{7,23},{8,24},{9,... | collective-permute-start | bytes 3145736 | tf_op jit(solution)/shard_map/ppermute | solution.py:156
  59.1 32.1 %collective-permute-start.2 = (bf16[512,1024]{1,0:T(8,128)(2,1)S(1)}, bf16[512,1024]{1,0:T(8,128)(2,1)S(1)}, u32[]{:S(2)}, u32[]{:S(2)}) collective-permute-start(bf16[512,1024]{1,0:T(8,128)(2,1)S(1)} %collective-permute-done.beside), channel_id=1, source_target_pairs={{0,16},{1,17},{2,18},{3,19},{4,20},{5,21},{6,22},{7,23},{8,24},{9,... | collective-permute-start | bytes 3145736 | tf_op jit(solution)/shard_map/ppermute | solution.py:157
  61.5 7.4 %collective-permute-start.6 = (bf16[1024,128]{1,0:T(8,128)(2,1)S(1)}, bf16[1024,128]{1,0:T(8,128)(2,1)S(1)}, u32[]{:S(2)}, u32[]{:S(2)}) collective-permute-start(bf16[1024,128]{1,0:T(8,128)(2,1)S(1)} %collective-permute-done.5.rest_2_), channel_id=1, source_target_pairs={{0,32},{16,496},{1,33},{17,497},{2,34},{18,498},{3,35},{19,499},{4... | collective-permute-start | bytes 786440 | tf_op jit(solution)/shard_map/ppermute | solution.py:151
  63.5 8.3 %collective-permute-start.10 = (bf16[1024,128]{1,0:T(8,128)(2,1)S(1)}, bf16[1024,128]{1,0:T(8,128)(2,1)S(1)}, u32[]{:S(2)}, u32[]{:S(2)}) collective-permute-start(bf16[1024,128]{1,0:T(8,128)(2,1)S(1)} %collective-permute-done.9.rest_6_), channel_id=1, source_target_pairs={{0,32},{16,496},{1,33},{17,497},{2,34},{18,498},{3,35},{19,499},{4... | collective-permute-start | bytes 786440 | tf_op jit(solution)/shard_map/ppermute | solution.py:151
  68.9 7.1 %collective-permute-start.11 = (bf16[1024,128]{1,0:T(8,128)(2,1)S(1)}, bf16[1024,128]{1,0:T(8,128)(2,1)S(1)}, u32[]{:S(2)}, u32[]{:S(2)}) collective-permute-start(bf16[1024,128]{1,0:T(8,128)(2,1)S(1)} %collective-permute-done.6.rest_3_), channel_id=1, source_target_pairs={{0,32},{16,496},{1,33},{17,497},{2,34},{18,498},{3,35},{19,499},{4... | collective-permute-start | bytes 786440 | tf_op jit(solution)/shard_map/ppermute | solution.py:151
  71.8 8.3 %collective-permute-start.13 = (bf16[1024,128]{1,0:T(8,128)(2,1)S(1)}, bf16[1024,128]{1,0:T(8,128)(2,1)S(1)}, u32[]{:S(2)}, u32[]{:S(2)}) collective-permute-start(bf16[1024,128]{1,0:T(8,128)(2,1)S(1)} %collective-permute-done.10.rest_7_), channel_id=1, source_target_pairs={{0,32},{16,496},{1,33},{17,497},{2,34},{18,498},{3,35},{19,499},{4... | collective-permute-start | bytes 786440 | tf_op jit(solution)/shard_map/ppermute | solution.py:151
  76.0 7.3 %collective-permute-start.12 = (bf16[1024,128]{1,0:T(8,128)(2,1)S(1)}, bf16[1024,128]{1,0:T(8,128)(2,1)S(1)}, u32[]{:S(2)}, u32[]{:S(2)}) collective-permute-start(bf16[1024,128]{1,0:T(8,128)(2,1)S(1)} %collective-permute-done.11.rest_0_), channel_id=1, source_target_pairs={{0,32},{16,496},{1,33},{17,497},{2,34},{18,498},{3,35},{19,499},{4... | collective-permute-start | bytes 786440 | tf_op jit(solution)/shard_map/ppermute | solution.py:151
  80.1 8.3 %collective-permute-start.14 = (bf16[1024,128]{1,0:T(8,128)(2,1)S(1)}, bf16[1024,128]{1,0:T(8,128)(2,1)S(1)}, u32[]{:S(2)}, u32[]{:S(2)}) collective-permute-start(bf16[1024,128]{1,0:T(8,128)(2,1)S(1)} %collective-permute-done.13.rest_2_), channel_id=1, source_target_pairs={{0,32},{16,496},{1,33},{17,497},{2,34},{18,498},{3,35},{19,499},{4... | collective-permute-start | bytes 786440 | tf_op jit(solution)/shard_map/ppermute | solution.py:151
  83.4 13.7 %collective-permute-start.15 = (bf16[1024,128]{1,0:T(8,128)(2,1)S(1)}, bf16[1024,128]{1,0:T(8,128)(2,1)S(1)}, u32[]{:S(2)}, u32[]{:S(2)}) collective-permute-start(bf16[1024,128]{1,0:T(8,128)(2,1)S(1)} %collective-permute-done.12.rest_1_), channel_id=1, source_target_pairs={{0,32},{16,496},{1,33},{17,497},{2,34},{18,498},{3,35},{19,499},{4... | collective-permute-start | bytes 786440 | tf_op jit(solution)/shard_map/ppermute | solution.py:151
  88.4 10.6 %collective-permute-start.16 = (bf16[1024,128]{1,0:T(8,128)(2,1)S(1)}, bf16[1024,128]{1,0:T(8,128)(2,1)S(1)}, u32[]{:S(2)}, u32[]{:S(2)}) collective-permute-start(bf16[1024,128]{1,0:T(8,128)(2,1)S(1)} %collective-permute-done.14.rest_3_), channel_id=1, source_target_pairs={{0,32},{16,496},{1,33},{17,497},{2,34},{18,498},{3,35},{19,499},{4... | collective-permute-start | bytes 786440 | tf_op jit(solution)/shard_map/ppermute | solution.py:151
  93.9 24.0 %collective-permute-start.19 = (bf16[2,2,128,512]{3,2,1,0:T(8,128)(2,1)S(1)}, bf16[2,2,128,512]{3,2,1,0:T(8,128)(2,1)S(1)}, u32[]{:S(2)}, u32[]{:S(2)}) collective-permute-start(bf16[2,2,128,512]{3,2,1,0:T(8,128)(2,1)S(1)} %get-tuple-element.17), channel_id=1, source_target_pairs={{0,4},{1,5},{2,6},{3,7},{4,0},{5,1},{6,2},{7,3},{8,12},{9,13},{10,... | collective-permute-start | bytes 1572872 | tf_op jit(solution)/shard_map/ppermute | solution.py:163
  97.1 7.7 %collective-permute-start.17 = (bf16[1024,128]{1,0:T(8,128)(2,1)S(1)}, bf16[1024,128]{1,0:T(8,128)(2,1)S(1)}, u32[]{:S(2)}, u32[]{:S(2)}) collective-permute-start(bf16[1024,128]{1,0:T(8,128)(2,1)S(1)} %collective-permute-done.15.rest_0_), channel_id=1, source_target_pairs={{0,32},{16,496},{1,33},{17,497},{2,34},{18,498},{3,35},{19,499},{4... | collective-permute-start | bytes 786440 | tf_op jit(solution)/shard_map/ppermute | solution.py:151
  99.0 8.3 %collective-permute-start.18 = (bf16[1024,128]{1,0:T(8,128)(2,1)S(1)}, bf16[1024,128]{1,0:T(8,128)(2,1)S(1)}, u32[]{:S(2)}, u32[]{:S(2)}) collective-permute-start(bf16[1024,128]{1,0:T(8,128)(2,1)S(1)} %collective-permute-done.16.rest_1_), channel_id=1, source_target_pairs={{0,32},{16,496},{1,33},{17,497},{2,34},{18,498},{3,35},{19,499},{4... | collective-permute-start | bytes 786440 | tf_op jit(solution)/shard_map/ppermute | solution.py:151
  102.7 15.2 %collective-permute-start.20 = (bf16[2,2,128,256]{3,2,1,0:T(8,128)(2,1)S(1)}, bf16[2,2,128,256]{3,2,1,0:T(8,128)(2,1)S(1)}, u32[]{:S(2)}, u32[]{:S(2)}) collective-permute-start(bf16[2,2,128,256]{3,2,1,0:T(8,128)(2,1)S(1)} %get-tuple-element.18), channel_id=1, source_target_pairs={{0,4},{1,5},{2,6},{3,7},{4,0},{5,1},{6,2},{7,3},{8,12},{9,13},{10,... | collective-permute-start | bytes 786440 | tf_op jit(solution)/shard_map/ppermute | solution.py:163
  108.7 7.4 %collective-permute-start.22 = (bf16[2,2,128,128]{3,2,1,0:T(8,128)(2,1)S(1)}, bf16[2,2,128,128]{3,2,1,0:T(8,128)(2,1)S(1)}, u32[]{:S(2)}, u32[]{:S(2)}) collective-permute-start(bf16[2,2,128,128]{3,2,1,0:T(8,128)(2,1)S(1)} %get-tuple-element.20), channel_id=1, source_target_pairs={{0,4},{1,5},{2,6},{3,7},{4,0},{5,1},{6,2},{7,3},{8,12},{9,13},{10,... | collective-permute-start | bytes 393224 | tf_op jit(solution)/shard_map/ppermute | solution.py:163
  112.1 5.8 %collective-permute-start.21 = (bf16[2,2,128,128]{3,2,1,0:T(8,128)(2,1)S(1)}, bf16[2,2,128,128]{3,2,1,0:T(8,128)(2,1)S(1)}, u32[]{:S(2)}, u32[]{:S(2)}) collective-permute-start(bf16[2,2,128,128]{3,2,1,0:T(8,128)(2,1)S(1)} %get-tuple-element.19), channel_id=1, source_target_pairs={{0,4},{1,5},{2,6},{3,7},{4,0},{5,1},{6,2},{7,3},{8,12},{9,13},{10,... | collective-permute-start | bytes 393224 | tf_op jit(solution)/shard_map/ppermute | solution.py:163
  119.1 31.8 %all-to-all-start = ((bf16[16,32,1024]{2,1,0:T(8,128)(2,1)}), bf16[16,32,1024]{2,1,0:T(8,128)(2,1)S(1)}, u32[]{:S(2)}, u32[]{:S(2)}) async-start(bf16[16,32,1024]{2,1,0:T(8,128)(2,1)} %bitcast.1), calls=%async_computation | async-start | bytes 2097152 | tf_op jit(solution)/shard_map/all_to_all | solution.py:166
  133.3 0.7 copy-start.3

commit v6 on v4

--- a/solution.py
+++ b/solution.py
@@ -48,7 +48,7 @@
     ]
 
 
-CHUNKS = ((3, 2), (2, 1))
+CHUNKS = ((4,), (4,))
 
 
 def calls_of():
@@ -116,13 +116,52 @@
     )(*[pltpu.with_memory_space_constraint(o, pltpu.VMEM) for o in operands])
 
 
+def gather_tiles(early, late, owner_map, nz, nslot):
+    part = late.shape[1]
+    ntile = owner_map.shape[0]
+    ncol = late.shape[0] // 2
+
+    def body(owner, summed, parts, out, done):
+        before = summed.shape[-1] // TILE
+        for core in (0, 1):
+            for odd in (0, 1):
+                base = (core * 2 + odd) * nslot
+                for slot in range(before):
+                    done[base + slot] = summed[core * 2 + odd, :, slot * TILE : (slot + 1) * TILE]
+                for slot in range(before, nslot):
+                    cols = slice((slot - before) * TILE, (slot - before + 1) * TILE)
+                    total = None
+                    for col in range(odd, ncol, 2):
+                        value = parts[core * ncol + col, :, cols].astype(jnp.float32)
+                        total = value if total is None else total + value
+                    done[base + slot] = total.astype(jnp.bfloat16)
+        z = lax.axis_index("z")
+        for t in range(ntile):
+            tile = owner[t]
+            chip = tile // 2
+            behind = (z - chip + nz) % nz
+            upward = (behind >= 1) & (behind <= nslot)
+            place = jnp.where(upward, behind - 1, 2 * nslot + (chip - z + nz) % nz) + tile % 2 * nslot
+            out[t // 2, :, t % 2 * TILE : (t % 2 + 1) * TILE] = done[place]
+
+    vmem = pl.BlockSpec(memory_space=pltpu.VMEM)
+    return pl.pallas_call(
+        body,
+        in_specs=[pl.BlockSpec(memory_space=pltpu.SMEM), vmem, vmem],
+        out_specs=vmem,
+        out_shape=pltpu.VMEM((ntile // 2, part, 2 * TILE), jnp.bfloat16),
+        scratch_shapes=[pltpu.VMEM((4 * nslot, part, TILE), jnp.bfloat16)],
+        compiler_params=pltpu.CompilerParams(vmem_limit_bytes=KERNEL_VMEM),
+        name="gather_tiles",
+    )(owner_map, *[pltpu.with_memory_space_constraint(o, pltpu.VMEM) for o in (early, late)])
+
+
 def make(nz, ncol):
     every = ("z", "core", "col")
     nslot = nz // 2
     assert sum(map(sum, CHUNKS)) == nslot
 
     def on_device(amplitudes, integrals, amp_occupancy, int_occupancy, owner_map):
-        z = lax.axis_index("z")
         own_tile = masked_tile(integrals, int_occupancy)
         nrow, _ = amplitudes.shape
         part = nrow // ncol
@@ -154,19 +193,10 @@
                 moved = product.reshape(2 * ncol, part, width)
                 product = None
                 moved = lax.all_to_all(moved, ("core", "col"), 0, 0, tiled=True)
-                moved = moved.reshape(2, ncol // 2, 2, part, width)
-                total = jnp.sum(moved.astype(jnp.float32), 1)
-                sums.append(total.astype(jnp.bfloat16))
-        done = jnp.concatenate(sums, 3).reshape(4, part, nslot, TILE)
-        done = done.transpose(0, 2, 1, 3).reshape(4 * nslot, part, TILE)
-        chip = owner_map // 2
-        parity = owner_map % 2
-        behind = (z - chip) % nz
-        upward = (behind >= 1) & (behind <= nslot)
-        side = jnp.where(upward, 0, 2)
-        slot_of = jnp.where(upward, behind - 1, (chip - z) % nz)
-        place = (side + parity) * nslot + slot_of
-        picked = done[place].reshape(ncol, 2, part, TILE).transpose(0, 2, 1, 3).reshape(ncol, part, 2 * TILE)
+                sums.append(moved)
+        early = sums[0].reshape(2, ncol // 2, 2, part, -1)
+        early = jnp.sum(early.astype(jnp.float32), 1).astype(jnp.bfloat16).reshape(4, part, -1)
+        picked = gather_tiles(early, sums[1], owner_map, nz, nslot)
         final = lax.all_to_all(picked, "col", 0, 0, tiled=True)
         return final.reshape(nrow, 2 * TILE)
 

time: 172 us -> 162 us (0.942)
  local copies, waits for them, and re-layouts: 17.5 us -> 4.34 us
  starting transfers between devices: 93 us -> 102 us
  waiting for transfers between devices: 39.7 us -> 31.2 us
  Pallas kernels: 6.95 us -> 9.1 us
    unnamed x54 -> x17, local copies, waits for them, and re-layouts: 16.6 us -> 4.14 us
    ppermute x16, waiting for transfers between devices: 18.9 us -> 6.54 us  [on_device(): current[stream] = lax.ppermute(current[stream], every, pairs)]
    ppermute x1, waiting for transfers between devices: 0.01 us -> 9.56 us  [on_device(): beside = lax.ppermute(own, every, swap_pairs(nz, ncol, 0, 1))]
    ppermute x1, starting transfers between devices: 2.41 us -> 10.1 us  [on_device(): beside_other = lax.ppermute(beside, every, swap_pairs(nz, ncol, 1, 0))]
    all_to_all x2, waiting for transfers between devices: 20.8 us -> 15.1 us  [on_device(): moved = lax.all_to_all(moved, ('core', 'col'), 0, 0, tiled=True)]
    ppermute x1, starting transfers between devices: 1.91 us -> 4.29 us  [on_device(): own_other = lax.ppermute(own, every, swap_pairs(nz, ncol, 1, 0))]
    ppermute x1, starting transfers between devices: 1.92 us -> 3.94 us  [on_device(): beside = lax.ppermute(own, every, swap_pairs(nz, ncol, 0, 1))]
    pallas_call x4 -> x2, Pallas kernels: 6.37 us -> 7.45 us  [multiply(): pl.pallas_call(body, in_specs=[vmem] * len(operands), out_specs=vmem, out...]
  transfers between devices with their start and end apart: 21 -> 21, of which waited for: 4 -> 8; matrix products, arithmetic and copies ran while one was open for 1% -> 1% of each run, Pallas kernels for 3% -> 5%
where the time goes in v6:
time: 162 us; the launch traced here: 161 us
  starting transfers between devices  102 us (63%)
  waiting for transfers between devices  31.2 us (19%)
  blocking collectives  11.3 us (7%)
  Pallas kernels  9.1 us (6%)
  local copies, waits for them, and re-layouts  4.34 us (3%)
  other arithmetic  2.29 us (1%)
    ppermute x16, starting transfers between devices, on_device(): current[stream] = lax.ppermute(current[stream], every, pairs)  66.2 us
    all_to_all x2, starting transfers between devices, on_device(): moved = lax.all_to_all(moved, ('core', 'col'), 0, 0, tiled=True)  17.6 us
    all_to_all x2, waiting for transfers between devices, on_device(): moved = lax.all_to_all(moved, ('core', 'col'), 0, 0, tiled=True)  15.1 us
    all_to_all x1, blocking collectives, on_device(): final = lax.all_to_all(picked, 'col', 0, 0, tiled=True)  11.3 us
    ppermute x1, starting transfers between devices, on_device(): beside_other = lax.ppermute(beside, every, swap_pairs(nz, ncol, 1, 0))  10.1 us
    ppermute x1, waiting for transfers between devices, on_device(): beside = lax.ppermute(own, every, swap_pairs(nz, ncol, 0, 1))  9.56 us
    pallas_call x2, Pallas kernels, multiply(): pl.pallas_call(body, in_specs=[vmem] * len(operands), out_specs=vmem, out...  7.45 us
    ppermute x16, waiting for transfers between devices, on_device(): current[stream] = lax.ppermute(current[stream], every, pairs)  6.54 us
  transfers between devices with their start and end apart: 21, of which 8 were waited for; matrix products, arithmetic and copies ran while one was open for 1% of the time, Pallas kernels for 5%

profile of v6, /device:TPU:1, one launch (start us, length us, event | category | flops | bytes accessed | tf_op | source)
XLA Modules:
  0.0 160.9 jit_solution(4632073868180565111)
XLA Ops:
  1.4 3.9 %collective-permute-start = (bf16[512,1024]{1,0:T(8,128)(2,1)S(1)}, bf16[512,1024]{1,0:T(8,128)(2,1)S(1)}, u32[]{:S(2)}, u32[]{:S(2)}) collective-permute-start(bf16[512,1024]{1,0:T(8,128)(2,1)S(1)} %bitcast_multiply_fusion.own), channel_id=1, source_target_pairs={{0,1},{1,0},{2,3},{3,2},{4,5},{5,4},{6,7},{7,6},{8,9},{9,8},{10,11... | collective-permute-start | bytes 3145736 | tf_op jit(solution)/shard_map/ppermute | solution.py:181
  6.0 4.4 %collective-permute-start.3 = (bf16[1024,128]{1,0:T(8,128)(2,1)S(1)}, bf16[1024,128]{1,0:T(8,128)(2,1)S(1)}, u32[]{:S(2)}, u32[]{:S(2)}) collective-permute-start(bf16[1024,128]{1,0:T(8,128)(2,1)S(1)} %masked_tile.1), channel_id=1, source_target_pairs={{0,32},{1,16},{16,33},{17,17},{2,34},{3,18},{18,35},{19,19},{4,36}... | collective-permute-start | bytes 786440 | tf_op jit(solution)/shard_map/ppermute | solution.py:177
  10.3 1.9 %collective-permute-start.7 = (bf16[1024,128]{1,0:T(8,128)(2,1)S(1)}, bf16[1024,128]{1,0:T(8,128)(2,1)S(1)}, u32[]{:S(2)}, u32[]{:S(2)}) collective-permute-start(bf16[1024,128]{1,0:T(8,128)(2,1)S(1)} %masked_tile.1), channel_id=1, source_target_pairs={{1,32},{0,16},{17,33},{16,17},{3,34},{2,18},{19,35},{18,19},{5,36}... | collective-permute-start | bytes 786440 | tf_op jit(solution)/shard_map/ppermute | solution.py:177
  12.2 4.3 %collective-permute-start.1 = (bf16[512,1024]{1,0:T(8,128)(2,1)S(1)}, bf16[512,1024]{1,0:T(8,128)(2,1)S(1)}, u32[]{:S(2)}, u32[]{:S(2)}) collective-permute-start(bf16[512,1024]{1,0:T(8,128)(2,1)S(1)} %bitcast_multiply_fusion.own), channel_id=1, source_target_pairs={{0,16},{1,17},{2,18},{3,19},{4,20},{5,21},{6,22},{7,23},{8,24},{9,... | collective-permute-start | bytes 3145736 | tf_op jit(solution)/shard_map/ppermute | solution.py:182
  16.5 9.6 %collective-permute-done.beside = bf16[512,1024]{1,0:T(8,128)(2,1)S(1)} collective-permute-done((bf16[512,1024]{1,0:T(8,128)(2,1)S(1)}, bf16[512,1024]{1,0:T(8,128)(2,1)S(1)}, u32[]{:S(2)}, u32[]{:S(2)}) %collective-permute-start) | collective-permute-done | bytes 1048608 | tf_op jit(solution)/shard_map/ppermute | solution.py:181
  26.1 10.1 %collective-permute-start.2 = (bf16[512,1024]{1,0:T(8,128)(2,1)S(1)}, bf16[512,1024]{1,0:T(8,128)(2,1)S(1)}, u32[]{:S(2)}, u32[]{:S(2)}) collective-permute-start(bf16[512,1024]{1,0:T(8,128)(2,1)S(1)} %collective-permute-done.beside), channel_id=1, source_target_pairs={{0,16},{1,17},{2,18},{3,19},{4,20},{5,21},{6,22},{7,23},{8,24},{9,... | collective-permute-start | bytes 3145736 | tf_op jit(solution)/shard_map/ppermute | solution.py:183
  36.2 9.5 %collective-permute-start.4 = (bf16[1024,128]{1,0:T(8,128)(2,1)S(1)}, bf16[1024,128]{1,0:T(8,128)(2,1)S(1)}, u32[]{:S(2)}, u32[]{:S(2)}) collective-permute-start(bf16[1024,128]{1,0:T(8,128)(2,1)S(1)} %collective-permute-done.3.rest_0_), channel_id=1, source_target_pairs={{0,32},{16,496},{1,33},{17,497},{2,34},{18,498},{3,35},{19,499},{4... | collective-permute-start | bytes 786440 | tf_op jit(solution)/shard_map/ppermute | solution.py:177
  45.7 2.6 %collective-permute-start.8 = (bf16[1024,128]{1,0:T(8,128)(2,1)S(1)}, bf16[1024,128]{1,0:T(8,128)(2,1)S(1)}, u32[]{:S(2)}, u32[]{:S(2)}) collective-permute-start(bf16[1024,128]{1,0:T(8,128)(2,1)S(1)} %collective-permute-done.7.rest_4_), channel_id=1, source_target_pairs={{0,32},{16,496},{1,33},{17,497},{2,34},{18,498},{3,35},{19,499},{4... | collective-permute-start | bytes 786440 | tf_op jit(solution)/shard_map/ppermute | solution.py:177
  49.0 5.0 %collective-permute-start.5 = (bf16[1024,128]{1,0:T(8,128)(2,1)S(1)}, bf16[1024,128]{1,0:T(8,128)(2,1)S(1)}, u32[]{:S(2)}, u32[]{:S(2)}) collective-permute-start(bf16[1024,128]{1,0:T(8,128)(2,1)S(1)} %collective-permute-done.4.rest_1_), channel_id=1, source_target_pairs={{0,32},{16,496},{1,33},{17,497},{2,34},{18,498},{3,35},{19,499},{4... | collective-permute-start | bytes 786440 | tf_op jit(solution)/shard_map/ppermute | solution.py:177
  54.1 2.8 %collective-permute-start.9 = (bf16[1024,128]{1,0:T(8,128)(2,1)S(1)}, bf16[1024,128]{1,0:T(8,128)(2,1)S(1)}, u32[]{:S(2)}, u32[]{:S(2)}) collective-permute-start(bf16[1024,128]{1,0:T(8,128)(2,1)S(1)} %collective-permute-done.8.rest_5_), channel_id=1, source_target_pairs={{0,32},{16,496},{1,33},{17,497},{2,34},{18,498},{3,35},{19,499},{4... | collective-permute-start | bytes 786440 | tf_op jit(solution)/shard_map/ppermute | solution.py:177
  57.3 5.0 %collective-permute-start.6 = (bf16[1024,128]{1,0:T(8,128)(2,1)S(1)}, bf16[1024,128]{1,0:T(8,128)(2,1)}, u32[]{:S(2)}, u32[]{:S(2)}) collective-permute-start(bf16[1024,128]{1,0:T(8,128)(2,1)S(1)} %collective-permute-done.5.rest_2_), channel_id=1, source_target_pairs={{0,32},{16,496},{1,33},{17,497},{2,34},{18,498},{3,35},{19,499},{4... | collective-permute-start | bytes 786440 | tf_op jit(solution)/shard_map/ppermute | solution.py:177
  62.4 2.8 %collective-permute-start.10 = (bf16[1024,128]{1,0:T(8,128)(2,1)S(1)}, bf16[1024,128]{1,0:T(8,128)(2,1)}, u32[]{:S(2)}, u32[]{:S(2)}) collective-permute-start(bf16[1024,128]{1,0:T(8,128)(2,1)S(1)} %collective-permute-done.9.rest_6_), channel_id=1, source_target_pairs={{0,32},{16,496},{1,33},{17,497},{2,34},{18,498},{3,35},{19,499},{4... | collective-permute-start | bytes 786440 | tf_op jit(solution)/shard_map/ppermute | solution.py:177
  65.7 5.1 %collective-permute-start.11 = (bf16[1024,128]{1,0:T(8,128)(2,1)}, bf16[1024,128]{1,0:T(8,128)(2,1)S(1)}, u32[]{:S(2)}, u32[]{:S(2)}) collective-permute-start(bf16[1024,128]{1,0:T(8,128)(2,1)} %collective-permute-done.6.rest_3_), channel_id=1, source_target_pairs={{0,32},{16,496},{1,33},{17,497},{2,34},{18,498},{3,35},{19,499},{4... | collective-permute-start | bytes 786440 | tf_op jit(solution)/shard_map/ppermute | solution.py:177
  70.8 2.8 %collective-permute-start.15 = (bf16[1024,128]{1,0:T(8,128)(2,1)}, bf16[1024,128]{1,0:T(8,128)(2,1)}, u32[]{:S(2)}, u32[]{:S(2)}) collective-permute-start(bf16[1024,128]{1,0:T(8,128)(2,1)} %collective-permute-done.10.rest_7_), channel_id=1, source_target_pairs={{0,32},{16,496},{1,33},{17,497},{2,34},{18,498},{3,35},{19,499},{4... | collective-permute-start | bytes 786440 | tf_op jit(solution)/shard_map/ppermute | solution.py:177
  73.6 4.0 %multiply.2 = bf16[2,512,512]{2,1,0:T(8,128)(2,1)S(1)} custom-call(bf16[512,1024]{1,0:T(8,128)(2,1)S(1)} %bitcast_multiply_fusion.own, bf16[512,1024]{1,0:T(8,128)(2,1)S(1)} %collective-permute-done.beside, bf16[512,1024]{1,0:T(8,128)(2,1)S(1)} %collective-permute-done.1.own_other, bf16[512,1024]{1,0:T(8,128)(2,1)S(1)} %collective-permute-done.2.beside_other, ...), custom_call_target="tpu_custom_call" | custom-call | tf_op jit(solution)/shard_map/multiply/pallas_call | solution.py:107
  77.6 0.9 copy-done.2
  78.6 8.3 %all-to-all-start = ((bf16[32,32,512]{2,1,0:T(8,128)(2,1)}), bf16[32,32,512]{2,1,0:T(8,128)(2,1)}, u32[]{:S(2)}, u32[]{:S(2)}) async-start(bf16[32,32,512]{2,1,0:T(8,128)(2,1)} %bitcast.10), calls=%async_computation | async-start | bytes 2097152 | tf_op jit(solution)/shard_map/all_to_all | solution.py:195
  86.9 4.8 %collective-permute-start.12 = (bf16[1024,128]{1,0:T(8,128)(2,1)S(1)}, bf16[1024,128]{1,0:T(8,128)(2,1)S(1)}, u32[]{:S(2)}, u32[]{:S(2)}) collective-permute-start(bf16[1024,128]{1,0:T(8,128)(2,1)S(1)} %collective-permute-done.11.rest_0_), channel_id=1, source_target_pairs={{0,32},{16,496},{1,33},{17,497},{2,34},{18,498},{3,35},{19,499},{4... | collective-permute-start | bytes 786440 | tf_op jit(solution)/shard_map/ppermute | solution.py:177
  91.8 2.8 %collective-permute-start.16 = (bf16[1024,128]{1,0:T(8,128)(2,1)}, bf16[1024,128]{1,0:T(8,128)(2,1)S(1)}, u32[]{:S(2)}, u32[]{:S(2)}) collective-permute-start(bf16[1024,128]{1,0:T(8,128)(2,1)} %collective-permute-done.15.rest_4_), channel_id=1, source_target_pairs={{0,32},{16,496},{1,33},{17,497},{2,34},{18,498},{3,35},{19,499},{4... | collective-permute-start | bytes 786440 | tf_op jit(solution)/shard_map/ppermute | solution.py:177
  95.1 5.0 %collective-permute-start.13 = (bf16[1024,128]{1,0:T(8,128)(2,1)S(1)}, bf16[1024,128]{1,0:T(8,128)(2,1)S(1)}, u32[]{:S(2)}, u32[]{:S(2)}) collective-permute-start(bf16[1024,128]{1,0:T(8,128)(2,1)S(1)} %collective-permute-done.12.rest_1_), channel_id=1, source_target_pairs={{0,32},{16,496},{1,33},{17,497},{2,34},{18,498},{3,35},{19,499},{4... | collective-permute-start | bytes 786440 | tf_op jit(solution)/shard_map/ppermute | solution.py:177
  100.1 3.4 %collective-permute-start.17 = (bf16[1024,128]{1,0:T(8,128)(2,1)S(1)}, bf16[1024,128]{1,0:T(8,128)(2,1)S(1)}, u32[]{:S(2)}, u32[]{:S(2)}) collective-permute-start(bf16[1024,128]{1,0:T(8,128)(2,1)S(1)} %collective-permute-done.16.rest_5_), channel_id=1, source_target_pairs={{0,32},{16,496},{1,33},{17,497},{2,34},{18,498},{3,35},{19,499},{4... | collective-permute-start | bytes 786440 | tf_op jit(solution)/shard_map/ppermute | solution.py:177
  103.5 5.3 %collective-permute-start.14 = (bf16[1024,128]{1,0:T(8,128)(2,1)S(1)}, bf16[1024,128]{1,0:T(8,128)(2,1)S(1)}, u32[]{:S(2)}, u32[]{:S(2)}) collective-permute-start(bf16[1024,128]{1,0:T(8,128)(2,1)S(1)} %collective-permute-done.13.rest_2_), channel_id=1, source_target_pairs={{0,32},{16,496},{1,33},{17,497},{2,34},{18,498},{3,35},{19,499},{4... | collective-permute-start | bytes 786440 | tf_op jit(solution)/shard_map/ppermute | solution.py:177
  108.8 3.0 %collective-permute-start.18 = (bf16[1024,128]{1,0:T(8,128)(2,1)S(1)}, bf16[1024,128]{1,0:T(8,128)(2,1)S(1)}, u32[]{:S(2)}, u32[]{:S(2)}) collective-permute-start(bf16[1024,128]{1,0:T(8,128)(2,1)S(1)} %collective-permute-done.17.rest_6_), channel_id=1, source_target_pairs={{0,32},{16,496},{1,33},{17,497},{2,34},{18,498},{3,35},{19,499},{4... | collective-permute-start | bytes 786440 | tf_op jit(solution)/shard_map/ppermute | solution.py:177
  112.1 4.1 %collective-permute-done.18.rest_7_ = bf16[1024,128]{1,0:T(8,128)(2,1)S(1)} collective-permute-done((bf16[1024,128]{1,0:T(8,128)(2,1)S(1)}, bf16[1024,128]{1,0:T(8,128)(2,1)S(1)}, u32[]{:S(2)}, u32[]{:S(2)}) %collective-permute-start.18) | collective-permute-done | bytes 262176 | tf_op jit(solution)/shard_map/ppermute | solution.py:177
  116.2 1.2 copy-done.1
  117.5 3.5 %multiply.3 = bf16[2,512,512]{2,1,0:T(8,128)(2,1)S(1)} custom-call(bf16[512,1024]{1,0:T(8,128)(2,1)S(1)} %bitcast_multiply_fusion.own, bf16[512,1024]{1,0:T(8,128)(2,1)S(1)} %collective-permute-done.beside, bf16[512,1024]{1,0:T(8,128)(2,1)S(1)} %collective-permute-done.1.own_other, bf16[512,1024]{1,0:T(8,128)(2,1)S(1)} %copy-done.1, ...), custom_call_target="tpu_custom_call" | custom-call | tf_op jit(solution)/shard_map/multiply/pallas_call | solution.py:107
  121.0 1.0 copy-done.3
  121.9 9.3 %all-to-all-start.1 = ((bf16[32,32,512]{2,1,0:T(8,128)(2,1)}), bf16[32,32,512]{2,1,0:T(8,128)(2,1)S(1)}, u32[]{:S(2)}, u32[]{:S(2)}) async-start(bf16[32,32,512]{2,1,0:T(8,128)(2,1)} %bitcast.11), calls=%async_computation.1 | async-start | bytes 2097152 | tf_op jit(solution)/shard_map/all_to_all | solution.py:195
  131.2 1.4 reduce_sum.12
  132.6 15.1 %all-to-all-done.1.parts = bf16[32,32,512]{2,1,0:T(8,128)(2,1)S(1)} async-done(((bf16[32,32,512]{2,1,0:T(8,128)(2,1)}), bf16[32,32,512]{2,1,0:T(8,128)(2,1)S(1)}, u32[]{:S(2)}, u32[]{:S(2)}) %all-to-all-start.1) | async-done | bytes 1048608 | tf_op jit(solution)/shard_map/all_to_all | solution.py:195
  147.8 1.1 gather_tiles.1
  148.9 11.3 %all_to_all.15 = bf16[16,32,256]{2,1,0:T(8,128)(2,1)S(1)} all-to-all(bf16[16,32,256]{2,1,0:T(8,128)(2,1)S(1)} %gather_tiles.1), channel_id=1, replica_groups=mesh['z'=16,'core'=2,'col'=16] {'col'}, dimensions={0} | all-to-all | bytes 524288 | tf_op jit(solution)/shard_map/all_to_all | solution.py:200
  (36 shorter events, 5.1 us)
Async XLA Ops:
  0.0 1.2 copy-start.7
  1.2 4.1 %copy-start.4 = (bf16[1024,128]{1,0:T(8,128)(2,1)S(1)}, bf16[1024,128]{1,0:T(8,128)(2,1)}, u32[]{:S(2)}) copy-start(bf16[1024,128]{1,0:T(8,128)(2,1)} %tile.1) | copy-start | bytes 786436
  1.4 4.0 %copy-start.5 = (s32[8,1]{0,1:T(1,128)S(1)}, s32[8,1]{0,1:T(1,128)}, u32[]{:S(2)}) copy-start(s32[8,1]{0,1:T(1,128)} %param.8) | copy-start | bytes 100
  1.4 24.7 %collective-permute-start = (bf16[512,1024]{1,0:T(8,128)(2,1)S(1)}, bf16[512,1024]{1,0:T(8,128)(2,1)S(1)}, u32[]{:S(2)}, u32[]{:S(2)}) collective-permute-start(bf16[512,1024]{1,0:T(8,128)(2,1)S(1)} %bitcast_multiply_fusion.own), channel_id=1, source_target_pairs={{0,1},{1,0},{2,3},{3,2},{4,5},{5,4},{6,7},{7,6},{8,9},{9,8},{10,11... | collective-permute-start | bytes 3145736 | tf_op jit(solution)/shard_map/ppermute | solution.py:181
  6.0 30.3 %collective-permute-start.3 = (bf16[1024,128]{1,0:T(8,128)(2,1)S(1)}, bf16[1024,128]{1,0:T(8,128)(2,1)S(1)}, u32[]{:S(2)}, u32[]{:S(2)}) collective-permute-start(bf16[1024,128]{1,0:T(8,128)(2,1)S(1)} %masked_tile.1), channel_id=1, source_target_pairs={{0,32},{1,16},{16,33},{17,17},{2,34},{3,18},{18,35},{19,19},{4,36}... | collective-permute-start | bytes 786440 | tf_op jit(solution)/shard_map/ppermute | solution.py:177
  10.3 35.4 %collective-permute-start.7 = (bf16[1024,128]{1,0:T(8,128)(2,1)S(1)}, bf16[1024,128]{1,0:T(8,128)(2,1)S(1)}, u32[]{:S(2)}, u32[]{:S(2)}) collective-permute-start(bf16[1024,128]{1,0:T(8,128)(2,1)S(1)} %masked_tile.1), channel_id=1, source_target_pairs={{1,32},{0,16},{17,33},{16,17},{3,34},{2,18},{19,35},{18,19},{5,36}... | collective-permute-start | bytes 786440 | tf_op jit(solution)/shard_map/ppermute | solution.py:177
  12.2 61.3 %collective-permute-start.1 = (bf16[512,1024]{1,0:T(8,128)(2,1)S(1)}, bf16[512,1024]{1,0:T(8,128)(2,1)S(1)}, u32[]{:S(2)}, u32[]{:S(2)}) collective-permute-start(bf16[512,1024]{1,0:T(8,128)(2,1)S(1)} %bitcast_multiply_fusion.own), channel_id=1, source_target_pairs={{0,16},{1,17},{2,18},{3,19},{4,20},{5,21},{6,22},{7,23},{8,24},{9,... | collective-permute-start | bytes 3145736 | tf_op jit(solution)/shard_map/ppermute | solution.py:182
  26.1 47.5 %collective-permute-start.2 = (bf16[512,1024]{1,0:T(8,128)(2,1)S(1)}, bf16[512,1024]{1,0:T(8,128)(2,1)S(1)}, u32[]{:S(2)}, u32[]{:S(2)}) collective-permute-start(bf16[512,1024]{1,0:T(8,128)(2,1)S(1)} %collective-permute-done.beside), channel_id=1, source_target_pairs={{0,16},{1,17},{2,18},{3,19},{4,20},{5,21},{6,22},{7,23},{8,24},{9,... | collective-permute-start | bytes 3145736 | tf_op jit(solution)/shard_map/ppermute | solution.py:183
  36.2 12.8 %collective-permute-start.4 = (bf16[1024,128]{1,0:T(8,128)(2,1)S(1)}, bf16[1024,128]{1,0:T(8,128)(2,1)S(1)}, u32[]{:S(2)}, u32[]{:S(2)}) collective-permute-start(bf16[1024,128]{1,0:T(8,128)(2,1)S(1)} %collective-permute-done.3.rest_0_), channel_id=1, source_target_pairs={{0,32},{16,496},{1,33},{17,497},{2,34},{18,498},{3,35},{19,499},{4... | collective-permute-start | bytes 786440 | tf_op jit(solution)/shard_map/ppermute | solution.py:177
  45.7 8.3 %collective-permute-start.8 = (bf16[1024,128]{1,0:T(8,128)(2,1)S(1)}, bf16[1024,128]{1,0:T(8,128)(2,1)S(1)}, u32[]{:S(2)}, u32[]{:S(2)}) collective-permute-start(bf16[1024,128]{1,0:T(8,128)(2,1)S(1)} %collective-permute-done.7.rest_4_), channel_id=1, source_target_pairs={{0,32},{16,496},{1,33},{17,497},{2,34},{18,498},{3,35},{19,499},{4... | collective-permute-start | bytes 786440 | tf_op jit(solution)/shard_map/ppermute | solution.py:177
  49.0 8.3 %collective-permute-start.5 = (bf16[1024,128]{1,0:T(8,128)(2,1)S(1)}, bf16[1024,128]{1,0:T(8,128)(2,1)S(1)}, u32[]{:S(2)}, u32[]{:S(2)}) collective-permute-start(bf16[1024,128]{1,0:T(8,128)(2,1)S(1)} %collective-permute-done.4.rest_1_), channel_id=1, source_target_pairs={{0,32},{16,496},{1,33},{17,497},{2,34},{18,498},{3,35},{19,499},{4... | collective-permute-start | bytes 786440 | tf_op jit(solution)/shard_map/ppermute | solution.py:177
  54.1 8.3 %collective-permute-start.9 = (bf16[1024,128]{1,0:T(8,128)(2,1)S(1)}, bf16[1024,128]{1,0:T(8,128)(2,1)S(1)}, u32[]{:S(2)}, u32[]{:S(2)}) collective-permute-start(bf16[1024,128]{1,0:T(8,128)(2,1)S(1)} %collective-permute-done.8.rest_5_), channel_id=1, source_target_pairs={{0,32},{16,496},{1,33},{17,497},{2,34},{18,498},{3,35},{19,499},{4... | collective-permute-start | bytes 786440 | tf_op jit(solution)/shard_map/ppermute | solution.py:177
  57.3 8.3 %collective-permute-start.6 = (bf16[1024,128]{1,0:T(8,128)(2,1)S(1)}, bf16[1024,128]{1,0:T(8,128)(2,1)}, u32[]{:S(2)}, u32[]{:S(2)}) collective-permute-start(bf16[1024,128]{1,0:T(8,128)(2,1)S(1)} %collective-permute-done.5.rest_2_), channel_id=1, source_target_pairs={{0,32},{16,496},{1,33},{17,497},{2,34},{18,498},{3,35},{19,499},{4... | collective-permute-start | bytes 786440 | tf_op jit(solution)/shard_map/ppermute | solution.py:177
  62.4 8.4 %collective-permute-start.10 = (bf16[1024,128]{1,0:T(8,128)(2,1)S(1)}, bf16[1024,128]{1,0:T(8,128)(2,1)}, u32[]{:S(2)}, u32[]{:S(2)}) collective-permute-start(bf16[1024,128]{1,0:T(8,128)(2,1)S(1)} %collective-permute-done.9.rest_6_), channel_id=1, source_target_pairs={{0,32},{16,496},{1,33},{17,497},{2,34},{18,498},{3,35},{19,499},{4... | collective-permute-start | bytes 786440 | tf_op jit(solution)/shard_map/ppermute | solution.py:177
  65.7 21.3 %collective-permute-start.11 = (bf16[1024,128]{1,0:T(8,128)(2,1)}, bf16[1024,128]{1,0:T(8,128)(2,1)S(1)}, u32[]{:S(2)}, u32[]{:S(2)}) collective-permute-start(bf16[1024,128]{1,0:T(8,128)(2,1)} %collective-permute-done.6.rest_3_), channel_id=1, source_target_pairs={{0,32},{16,496},{1,33},{17,497},{2,34},{18,498},{3,35},{19,499},{4... | collective-permute-start | bytes 786440 | tf_op jit(solution)/shard_map/ppermute | solution.py:177
  70.8 21.0 %collective-permute-start.15 = (bf16[1024,128]{1,0:T(8,128)(2,1)}, bf16[1024,128]{1,0:T(8,128)(2,1)}, u32[]{:S(2)}, u32[]{:S(2)}) collective-permute-start(bf16[1024,128]{1,0:T(8,128)(2,1)} %collective-permute-done.10.rest_7_), channel_id=1, source_target_pairs={{0,32},{16,496},{1,33},{17,497},{2,34},{18,498},{3,35},{19,499},{4... | collective-permute-start | bytes 786440 | tf_op jit(solution)/shard_map/ppermute | solution.py:177
  73.6 4.0 %copy-start = (bf16[512,1024]{1,0:T(8,128)(2,1)}, bf16[512,1024]{1,0:T(8,128)(2,1)S(1)}, u32[]{:S(2)}) copy-start(bf16[512,1024]{1,0:T(8,128)(2,1)S(1)} %collective-permute-done.2.beside_other) | copy-start | bytes 3145732
  77.6 1.0 copy-start.2
  78.6 43.4 %all-to-all-start = ((bf16[32,32,512]{2,1,0:T(8,128)(2,1)}), bf16[32,32,512]{2,1,0:T(8,128)(2,1)}, u32[]{:S(2)}, u32[]{:S(2)}) async-start(bf16[32,32,512]{2,1,0:T(8,128)(2,1)} %bitcast.10), calls=%async_computation | async-start | bytes 2097152 | tf_op jit(solution)/shard_map/all_to_all | solution.py:195
  86.9 8.1 %collective-permute-start.12 = (bf16[1024,128]{1,0:T(8,128)(2,1)S(1)}, bf16[1024,128]{1,0:T(8,128)(2,1)S(1)}, u32[]{:S(2)}, u32[]{:S(2)}) collective-permute-start(bf16[1024,128]{1,0:T(8,128)(2,1)S(1)} %collective-permute-done.11.rest_0_), channel_id=1, source_target_pairs={{0,32},{16,496},{1,33},{17,497},{2,34},{18,498},{3,35},{19,499},{4... | collective-permute-start | bytes 786440 | tf_op jit(solution)/shard_map/ppermute | solution.py:177
  91.8 8.3 %collective-permute-start.16 = (bf16[1024,128]{1,0:T(8,128)(2,1)}, bf16[1024,128]{1,0:T(8,128)(2,1)S(1)}, u32[]{:S(2)}, u32[]{:S(2)}) collective-permute-start(bf16[1024,128]{1,0:T(8,128)(2,1)} %collective-permute-done.15.rest_4_), channel_id=1, source_target_pairs={{0,32},{16,496},{1,33},{17,497},{2,34},{18,498},{3,35},{19,499},{4... | collective-permute-start | bytes 786440 | tf_op jit(solution)/shard_map/ppermute | solution.py:177
  95.1 8.4 %collective-permute-start.13 = (bf16[1024,128]{1,0:T(8,128)(2,1)S(1)}, bf16[1024,128]{1,0:T(8,128)(2,1)S(1)}, u32[]{:S(2)}, u32[]{:S(2)}) collective-permute-start(bf16[1024,128]{1,0:T(8,128)(2,1)S(1)} %collective-permute-done.12.rest_1_), channel_id=1, source_target_pairs={{0,32},{16,496},{1,33},{17,497},{2,34},{18,498},{3,35},{19,499},{4... | collective-permute-start | bytes 786440 | tf_op jit(solution)/shard_map/ppermute | solution.py:177
  100.1 8.7 %collective-permute-start.17 = (bf16[1024,128]{1,0:T(8,128)(2,1)S(1)}, bf16[1024,128]{1,0:T(8,128)(2,1)S(1)}, u32[]{:S(2)}, u32[]{:S(2)}) collective-permute-start(bf16[1024,128]{1,0:T(8,128)(2,1)S(1)} %collective-permute-done.16.rest_5_), channel_id=1, source_target_pairs={{0,32},{16,496},{1,33},{17,497},{2,34},{18,498},{3,35},{19,499},{4... | collective-permute-start | bytes 786440 | tf_op jit(solution)/shard_map/ppermute | solution.py:177
  103.5 8.6 %collective-permute-start.14 = (bf16[1024,128]{1,0:T(8,128)(2,1)S(1)}, bf16[1024,128]{1,0:T(8,128)(2,1)S(1)}, u32[]{:S(2)}, u32[]{:S(2)}) collective-permute-start(bf16[1024,128]{1,0:T(8,128)(2,1)S(1)} %collective-permute-done.13.rest_2_), channel_id=1, source_target_pairs={{0,32},{16,496},{1,33},{17,497},{2,34},{18,498},{3,35},{19,499},{4... | collective-permute-start | bytes 786440 | tf_op jit(solution)/shard_map/ppermute | solution.py:177
  108.8 7.4 %collective-permute-start.18 = (bf16[1024,128]{1,0:T(8,128)(2,1)S(1)}, bf16[1024,128]{1,0:T(8,128)(2,1)S(1)}, u32[]{:S(2)}, u32[]{:S(2)}) collective-permute-start(bf16[1024,128]{1,0:T(8,128)(2,1)S(1)} %collective-permute-done.17.rest_6_), channel_id=1, source_target_pairs={{0,32},{16,496},{1,33},{17,497},{2,34},{18,498},{3,35},{19,499},{4... | collective-permute-start | bytes 786440 | tf_op jit(solution)/shard_map/ppermute | solution.py:177
  116.2 1.2 copy-start.1
  121.0 1.0 copy-start.3
  121.9 25.8 %all-to-all-start.1 = ((bf16[32,32,512]{2,1,0:T(8,128)(2,1)}), bf16[32,32,512]{2,1,0:T(8,128)(2,1)S(1)}, u32[]{:S(2)}, u32[]{:S(2)}) async-start(bf16[32,32,512]{2,1,0:T(8,128)(2,1)} %bitcast.11), calls=%async_computation.1 | async-start | bytes 2097152 | tf_op jit(solution)/shard_map/all_to_all | solution.py:195
  132.6 15.2 %copy-start.6 = (s32[32]{0:T(128)S(1)}, s32[32]{0:T(128)}, u32[]{:S(2)}) copy-start(s32[32]{0:T(128)} %owner.1) | copy-start | bytes 388

commit v7 on v6

--- a/solution.py
+++ b/solution.py
@@ -36,9 +36,15 @@
             even = col & ~1
             for core in (0, 1):
                 source = rank(nz, ncol, z, col & 1, even | (core ^ stream))
-                target = rank(nz, ncol, z + 1 if core == 0 else z, core, col)
-                pairs.append((source, target))
+                pairs.append((source, rank(nz, ncol, z + 1 - 2 * core, core, col)))
     return pairs
+
+
+def own_pairs(nz, ncol):
+    return [
+        (rank(nz, ncol, z, col & 1, (col & ~1) | core), rank(nz, ncol, z, core, col))
+        for z in range(nz) for col in range(ncol) for core in (0, 1)
+    ]
 
 
 def swap_pairs(nz, ncol, core, col):
@@ -48,12 +54,12 @@
     ]
 
 
-CHUNKS = ((4,), (4,))
+CHUNKS = ((5,), (3, 1))
 
 
 def calls_of():
     calls = []
-    slot = 0
+    slot = -1
     for k, chunk in enumerate(CHUNKS):
         begin = 0
         for count in chunk:
@@ -85,13 +91,27 @@
     part = count * TILE
 
     def body(own, beside, own_other, beside_other, *rest):
-        tile_refs = rest[: 2 * count]
         out, right = rest[-2:]
         core = lax.axis_index("core")
         stream = (lax.axis_index("col") + core) % 2
+        used = 0
         for i in range(2 * count):
-            right[i // count, :, (i % count) * TILE : (i % count + 1) * TILE] = tile_refs[i][...]
+            cols = slice((i % count) * TILE, (i % count + 1) * TILE)
+            if tiles[i // count][i % count] is None:
+                right[i // count, :, cols] = jnp.zeros((kloc, TILE), jnp.bfloat16)
+            else:
+                right[i // count, :, cols] = rest[used][...]
+                used += 1
         for side, near, far in ((core, own, beside), (1 - core, own_other, beside_other)):
+            if all(t is None for t in tiles[1]):
+                for pick, left in ((0, near), (1, far)):
+
+                    @pl.when(stream == pick)
+                    def _(side=side, left=left):
+                        value = jnp.dot(left[...], right[0], preferred_element_type=jnp.float32)
+                        out[side, :, start : start + part] = value.astype(jnp.bfloat16)
+
+                continue
             for first in range(0, part, 2 * TILE):
                 last = min(first + 2 * TILE, part)
                 value = jnp.dot(near[...], right[stream, :, first:last], preferred_element_type=jnp.float32)
@@ -99,7 +119,7 @@
                 out[side, :, start + first : start + last] = value.astype(jnp.bfloat16)
 
     vmem = pl.BlockSpec(memory_space=pltpu.VMEM)
-    operands = [*blocks, *tiles[0], *tiles[1]]
+    operands = [*blocks, *(t for t in tiles[0] + tiles[1] if t is not None)]
     aliases = {}
     if previous is not None:
         aliases = {len(operands): 0}
@@ -121,27 +141,32 @@
     ntile = owner_map.shape[0]
     ncol = late.shape[0] // 2
 
-    def body(owner, summed, parts, out, done):
-        before = summed.shape[-1] // TILE
-        for core in (0, 1):
-            for odd in (0, 1):
-                base = (core * 2 + odd) * nslot
-                for slot in range(before):
-                    done[base + slot] = summed[core * 2 + odd, :, slot * TILE : (slot + 1) * TILE]
-                for slot in range(before, nslot):
-                    cols = slice((slot - before) * TILE, (slot - before + 1) * TILE)
-                    total = None
-                    for col in range(odd, ncol, 2):
-                        value = parts[core * ncol + col, :, cols].astype(jnp.float32)
-                        total = value if total is None else total + value
-                    done[base + slot] = total.astype(jnp.bfloat16)
+    before = early.shape[-1] // TILE
+    block = nslot + 1
+
+    def body(owner, first, second, out, done):
+        def total_of(core, odd, slot):
+            parts, at = (first, slot) if slot < before else (second, slot - before)
+            total = None
+            for col in range(odd, ncol, 2):
+                value = parts[core * ncol + col, :, at * TILE : (at + 1) * TILE].astype(jnp.float32)
+                total = value if total is None else total + value
+            return total
+
+        for odd in (0, 1):
+            for slot in range(block):
+                if slot in (0, nslot):
+                    both = total_of(0, odd, slot) + total_of(1, odd, slot)
+                    done[odd * block + slot] = both.astype(jnp.bfloat16)
+                    continue
+                for core in (0, 1):
+                    done[(core * 2 + odd) * block + slot] = total_of(core, odd, slot).astype(jnp.bfloat16)
         z = lax.axis_index("z")
         for t in range(ntile):
             tile = owner[t]
             chip = tile // 2
             behind = (z - chip + nz) % nz
-            upward = (behind >= 1) & (behind <= nslot)
-            place = jnp.where(upward, behind - 1, 2 * nslot + (chip - z + nz) % nz) + tile % 2 * nslot
+            place = jnp.where(behind <= nslot, behind, 2 * block + nz - behind) + tile % 2 * block
             out[t // 2, :, t % 2 * TILE : (t % 2 + 1) * TILE] = done[place]
 
     vmem = pl.BlockSpec(memory_space=pltpu.VMEM)
@@ -150,7 +175,7 @@
         in_specs=[pl.BlockSpec(memory_space=pltpu.SMEM), vmem, vmem],
         out_specs=vmem,
         out_shape=pltpu.VMEM((ntile // 2, part, 2 * TILE), jnp.bfloat16),
-        scratch_shapes=[pltpu.VMEM((4 * nslot, part, TILE), jnp.bfloat16)],
+        scratch_shapes=[pltpu.VMEM((4 * (nslot + 1), part, TILE), jnp.bfloat16)],
         compiler_params=pltpu.CompilerParams(vmem_limit_bytes=KERNEL_VMEM),
         name="gather_tiles",
     )(owner_map, *[pltpu.with_memory_space_constraint(o, pltpu.VMEM) for o in (early, late)])
@@ -159,7 +184,7 @@
 def make(nz, ncol):
     every = ("z", "core", "col")
     nslot = nz // 2
-    assert sum(map(sum, CHUNKS)) == nslot
+    assert sum(map(sum, CHUNKS)) == nslot + 1
 
     def on_device(amplitudes, integrals, amp_occupancy, int_occupancy, owner_map):
         own_tile = masked_tile(integrals, int_occupancy)
@@ -167,12 +192,15 @@
         part = nrow // ncol
         current = [own_tile, own_tile]
         sums = []
-        tiles = [[], []]
+        tiles = [[lax.ppermute(own_tile, every, own_pairs(nz, ncol))], [None]]
         ends = calls_of()
         call = 0
         product = None
         for slot in range(1, nslot + 1):
             for stream in (0, 1):
+                if stream == 1 and slot == nslot:
+                    tiles[1].append(None)
+                    continue
                 pairs = first_pairs(nz, ncol, stream) if slot == 1 else ring_pairs(nz, ncol)
                 current[stream] = lax.ppermute(current[stream], every, pairs)
                 tiles[stream].append(current[stream])
@@ -194,9 +222,7 @@
                 product = None
                 moved = lax.all_to_all(moved, ("core", "col"), 0, 0, tiled=True)
                 sums.append(moved)
-        early = sums[0].reshape(2, ncol // 2, 2, part, -1)
-        early = jnp.sum(early.astype(jnp.float32), 1).astype(jnp.bfloat16).reshape(4, part, -1)
-        picked = gather_tiles(early, sums[1], owner_map, nz, nslot)
+        picked = gather_tiles(sums[0], sums[1], owner_map, nz, nslot)
         final = lax.all_to_all(picked, "col", 0, 0, tiled=True)
         return final.reshape(nrow, 2 * TILE)
 

time: 162 us -> 170 us (1.049)
  blocking collectives: 11.3 us -> 37.5 us
  starting transfers between devices: 102 us -> 85 us
  local copies, waits for them, and re-layouts: 4.34 us -> 17.3 us
  waiting for transfers between devices: 31.2 us -> 18.5 us
    all_to_all x0 -> x1, blocking collectives: none -> 26 us  [on_device(): moved = lax.all_to_all(moved, ('core', 'col'), 0, 0, tiled=True)]
    all_to_all x2 -> x1, waiting for transfers between devices: 15.1 us -> 0.01 us  [on_device(): moved = lax.all_to_all(moved, ('core', 'col'), 0, 0, tiled=True)]
    ppermute x0 -> x1, waiting for transfers between devices: none -> 13.2 us  [on_device(): tiles = [[lax.ppermute(own_tile, every, own_pairs(nz, ncol))], [None]]]
    unnamed x17 -> x47, local copies, waits for them, and re-layouts: 4.14 us -> 17.1 us
    ppermute x16 -> x15, starting transfers between devices: 66.2 us -> 55 us  [on_device(): current[stream] = lax.ppermute(current[stream], every, pairs)]
    ppermute x1, waiting for transfers between devices: 9.56 us -> 0.01 us  [on_device(): beside = lax.ppermute(own, every, swap_pairs(nz, ncol, 0, 1))]
    ppermute x1, starting transfers between devices: 10.1 us -> 1.91 us  [on_device(): beside_other = lax.ppermute(beside, every, swap_pairs(nz, ncol, 1, 0))]
    all_to_all x2 -> x1, starting transfers between devices: 17.6 us -> 12.1 us  [on_device(): moved = lax.all_to_all(moved, ('core', 'col'), 0, 0, tiled=True)]
  transfers between devices with their start and end apart: 21 -> 20, of which waited for: 8 -> 5; matrix products, arithmetic and copies ran while one was open for 1% -> 1% of each run, Pallas kernels for 5% -> 4%
where the time goes in v7:
time: 170 us; the launch traced here: 169 us
  starting transfers between devices  85 us (50%)
  blocking collectives  37.5 us (22%)
  waiting for transfers between devices  18.5 us (11%)
  local copies, waits for them, and re-layouts  17.3 us (10%)
  Pallas kernels  9.34 us (5%)
    ppermute x15, starting transfers between devices, on_device(): current[stream] = lax.ppermute(current[stream], every, pairs)  55 us
    all_to_all x1, blocking collectives, on_device(): moved = lax.all_to_all(moved, ('core', 'col'), 0, 0, tiled=True)  26 us
    unnamed x47, local copies, waits for them, and re-layouts  17.1 us
    ppermute x1, waiting for transfers between devices, on_device(): tiles = [[lax.ppermute(own_tile, every, own_pairs(nz, ncol))], [None]]  13.2 us
    all_to_all x1, starting transfers between devices, on_device(): moved = lax.all_to_all(moved, ('core', 'col'), 0, 0, tiled=True)  12.1 us
    all_to_all x1, blocking collectives, on_device(): final = lax.all_to_all(picked, 'col', 0, 0, tiled=True)  11.5 us
    ppermute x1, starting transfers between devices, on_device(): beside = lax.ppermute(own, every, swap_pairs(nz, ncol, 0, 1))  9.21 us
    pallas_call x3, Pallas kernels, multiply(): pl.pallas_call(body, in_specs=[vmem] * len(operands), out_specs=vmem, out...  6.95 us
  transfers between devices with their start and end apart: 20, of which 5 were waited for; matrix products, arithmetic and copies ran while one was open for 1% of the time, Pallas kernels for 4%

profile of v7, /device:TPU:1, one launch (start us, length us, event | category | flops | bytes accessed | tf_op | source)
XLA Modules:
  0.0 168.9 jit_solution(18141006396671866370)
XLA Ops:
  0.0 0.9 copy-done.18
  2.2 5.9 %collective-permute-start.4 = (bf16[1024,128]{1,0:T(8,128)(2,1)S(1)}, bf16[1024,128]{1,0:T(8,128)(2,1)S(1)}, u32[]{:S(2)}, u32[]{:S(2)}) collective-permute-start(bf16[1024,128]{1,0:T(8,128)(2,1)S(1)} %masked_tile.1), channel_id=1, source_target_pairs={{0,32},{1,496},{16,33},{17,497},{2,34},{3,498},{18,35},{19,499},{4... | collective-permute-start | bytes 786440 | tf_op jit(solution)/shard_map/ppermute | solution.py:205
  9.1 9.2 %collective-permute-start = (bf16[512,1024]{1,0:T(8,128)(2,1)S(1)}, bf16[512,1024]{1,0:T(8,128)(2,1)S(1)}, u32[]{:S(2)}, u32[]{:S(2)}) collective-permute-start(bf16[512,1024]{1,0:T(8,128)(2,1)S(1)} %bitcast_multiply_fusion.own), channel_id=1, source_target_pairs={{0,1},{1,0},{2,3},{3,2},{4,5},{5,4},{6,7},{7,6},{8,9},{9,8},{10,11... | collective-permute-start | bytes 3145736 | tf_op jit(solution)/shard_map/ppermute | solution.py:209
  18.4 2.4 %collective-permute-start.8 = (bf16[1024,128]{1,0:T(8,128)(2,1)S(1)}, bf16[1024,128]{1,0:T(8,128)(2,1)S(1)}, u32[]{:S(2)}, u32[]{:S(2)}) collective-permute-start(bf16[1024,128]{1,0:T(8,128)(2,1)S(1)} %masked_tile.1), channel_id=1, source_target_pairs={{1,32},{0,496},{17,33},{16,497},{3,34},{2,498},{19,35},{18,499},{5... | collective-permute-start | bytes 786440 | tf_op jit(solution)/shard_map/ppermute | solution.py:205
  20.7 5.6 %collective-permute-start.5 = (bf16[1024,128]{1,0:T(8,128)(2,1)S(1)}, bf16[1024,128]{1,0:T(8,128)(2,1)S(1)}, u32[]{:S(2)}, u32[]{:S(2)}) collective-permute-start(bf16[1024,128]{1,0:T(8,128)(2,1)S(1)} %collective-permute-done.4.rest_1_), channel_id=1, source_target_pairs={{0,32},{16,496},{1,33},{17,497},{2,34},{18,498},{3,35},{19,499},{4... | collective-permute-start | bytes 786440 | tf_op jit(solution)/shard_map/ppermute | solution.py:205
  26.3 2.8 %collective-permute-done.8.rest_5_ = bf16[1024,128]{1,0:T(8,128)(2,1)S(1)} collective-permute-done((bf16[1024,128]{1,0:T(8,128)(2,1)S(1)}, bf16[1024,128]{1,0:T(8,128)(2,1)S(1)}, u32[]{:S(2)}, u32[]{:S(2)}) %collective-permute-start.8) | collective-permute-done | bytes 262176 | tf_op jit(solution)/shard_map/ppermute | solution.py:205
  29.1 2.8 %collective-permute-start.9 = (bf16[1024,128]{1,0:T(8,128)(2,1)S(1)}, bf16[1024,128]{1,0:T(8,128)(2,1)S(1)}, u32[]{:S(2)}, u32[]{:S(2)}) collective-permute-start(bf16[1024,128]{1,0:T(8,128)(2,1)S(1)} %collective-permute-done.8.rest_5_), channel_id=1, source_target_pairs={{0,32},{16,496},{1,33},{17,497},{2,34},{18,498},{3,35},{19,499},{4... | collective-permute-start | bytes 786440 | tf_op jit(solution)/shard_map/ppermute | solution.py:205
  32.7 2.1 %collective-permute-start.6 = (bf16[1024,128]{1,0:T(8,128)(2,1)S(1)}, bf16[1024,128]{1,0:T(8,128)(2,1)S(1)}, u32[]{:S(2)}, u32[]{:S(2)}) collective-permute-start(bf16[1024,128]{1,0:T(8,128)(2,1)S(1)} %collective-permute-done.5.rest_2_), channel_id=1, source_target_pairs={{0,32},{16,496},{1,33},{17,497},{2,34},{18,498},{3,35},{19,499},{4... | collective-permute-start | bytes 786440 | tf_op jit(solution)/shard_map/ppermute | solution.py:205
  35.5 1.0 collective-permute-done.9.rest_6_
  36.5 3.8 %collective-permute-start.10 = (bf16[1024,128]{1,0:T(8,128)(2,1)S(1)}, bf16[1024,128]{1,0:T(8,128)(2,1)S(1)}, u32[]{:S(2)}, u32[]{:S(2)}) collective-permute-start(bf16[1024,128]{1,0:T(8,128)(2,1)S(1)} %collective-permute-done.9.rest_6_), channel_id=1, source_target_pairs={{0,32},{16,496},{1,33},{17,497},{2,34},{18,498},{3,35},{19,499},{4... | collective-permute-start | bytes 786440 | tf_op jit(solution)/shard_map/ppermute | solution.py:205
  41.0 2.1 %collective-permute-start.7 = (bf16[1024,128]{1,0:T(8,128)(2,1)S(1)}, bf16[1024,128]{1,0:T(8,128)(2,1)S(1)}, u32[]{:S(2)}, u32[]{:S(2)}) collective-permute-start(bf16[1024,128]{1,0:T(8,128)(2,1)S(1)} %collective-permute-done.6.rest_3_), channel_id=1, source_target_pairs={{0,32},{16,496},{1,33},{17,497},{2,34},{18,498},{3,35},{19,499},{4... | collective-permute-start | bytes 786440 | tf_op jit(solution)/shard_map/ppermute | solution.py:205
  43.8 3.2 %collective-permute-start.1 = (bf16[512,1024]{1,0:T(8,128)(2,1)S(1)}, bf16[512,1024]{1,0:T(8,128)(2,1)S(1)}, u32[]{:S(2)}, u32[]{:S(2)}) collective-permute-start(bf16[512,1024]{1,0:T(8,128)(2,1)S(1)} %bitcast_multiply_fusion.own), channel_id=1, source_target_pairs={{0,16},{1,17},{2,18},{3,19},{4,20},{5,21},{6,22},{7,23},{8,24},{9,... | collective-permute-start | bytes 3145736 | tf_op jit(solution)/shard_map/ppermute | solution.py:210
  47.1 4.9 %collective-permute-start.11 = (bf16[1024,128]{1,0:T(8,128)(2,1)S(1)}, bf16[1024,128]{1,0:T(8,128)(2,1)S(1)}, u32[]{:S(2)}, u32[]{:S(2)}) collective-permute-start(bf16[1024,128]{1,0:T(8,128)(2,1)S(1)} %collective-permute-done.10.rest_7_), channel_id=1, source_target_pairs={{0,32},{16,496},{1,33},{17,497},{2,34},{18,498},{3,35},{19,499},{4... | collective-permute-start | bytes 786440 | tf_op jit(solution)/shard_map/ppermute | solution.py:205
  52.6 3.4 %collective-permute-start.12 = (bf16[1024,128]{1,0:T(8,128)(2,1)S(1)}, bf16[1024,128]{1,0:T(8,128)(2,1)S(1)}, u32[]{:S(2)}, u32[]{:S(2)}) collective-permute-start(bf16[1024,128]{1,0:T(8,128)(2,1)S(1)} %collective-permute-done.7.rest_4_), channel_id=1, source_target_pairs={{0,32},{16,496},{1,33},{17,497},{2,34},{18,498},{3,35},{19,499},{4... | collective-permute-start | bytes 786440 | tf_op jit(solution)/shard_map/ppermute | solution.py:205
  56.8 1.9 %collective-permute-start.2 = (bf16[512,1024]{1,0:T(8,128)(2,1)S(1)}, bf16[512,1024]{1,0:T(8,128)(2,1)S(1)}, u32[]{:S(2)}, u32[]{:S(2)}) collective-permute-start(bf16[512,1024]{1,0:T(8,128)(2,1)S(1)} %collective-permute-done.beside), channel_id=1, source_target_pairs={{0,16},{1,17},{2,18},{3,19},{4,20},{5,21},{6,22},{7,23},{8,24},{9,... | collective-permute-start | bytes 3145736 | tf_op jit(solution)/shard_map/ppermute | solution.py:211
  58.7 2.7 %collective-permute-start.16 = (bf16[1024,128]{1,0:T(8,128)(2,1)S(1)}, bf16[1024,128]{1,0:T(8,128)(2,1)S(1)}, u32[]{:S(2)}, u32[]{:S(2)}) collective-permute-start(bf16[1024,128]{1,0:T(8,128)(2,1)S(1)} %collective-permute-done.11.rest_8_), channel_id=1, source_target_pairs={{0,32},{16,496},{1,33},{17,497},{2,34},{18,498},{3,35},{19,499},{4... | collective-permute-start | bytes 786440 | tf_op jit(solution)/shard_map/ppermute | solution.py:205
  62.1 3.4 %collective-permute-start.13 = (bf16[1024,128]{1,0:T(8,128)(2,1)S(1)}, bf16[1024,128]{1,0:T(8,128)(2,1)S(1)}, u32[]{:S(2)}, u32[]{:S(2)}) collective-permute-start(bf16[1024,128]{1,0:T(8,128)(2,1)S(1)} %collective-permute-done.12.rest_0_), channel_id=1, source_target_pairs={{0,32},{16,496},{1,33},{17,497},{2,34},{18,498},{3,35},{19,499},{4... | collective-permute-start | bytes 786440 | tf_op jit(solution)/shard_map/ppermute | solution.py:205
  66.1 3.6 %collective-permute-start.17 = (bf16[1024,128]{1,0:T(8,128)(2,1)S(1)}, bf16[1024,128]{1,0:T(8,128)(2,1)S(1)}, u32[]{:S(2)}, u32[]{:S(2)}) collective-permute-start(bf16[1024,128]{1,0:T(8,128)(2,1)S(1)} %collective-permute-done.16.rest_3_), channel_id=1, source_target_pairs={{0,32},{16,496},{1,33},{17,497},{2,34},{18,498},{3,35},{19,499},{4... | collective-permute-start | bytes 786440 | tf_op jit(solution)/shard_map/ppermute | solution.py:205
  69.7 4.1 %collective-permute-start.14 = (bf16[1024,128]{1,0:T(8,128)(2,1)S(1)}, bf16[1024,128]{1,0:T(8,128)(2,1)S(1)}, u32[]{:S(2)}, u32[]{:S(2)}) collective-permute-start(bf16[1024,128]{1,0:T(8,128)(2,1)S(1)} %collective-permute-done.13.rest_1_), channel_id=1, source_target_pairs={{0,32},{16,496},{1,33},{17,497},{2,34},{18,498},{3,35},{19,499},{4... | collective-permute-start | bytes 786440 | tf_op jit(solution)/shard_map/ppermute | solution.py:205
  73.9 4.1 %collective-permute-start.18 = (bf16[1024,128]{1,0:T(8,128)(2,1)S(1)}, bf16[1024,128]{1,0:T(8,128)(2,1)S(1)}, u32[]{:S(2)}, u32[]{:S(2)}) collective-permute-start(bf16[1024,128]{1,0:T(8,128)(2,1)S(1)} %collective-permute-done.17.rest_4_), channel_id=1, source_target_pairs={{0,32},{16,496},{1,33},{17,497},{2,34},{18,498},{3,35},{19,499},{4... | collective-permute-start | bytes 786440 | tf_op jit(solution)/shard_map/ppermute | solution.py:205
  78.0 4.1 %collective-permute-start.15 = (bf16[1024,128]{1,0:T(8,128)(2,1)S(1)}, bf16[1024,128]{1,0:T(8,128)(2,1)S(1)}, u32[]{:S(2)}, u32[]{:S(2)}) collective-permute-start(bf16[1024,128]{1,0:T(8,128)(2,1)S(1)} %collective-permute-done.14.rest_2_), channel_id=1, source_target_pairs={{0,32},{16,496},{1,33},{17,497},{2,34},{18,498},{3,35},{19,499},{4... | collective-permute-start | bytes 786440 | tf_op jit(solution)/shard_map/ppermute | solution.py:205
  82.2 2.5 %multiply.4.rest_1_ = bf16[2,512,512]{2,1,0:T(8,128)(2,1)S(1)} custom-call(bf16[512,1024]{1,0:T(8,128)(2,1)S(1)} %bitcast_multiply_fusion.own, bf16[512,1024]{1,0:T(8,128)(2,1)S(1)} %collective-permute-done.beside, bf16[512,1024]{1,0:T(8,128)(2,1)S(1)} %collective-permute-done.1.own_other, bf16[512,1024]{1,0:T(8,128)(2,1)S(1)} %collective-permute-done.2.beside_other, ...), custom_call_target="tpu_custom_call" | custom-call | tf_op jit(solution)/shard_map/multiply/pallas_call | solution.py:127
  86.4 1.0 copy-done.2
  87.4 12.1 %all-to-all-start.1 = ((bf16[32,32,512]{2,1,0:T(8,128)(2,1)}), bf16[32,32,512]{2,1,0:T(8,128)(2,1)}, u32[]{:S(2)}, u32[]{:S(2)}) async-start(bf16[32,32,512]{2,1,0:T(8,128)(2,1)} %bitcast.8), calls=%async_computation.1 | async-start | bytes 2097152 | tf_op jit(solution)/shard_map/all_to_all | solution.py:223
  99.5 3.5 %collective-permute-start.3 = (bf16[1024,128]{1,0:T(8,128)(2,1)}, bf16[1024,128]{1,0:T(8,128)(2,1)S(1)}, u32[]{:S(2)}, u32[]{:S(2)}) collective-permute-start(bf16[1024,128]{1,0:T(8,128)(2,1)} %copy-done.19), channel_id=1, source_target_pairs={{0,0},{1,16},{16,1},{17,17},{2,2},{3,18},{18,3},{19,19},{4,4},{5,2... | collective-permute-start | bytes 786440 | tf_op jit(solution)/shard_map/ppermute | solution.py:195
  103.0 13.2 %collective-permute-done.3.rest_0_ = bf16[1024,128]{1,0:T(8,128)(2,1)S(1)} collective-permute-done((bf16[1024,128]{1,0:T(8,128)(2,1)}, bf16[1024,128]{1,0:T(8,128)(2,1)S(1)}, u32[]{:S(2)}, u32[]{:S(2)}) %collective-permute-start.3) | collective-permute-done | bytes 262176 | tf_op jit(solution)/shard_map/ppermute | solution.py:195
  116.3 1.2 copy-done.1
  124.1 3.6 %multiply.3 = bf16[2,512,640]{2,1,0:T(8,128)(2,1)S(1)} custom-call(bf16[512,1024]{1,0:T(8,128)(2,1)S(1)} %bitcast_multiply_fusion.own, bf16[512,1024]{1,0:T(8,128)(2,1)S(1)} %collective-permute-done.beside, bf16[512,1024]{1,0:T(8,128)(2,1)S(1)} %collective-permute-done.1.own_other, bf16[512,1024]{1,0:T(8,128)(2,1)S(1)} %copy-done.1, ...), custom_call_target="tpu_custom_call" | custom-call | tf_op jit(solution)/shard_map/multiply/pallas_call | solution.py:127
  127.8 1.1 copy-done.3
  128.8 26.0 %all_to_all.15.first = bf16[32,32,640]{2,1,0:T(8,128)(2,1)S(1)} all-to-all(bf16[32,32,640]{2,1,0:T(8,128)(2,1)} %bitcast.9), channel_id=1, replica_groups=mesh['z'=16,'core'=2,'col'=16] {'core','col'}, dimensions={0} | all-to-all | bytes 2621440 | tf_op jit(solution)/shard_map/all_to_all | solution.py:223
  154.8 1.8 %gather_tiles.1 = bf16[16,32,256]{2,1,0:T(8,128)(2,1)S(1)} custom-call(s32[32]{0:T(128)S(1)} %copy-done.21, bf16[32,32,640]{2,1,0:T(8,128)(2,1)S(1)} %all_to_all.15.first, bf16[32,32,512]{2,1,0:T(8,128)(2,1)} %all-to-all-done.1.second), custom_call_target="tpu_custom_call" | custom-call | tf_op jit(solution)/shard_map/gather_tiles/pallas_call | solution.py:173
  156.7 11.5 %all_to_all.16 = bf16[16,32,256]{2,1,0:T(8,128)(2,1)S(1)} all-to-all(bf16[16,32,256]{2,1,0:T(8,128)(2,1)S(1)} %gather_tiles.1), channel_id=1, replica_groups=mesh['z'=16,'core'=2,'col'=16] {'col'}, dimensions={0} | all-to-all | bytes 524288 | tf_op jit(solution)/shard_map/all_to_all | solution.py:226
  (65 shorter events, 16.8 us)
Async XLA Ops:
  0.0 0.9 copy-start.18
  1.6 7.4 %copy-start.22 = (bf16[512,1024]{1,0:T(8,128)(2,1)S(1)}, bf16[512,1024]{1,0:T(8,128)(2,1)}, u32[]{:S(2)}) copy-start(bf16[512,1024]{1,0:T(8,128)(2,1)} %param.5) | copy-start | bytes 3145732
  2.2 16.1 %copy-start.19 = (bf16[1024,128]{1,0:T(8,128)(2,1)}, bf16[1024,128]{1,0:T(8,128)(2,1)S(1)}, u32[]{:S(2)}) copy-start(bf16[1024,128]{1,0:T(8,128)(2,1)S(1)} %masked_tile.1) | copy-start | bytes 786436
  2.2 18.5 %collective-permute-start.4 = (bf16[1024,128]{1,0:T(8,128)(2,1)S(1)}, bf16[1024,128]{1,0:T(8,128)(2,1)S(1)}, u32[]{:S(2)}, u32[]{:S(2)}) collective-permute-start(bf16[1024,128]{1,0:T(8,128)(2,1)S(1)} %masked_tile.1), channel_id=1, source_target_pairs={{0,32},{1,496},{16,33},{17,497},{2,34},{3,498},{18,35},{19,499},{4... | collective-permute-start | bytes 786440 | tf_op jit(solution)/shard_map/ppermute | solution.py:205
  9.1 47.7 %collective-permute-start = (bf16[512,1024]{1,0:T(8,128)(2,1)S(1)}, bf16[512,1024]{1,0:T(8,128)(2,1)S(1)}, u32[]{:S(2)}, u32[]{:S(2)}) collective-permute-start(bf16[512,1024]{1,0:T(8,128)(2,1)S(1)} %bitcast_multiply_fusion.own), channel_id=1, source_target_pairs={{0,1},{1,0},{2,3},{3,2},{4,5},{5,4},{6,7},{7,6},{8,9},{9,8},{10,11... | collective-permute-start | bytes 3145736 | tf_op jit(solution)/shard_map/ppermute | solution.py:209
  18.4 10.8 %collective-permute-start.8 = (bf16[1024,128]{1,0:T(8,128)(2,1)S(1)}, bf16[1024,128]{1,0:T(8,128)(2,1)S(1)}, u32[]{:S(2)}, u32[]{:S(2)}) collective-permute-start(bf16[1024,128]{1,0:T(8,128)(2,1)S(1)} %masked_tile.1), channel_id=1, source_target_pairs={{1,32},{0,496},{17,33},{16,497},{3,34},{2,498},{19,35},{18,499},{5... | collective-permute-start | bytes 786440 | tf_op jit(solution)/shard_map/ppermute | solution.py:205
  20.7 12.0 %collective-permute-start.5 = (bf16[1024,128]{1,0:T(8,128)(2,1)S(1)}, bf16[1024,128]{1,0:T(8,128)(2,1)S(1)}, u32[]{:S(2)}, u32[]{:S(2)}) collective-permute-start(bf16[1024,128]{1,0:T(8,128)(2,1)S(1)} %collective-permute-done.4.rest_1_), channel_id=1, source_target_pairs={{0,32},{16,496},{1,33},{17,497},{2,34},{18,498},{3,35},{19,499},{4... | collective-permute-start | bytes 786440 | tf_op jit(solution)/shard_map/ppermute | solution.py:205
  29.1 7.4 %collective-permute-start.9 = (bf16[1024,128]{1,0:T(8,128)(2,1)S(1)}, bf16[1024,128]{1,0:T(8,128)(2,1)S(1)}, u32[]{:S(2)}, u32[]{:S(2)}) collective-permute-start(bf16[1024,128]{1,0:T(8,128)(2,1)S(1)} %collective-permute-done.8.rest_5_), channel_id=1, source_target_pairs={{0,32},{16,496},{1,33},{17,497},{2,34},{18,498},{3,35},{19,499},{4... | collective-permute-start | bytes 786440 | tf_op jit(solution)/shard_map/ppermute | solution.py:205
  32.7 8.3 %collective-permute-start.6 = (bf16[1024,128]{1,0:T(8,128)(2,1)S(1)}, bf16[1024,128]{1,0:T(8,128)(2,1)S(1)}, u32[]{:S(2)}, u32[]{:S(2)}) collective-permute-start(bf16[1024,128]{1,0:T(8,128)(2,1)S(1)} %collective-permute-done.5.rest_2_), channel_id=1, source_target_pairs={{0,32},{16,496},{1,33},{17,497},{2,34},{18,498},{3,35},{19,499},{4... | collective-permute-start | bytes 786440 | tf_op jit(solution)/shard_map/ppermute | solution.py:205
  36.5 10.5 %collective-permute-start.10 = (bf16[1024,128]{1,0:T(8,128)(2,1)S(1)}, bf16[1024,128]{1,0:T(8,128)(2,1)S(1)}, u32[]{:S(2)}, u32[]{:S(2)}) collective-permute-start(bf16[1024,128]{1,0:T(8,128)(2,1)S(1)} %collective-permute-done.9.rest_6_), channel_id=1, source_target_pairs={{0,32},{16,496},{1,33},{17,497},{2,34},{18,498},{3,35},{19,499},{4... | collective-permute-start | bytes 786440 | tf_op jit(solution)/shard_map/ppermute | solution.py:205
  41.0 11.6 %collective-permute-start.7 = (bf16[1024,128]{1,0:T(8,128)(2,1)S(1)}, bf16[1024,128]{1,0:T(8,128)(2,1)S(1)}, u32[]{:S(2)}, u32[]{:S(2)}) collective-permute-start(bf16[1024,128]{1,0:T(8,128)(2,1)S(1)} %collective-permute-done.6.rest_3_), channel_id=1, source_target_pairs={{0,32},{16,496},{1,33},{17,497},{2,34},{18,498},{3,35},{19,499},{4... | collective-permute-start | bytes 786440 | tf_op jit(solution)/shard_map/ppermute | solution.py:205
  43.8 38.4 %collective-permute-start.1 = (bf16[512,1024]{1,0:T(8,128)(2,1)S(1)}, bf16[512,1024]{1,0:T(8,128)(2,1)S(1)}, u32[]{:S(2)}, u32[]{:S(2)}) collective-permute-start(bf16[512,1024]{1,0:T(8,128)(2,1)S(1)} %bitcast_multiply_fusion.own), channel_id=1, source_target_pairs={{0,16},{1,17},{2,18},{3,19},{4,20},{5,21},{6,22},{7,23},{8,24},{9,... | collective-permute-start | bytes 3145736 | tf_op jit(solution)/shard_map/ppermute | solution.py:210
  47.1 11.6 %collective-permute-start.11 = (bf16[1024,128]{1,0:T(8,128)(2,1)S(1)}, bf16[1024,128]{1,0:T(8,128)(2,1)S(1)}, u32[]{:S(2)}, u32[]{:S(2)}) collective-permute-start(bf16[1024,128]{1,0:T(8,128)(2,1)S(1)} %collective-permute-done.10.rest_7_), channel_id=1, source_target_pairs={{0,32},{16,496},{1,33},{17,497},{2,34},{18,498},{3,35},{19,499},{4... | collective-permute-start | bytes 786440 | tf_op jit(solution)/shard_map/ppermute | solution.py:205
  52.6 9.5 %collective-permute-start.12 = (bf16[1024,128]{1,0:T(8,128)(2,1)S(1)}, bf16[1024,128]{1,0:T(8,128)(2,1)S(1)}, u32[]{:S(2)}, u32[]{:S(2)}) collective-permute-start(bf16[1024,128]{1,0:T(8,128)(2,1)S(1)} %collective-permute-done.7.rest_4_), channel_id=1, source_target_pairs={{0,32},{16,496},{1,33},{17,497},{2,34},{18,498},{3,35},{19,499},{4... | collective-permute-start | bytes 786440 | tf_op jit(solution)/shard_map/ppermute | solution.py:205
  56.8 25.4 %collective-permute-start.2 = (bf16[512,1024]{1,0:T(8,128)(2,1)S(1)}, bf16[512,1024]{1,0:T(8,128)(2,1)S(1)}, u32[]{:S(2)}, u32[]{:S(2)}) collective-permute-start(bf16[512,1024]{1,0:T(8,128)(2,1)S(1)} %collective-permute-done.beside), channel_id=1, source_target_pairs={{0,16},{1,17},{2,18},{3,19},{4,20},{5,21},{6,22},{7,23},{8,24},{9,... | collective-permute-start | bytes 3145736 | tf_op jit(solution)/shard_map/ppermute | solution.py:211
  58.7 7.4 %collective-permute-start.16 = (bf16[1024,128]{1,0:T(8,128)(2,1)S(1)}, bf16[1024,128]{1,0:T(8,128)(2,1)S(1)}, u32[]{:S(2)}, u32[]{:S(2)}) collective-permute-start(bf16[1024,128]{1,0:T(8,128)(2,1)S(1)} %collective-permute-done.11.rest_8_), channel_id=1, source_target_pairs={{0,32},{16,496},{1,33},{17,497},{2,34},{18,498},{3,35},{19,499},{4... | collective-permute-start | bytes 786440 | tf_op jit(solution)/shard_map/ppermute | solution.py:205
  62.1 7.6 %collective-permute-start.13 = (bf16[1024,128]{1,0:T(8,128)(2,1)S(1)}, bf16[1024,128]{1,0:T(8,128)(2,1)S(1)}, u32[]{:S(2)}, u32[]{:S(2)}) collective-permute-start(bf16[1024,128]{1,0:T(8,128)(2,1)S(1)} %collective-permute-done.12.rest_0_), channel_id=1, source_target_pairs={{0,32},{16,496},{1,33},{17,497},{2,34},{18,498},{3,35},{19,499},{4... | collective-permute-start | bytes 786440 | tf_op jit(solution)/shard_map/ppermute | solution.py:205
  66.1 7.8 %collective-permute-start.17 = (bf16[1024,128]{1,0:T(8,128)(2,1)S(1)}, bf16[1024,128]{1,0:T(8,128)(2,1)S(1)}, u32[]{:S(2)}, u32[]{:S(2)}) collective-permute-start(bf16[1024,128]{1,0:T(8,128)(2,1)S(1)} %collective-permute-done.16.rest_3_), channel_id=1, source_target_pairs={{0,32},{16,496},{1,33},{17,497},{2,34},{18,498},{3,35},{19,499},{4... | collective-permute-start | bytes 786440 | tf_op jit(solution)/shard_map/ppermute | solution.py:205
  69.7 8.3 %collective-permute-start.14 = (bf16[1024,128]{1,0:T(8,128)(2,1)S(1)}, bf16[1024,128]{1,0:T(8,128)(2,1)S(1)}, u32[]{:S(2)}, u32[]{:S(2)}) collective-permute-start(bf16[1024,128]{1,0:T(8,128)(2,1)S(1)} %collective-permute-done.13.rest_1_), channel_id=1, source_target_pairs={{0,32},{16,496},{1,33},{17,497},{2,34},{18,498},{3,35},{19,499},{4... | collective-permute-start | bytes 786440 | tf_op jit(solution)/shard_map/ppermute | solution.py:205
  73.9 8.3 %collective-permute-start.18 = (bf16[1024,128]{1,0:T(8,128)(2,1)S(1)}, bf16[1024,128]{1,0:T(8,128)(2,1)S(1)}, u32[]{:S(2)}, u32[]{:S(2)}) collective-permute-start(bf16[1024,128]{1,0:T(8,128)(2,1)S(1)} %collective-permute-done.17.rest_4_), channel_id=1, source_target_pairs={{0,32},{16,496},{1,33},{17,497},{2,34},{18,498},{3,35},{19,499},{4... | collective-permute-start | bytes 786440 | tf_op jit(solution)/shard_map/ppermute | solution.py:205
  78.0 7.4 %collective-permute-start.15 = (bf16[1024,128]{1,0:T(8,128)(2,1)S(1)}, bf16[1024,128]{1,0:T(8,128)(2,1)S(1)}, u32[]{:S(2)}, u32[]{:S(2)}) collective-permute-start(bf16[1024,128]{1,0:T(8,128)(2,1)S(1)} %collective-permute-done.14.rest_2_), channel_id=1, source_target_pairs={{0,32},{16,496},{1,33},{17,497},{2,34},{18,498},{3,35},{19,499},{4... | collective-permute-start | bytes 786440 | tf_op jit(solution)/shard_map/ppermute | solution.py:205
  82.2 3.3 %copy-start = (bf16[512,1024]{1,0:T(8,128)(2,1)}, bf16[512,1024]{1,0:T(8,128)(2,1)S(1)}, u32[]{:S(2)}) copy-start(bf16[512,1024]{1,0:T(8,128)(2,1)S(1)} %collective-permute-done.2.beside_other) | copy-start | bytes 3145732
  86.4 1.0 copy-start.2
  87.4 41.5 %all-to-all-start.1 = ((bf16[32,32,512]{2,1,0:T(8,128)(2,1)}), bf16[32,32,512]{2,1,0:T(8,128)(2,1)}, u32[]{:S(2)}, u32[]{:S(2)}) async-start(bf16[32,32,512]{2,1,0:T(8,128)(2,1)} %bitcast.8), calls=%async_computation.1 | async-start | bytes 2097152 | tf_op jit(solution)/shard_map/all_to_all | solution.py:223
  99.5 16.8 %collective-permute-start.3 = (bf16[1024,128]{1,0:T(8,128)(2,1)}, bf16[1024,128]{1,0:T(8,128)(2,1)S(1)}, u32[]{:S(2)}, u32[]{:S(2)}) collective-permute-start(bf16[1024,128]{1,0:T(8,128)(2,1)} %copy-done.19), channel_id=1, source_target_pairs={{0,0},{1,16},{16,1},{17,17},{2,2},{3,18},{18,3},{19,19},{4,4},{5,2... | collective-permute-start | bytes 786440 | tf_op jit(solution)/shard_map/ppermute | solution.py:195
  116.2 1.2 copy-start.1
  117.5 0.9 copy-start.5
  118.4 0.9 copy-start.7
  119.4 0.9 copy-start.9
  120.3 0.9 copy-start.11
  127.7 1.1 copy-start.3
  128.8 26.0 %copy-start.21 = (s32[32]{0:T(128)S(1)}, s32[32]{0:T(128)}, u32[]{:S(2)}) copy-start(s32[32]{0:T(128)} %owner.1) | copy-start | bytes 388
  (11 other events, 8.4 us)
